TPU v7x, 128 devices: a whole 4x4x4 slice. The times are simulated.
128 devices in a mesh: tiles: 128 (over x, z, y, core).
Axes of the slice: x: 4, y: 4, z: 4, core: 2. Of those that a mesh axis runs over, the one named last changes fastest.
Arguments:
- primal_start: float32 [256, 512, 1024], P('tiles'), may hold values from 0 to 1
- cost: bfloat16 [256, 512, 1024], P('tiles'), may hold values from -4 to 4
- mask: int32 [256, 64, 8], P('tiles'), may hold values 0 or 1
- tile_adv: int32 [256], P('tiles'), may hold values from -1 to 127, as said below
- tile_slot: int32 [256], P('tiles'), may hold values from -1 to 127
- adv_dual: float32 [128, 512], P('tiles'), may hold values from 0 to 2
- slot_dual: float32 [128, 1024], P('tiles'), may hold values from 0 to 2
- spend_limit: float32 [128, 512], P('tiles'), may hold values from 204 to 921
- capacity: float32 [128, 1024], P('tiles'), may hold values from 64 to 384
Outputs:
- primal: float32 [256, 512, 1024], P('tiles')
- adv_out: float32 [128, 512], P('tiles')
- slot_out: float32 [128, 1024], P('tiles')
Inputs may be any that keep to these rules, and one draw needn't show every extreme that they name: -1 marks an empty tile slot; tile_adv and tile_slot are -1 at the same slots. Each device's 2 slots hold 1 to 2 tiles, in its first slots, and some device holds exactly 2.
All inputs are finite; a program needn't handle non-finite values. No bound on the sum of `mask` on one device may be relied on, other than what follows from the above.
Results may differ from a plain program's by a relative error of at most 0.0003.
Values sent between devices are 32-bit elements; how exact they have to be, the bound alone decides.
No kernel may reach another device: no remote copies, remote signals or barrier semaphores. Data moves between devices by JAX's collectives and lax.ppermute only.
A program may use at most 64 MiB of HBM per device.

v0:
```python
import jax
import jax.numpy as jnp
from jax import lax
from jax.sharding import PartitionSpec as P

MB_ROWS = 8
MB_COLS = 128
ITERS = 2


tau_step = 0.5


def expand_mask(blocks, block_rows, block_cols):
    values = blocks.astype(jnp.float32)
    rows_in = values.shape[-2]
    cols_in = values.shape[-1]
    shaped = jnp.broadcast_to(
        values[..., :, None, :, None],
        values.shape[:-2] + (rows_in, block_rows, cols_in, block_cols),
    )
    return shaped.reshape(values.shape[:-2] + (rows_in * block_rows, cols_in * block_cols))


def body(primal_start, cost, mask, tile_adv, tile_slot, adv_dual, slot_dual, spend_limit, capacity):
    highest = lax.Precision.HIGHEST
    devices = lax.axis_size("tiles")
    adv_local = adv_dual.shape[0]
    slot_local = slot_dual.shape[0]
    rows_tile = primal_start.shape[1]
    cols_tile = primal_start.shape[2]
    adv_onehot = (
        tile_adv[:, None] == jnp.arange(adv_local * devices, dtype=jnp.int32)[None, :]
    ).astype(jnp.float32)
    slot_onehot = (
        tile_slot[:, None] == jnp.arange(slot_local * devices, dtype=jnp.int32)[None, :]
    ).astype(jnp.float32)
    present = (tile_adv >= 0).astype(jnp.float32)
    weight = expand_mask(mask, MB_ROWS, MB_COLS) * present[:, None, None]
    primal = weight * primal_start
    for sweep_index in range(ITERS):
        adv_all, slot_all = (
            lax.all_gather(adv_dual, "tiles", axis=0, tiled=True),
            lax.all_gather(slot_dual, "tiles", axis=0, tiled=True),
        )
        adv_rows = jnp.dot(adv_onehot, adv_all, precision=highest)
        slot_cols = jnp.dot(slot_onehot, slot_all, precision=highest)
        update = weight * jnp.clip(
            primal
            - tau_step * (cost.astype(jnp.float32) + adv_rows[:, :, None] + slot_cols[:, None, :]),
            0.0,
            1.0,
        )
        extended = 2.0 * update - primal
        row_blocks = jnp.dot(adv_onehot.T, jnp.sum(extended, axis=2), precision=highest)
        col_blocks = jnp.dot(slot_onehot.T, jnp.sum(extended, axis=1), precision=highest)
        primal, row_blocks, col_blocks = (update, row_blocks, col_blocks)
        row_mine, col_mine = (
            lax.psum_scatter(row_blocks, "tiles", scatter_dimension=0, tiled=True),
            lax.psum_scatter(col_blocks, "tiles", scatter_dimension=0, tiled=True),
        )
        adv_dual = jnp.maximum(adv_dual + (row_mine - spend_limit) / cols_tile, 0.0)
        slot_dual = jnp.maximum(slot_dual + (col_mine - capacity) / rows_tile, 0.0)
    return (primal, adv_dual, slot_dual)


def solution(mesh):
    return jax.shard_map(
        body,
        mesh=mesh,
        in_specs=(
            P("tiles", None, None),
            P("tiles", None, None),
            P("tiles", None, None),
            P("tiles"),
            P("tiles"),
            P("tiles", None),
            P("tiles", None),
            P("tiles", None),
            P("tiles", None),
        ),
        out_specs=(P("tiles", None, None), P("tiles", None), P("tiles", None)),
        check_vma=False,
    )
```

profile of v0, /device:TPU:0, one launch (start us, length us, event | category | flops | bytes accessed | tf_op | source)
XLA Modules:
  0.0 469.6 jit_solution(5772442257037595880)
XLA Ops:
  7.2 0.0 copy-start.3
  7.2 0.0 copy-start.4
  7.2 0.0 all-reduce.11.cloned.1.call-start
  7.2 0.7 compare_convert_fusion
  7.9 0.7 convert_element_type.12
  8.6 0.1 copy.13
  8.7 37.6 %all-gather = f32[128,1,512]{2,1,0:T(1,128)S(1)} all-gather(f32[1,1,512]{2,1,0:T(1,128)} %bitcast.50), channel_id=1, replica_groups=mesh['tiles'=128] {'tiles'}, dimensions={0}, use_global_device_ids=true | all-gather | bytes 264192 | tf_op jit(solution)/shard_map/all_gather | solution.py:43
  46.3 0.9 fusion.22
  47.2 33.9 %all-gather.1 = f32[128,1,1024]{2,1,0:T(1,128)S(1)} all-gather(f32[1,1,1024]{2,1,0:T(1,128)} %bitcast.49), channel_id=1, replica_groups=mesh['tiles'=128] {'tiles'}, dimensions={0}, use_global_device_ids=true | all-gather | bytes 528384 | tf_op jit(solution)/shard_map/all_gather | solution.py:44
  81.1 1.0 fusion.16
  82.2 0.0 copy-start.2
  82.2 0.0 copy-start
  82.2 5.0 %fusion.26 = (f32[2,512]{1,0:T(2,128)S(1)}, f32[2,1024]{1,0:T(2,128)S(1)}) fusion(f32[2,512,1024]{2,1,0:T(8,128)} %param.9, f32[2]{0:T(128)S(1)} %compare_convert_fusion, f32[2,64,8]{2,1,0:T(8,128)S(1)} %copy.13, f32[2,1024]{1,0:T(2,128)S(1)} %fusion.16, f32[2,512]{1,0:T(2,128)S(1)} %fusion.22, bf16[2,512,1024]{2,1,0:T(8,128)(2,1)} %param.10), kind=kLoop, calls=%fused_computation.31 | loop fusion | flops 13628416 | bytes 6320136 | tf_op jit(solution)/shard_map/reduce_sum | solution.py:55
  87.2 1.1 fusion.42
  88.3 1.3 fusion.40
  89.6 0.0 all-reduce.11.cloned.1.call-update
  89.6 0.0 all-reduce.9.cloned.1.call-start
  89.6 146.1 %all-reduce.11.cloned.1.call-done = (f32[128,1024]{1,0:T(8,128)}, f32[128,512]{1,0:T(8,128)}) async-done(((f32[128,1024]{1,0:T(8,128)}, f32[128,512]{1,0:T(8,128)}), (f32[128,1024]{1,0:T(8,128)}, f32[128,512]{1,0:T(8,128)})) %all-reduce.11.cloned.1.call-update) | async-done | bytes 786448
  235.7 0.0 copy-done.6
  235.7 0.7 fusion.37
  236.4 34.3 %all-gather.2 = f32[128,1,512]{2,1,0:T(1,128)S(1)} all-gather(f32[1,1,512]{2,1,0:T(1,128)S(1)} %bitcast.48), channel_id=1, replica_groups=mesh['tiles'=128] {'tiles'}, dimensions={0}, use_global_device_ids=true | all-gather | bytes 264192 | tf_op jit(solution)/shard_map/all_gather | solution.py:43
  270.8 0.2 fusion.19
  271.0 0.8 fusion.31
  271.8 34.0 %all-gather.3 = f32[128,1,1024]{2,1,0:T(1,128)S(1)} all-gather(f32[1,1,1024]{2,1,0:T(1,128)S(1)} %bitcast.47), channel_id=1, replica_groups=mesh['tiles'=128] {'tiles'}, dimensions={0}, use_global_device_ids=true | all-gather | bytes 528384 | tf_op jit(solution)/shard_map/all_gather | solution.py:44
  305.8 0.3 fusion.13
  306.1 6.4 %fusion.11 = (f32[2,1024]{1,0:T(2,128)S(1)}, f32[2,512]{1,0:T(2,128)S(1)}, f32[2,512,1024]{2,1,0:T(8,128)}) fusion(f32[2,1024]{1,0:T(2,128)S(1)} %fusion.16, f32[2,512]{1,0:T(2,128)S(1)} %fusion.22, bf16[2,512,1024]{2,1,0:T(8,128)(2,1)S(1)} %copy-done, f32[2,512,1024]{2,1,0:T(8,128)} %param.9, f32[2]{0:T(128)S(1)} %compare_convert_fusion, ...), kind=kLoop, calls=%fused_computation.16 | loop fusion | flops 19919872 | bytes 10526728 | tf_op jit(solution)/shard_map/reduce_sum | solution.py:56
  312.5 1.1 fusion.41
  313.6 1.3 fusion.39
  314.9 0.0 all-reduce.9.cloned.1.call-update
  314.9 145.2 %all-reduce.9.cloned.1.call-done = (f32[128,512]{1,0:T(8,128)}, f32[128,1024]{1,0:T(8,128)}) async-done(((f32[128,512]{1,0:T(8,128)}, f32[128,1024]{1,0:T(8,128)}), (f32[128,512]{1,0:T(8,128)}, f32[128,1024]{1,0:T(8,128)})) %all-reduce.9.cloned.1.call-update) | async-done | bytes 786448
  460.1 1.3 fusion.38
  461.4 1.4 fusion.32
  (9 shorter events, 0.0 us)
Async XLA Ops:
  7.2 80.0 %copy-start.3 = (s32[2]{0:T(128)S(1)}, s32[2]{0:T(128)}, u32[]{:S(2)}) copy-start(s32[2]{0:T(128)} %param.12) | copy-start | bytes 28
  7.2 81.1 %copy-start.4 = (s32[2]{0:T(128)S(1)}, s32[2]{0:T(128)}, u32[]{:S(2)}) copy-start(s32[2]{0:T(128)} %param.13) | copy-start | bytes 28
  7.2 228.5 %all-reduce.11.cloned.1.call-start = ((), (), s32[]{:S(2)}) async-start(), calls=%async_computation.1 | async-start | bytes 1572864
  81.1 154.6 %copy-start.5 = (f32[1,512]{1,0:T(1,128)S(1)}, f32[1,512]{1,0:T(1,128)}, u32[]{:S(2)}) copy-start(f32[1,512]{1,0:T(1,128)} %param.14) | copy-start | bytes 6148
  81.1 154.6 %copy-start.6 = (f32[1,512]{1,0:T(1,128)S(1)}, f32[1,512]{1,0:T(1,128)}, u32[]{:S(2)}) copy-start(f32[1,512]{1,0:T(1,128)} %param.16) | copy-start | bytes 6148
  82.2 188.8 %copy-start.1 = (f32[1,1024]{1,0:T(1,128)S(1)}, f32[1,1024]{1,0:T(1,128)}, u32[]{:S(2)}) copy-start(f32[1,1024]{1,0:T(1,128)} %param.15) | copy-start | bytes 12292
  82.2 188.8 %copy-start.2 = (f32[1,1024]{1,0:T(1,128)S(1)}, f32[1,1024]{1,0:T(1,128)}, u32[]{:S(2)}) copy-start(f32[1,1024]{1,0:T(1,128)} %param.17) | copy-start | bytes 12292
  82.2 223.9 %copy-start = (bf16[2,512,1024]{2,1,0:T(8,128)(2,1)S(1)}, bf16[2,512,1024]{2,1,0:T(8,128)(2,1)}, u32[]{:S(2)}) copy-start(bf16[2,512,1024]{2,1,0:T(8,128)(2,1)} %param.10) | copy-start | bytes 6291460
  89.6 370.5 %all-reduce.9.cloned.1.call-start = ((), (), s32[]{:S(2)}) async-start(), calls=%async_computation | async-start | bytes 1572864
Sparse Core Ops, SparseCore 0:
  89.7 145.9 all-reduce.10
  315.0 144.9 all-reduce.8
where the time goes:
time: 471 us; the launch traced here: 470 us
  waiting for transfers between devices  291 us (62%)
  blocking collectives  140 us (30%)
  other arithmetic  16.9 us (4%)
  between operations  14.1 us (3%)
  matrix products  7.18 us (2%)
    unnamed x4, waiting for transfers between devices  291 us
    all_gather x2, blocking collectives, body(): lax.all_gather(adv_dual, 'tiles', axis=0, tiled=True)  71.9 us
    all_gather x2, blocking collectives, body(): lax.all_gather(slot_dual, 'tiles', axis=0, tiled=True)  68 us
  transfers between devices with their start and end apart: 2, of which 2 were waited for; matrix products, arithmetic and copies ran while one was open for 0% of the time, Pallas kernels for 0%

commit v1 on v0

v1 whole, which is shorter than its diff:
```python
import functools

import jax
import jax.numpy as jnp
from jax import lax
from jax.experimental import pallas as pl
from jax.experimental.pallas import tpu as pltpu
from jax.sharding import PartitionSpec as P

DEV = 128
XZ = 16
YC = 8
L = 128
AR = 4
SR = 8
REC = AR + SR + 1
TS = 2 * (AR + SR)
MSG = TS + SR + AR
RB = 128
NRB = 4

XZ_GROUPS = [[j * YC + q for j in range(XZ)] for q in range(YC)]
YC_GROUPS = [[j * YC + q for q in range(YC)] for j in range(XZ)]

VMEM_WHOLE = pl.BlockSpec(memory_space=pltpu.VMEM)
SMEM_WHOLE = pl.BlockSpec(memory_space=pltpu.SMEM)


def spread_rows(row, buf):
    for b in range(NRB):
        block = jnp.broadcast_to(row[b : b + 1, :], (L, L))
        buf[b * L : (b + 1) * L, :] = block.T


def sweep_block(w_ref, t, rb, p_ref, c_ref, out_ref, a_buf, s_buf, r_buf, col_buf, first):
    def step(g, cols):
        r0 = pl.multiple_of(g * 16, 16)
        cols = list(cols)
        racc = [None, None]
        for cb in range(SR):
            lanes = pl.ds(cb * L, L)
            c16 = c_ref[0, pl.ds(r0, 16), lanes].astype(jnp.float32)
            s = s_buf[pl.ds(cb * 8, 8), :]
            for h in range(2):
                rows = pl.ds(pl.multiple_of(r0 + 8 * h, 8), 8)
                w = w_ref[t * 512 + (rb * 16 + g * 2 + h) * SR + cb]
                p = p_ref[0, rows, lanes]
                if first:
                    p = p * w
                arow = a_buf[pl.ds(pl.multiple_of(rb * RB + r0 + 8 * h, 8), 8), :]
                v = p - 0.5 * ((c16[8 * h : 8 * h + 8] + arow) + s)
                u = jnp.minimum(jnp.maximum(v, 0.0), w)
                out_ref[0, rows, lanes] = u
                e = (u + u) - p
                racc[h] = e if racc[h] is None else racc[h] + e
                cols[cb] = cols[cb] + e
        for h in range(2):
            r_buf[pl.ds(pl.multiple_of(r0 + 8 * h, 8), 8), :] = racc[h]
        return tuple(cols)

    cols = tuple(col_buf[pl.ds(cb * 8, 8), :] for cb in range(SR))
    cols = lax.fori_loop(0, RB // 16, step, cols)
    for cb in range(SR):
        col_buf[pl.ds(cb * 8, 8), :] = cols[cb]


def begin_tile(arow, srow, a_buf, s_buf, col_buf):
    spread_rows(arow, a_buf)
    for cb in range(SR):
        s_buf[cb * 8 : (cb + 1) * 8, :] = jnp.broadcast_to(srow[cb : cb + 1, :], (8, L))
    col_buf[...] = jnp.zeros_like(col_buf)


def keep_sums(t, rb, r_buf, col_buf, sums):
    sums[pl.ds(t * AR + rb, 1), :] = jnp.sum(r_buf[...].T, axis=0, keepdims=True)

    @pl.when(rb == NRB - 1)
    def _():
        rows = [jnp.sum(col_buf[cb * 8 : (cb + 1) * 8, :], axis=0, keepdims=True) for cb in range(SR)]
        sums[pl.ds(pl.multiple_of(8 + t * SR, 8), SR), :] = jnp.concatenate(rows, axis=0)


def first_kernel(adv_id, slot_id, w_ref, rec, own_adv, own_slot, limit, cap, p_ref, c_ref, out_ref, msg, a_buf, s_buf, r_buf, col_buf, sums):
    t = pl.program_id(0)
    rb = pl.program_id(1)

    @pl.when(rb == 0)
    def _():
        a = jnp.maximum(adv_id[t], 0) * REC
        s = jnp.maximum(slot_id[t], 0) * REC + AR
        begin_tile(rec[pl.ds(a, AR), :], rec[pl.ds(s, SR), :], a_buf, s_buf, col_buf)

    sweep_block(w_ref, t, rb, p_ref, c_ref, out_ref, a_buf, s_buf, r_buf, col_buf, True)
    keep_sums(t, rb, r_buf, col_buf, sums)

    @pl.when((t == 1) & (rb == NRB - 1))
    def _():
        data = jnp.concatenate(
            [sums[...], own_slot[...] * 512.0 - cap[...], own_adv[...] * 1024.0 - limit[...]], axis=0
        )
        for j in range(XZ):
            msg[j * MSG : (j + 1) * MSG, :] = data


def second_kernel(w_ref, rec, p_ref, c_ref, out_ref, msg, own, a_buf, s_buf, r_buf, col_buf, sums, dual):
    t = pl.program_id(0)
    rb = pl.program_id(1)

    @pl.when((t == 0) & (rb == 0))
    def _():
        total = rec[0:MSG, :]
        for q in range(1, YC):
            total = total + rec[q * MSG : (q + 1) * MSG, :]
        dual[0:8, :] = jnp.maximum(total[0:8] * (1.0 / 1024), 0.0)
        dual[8:32, :] = jnp.maximum(total[8:32] * (1.0 / 512), 0.0)
        dual[32:36, :] = jnp.maximum(total[32:36] * (1.0 / 1024), 0.0)
        own[...] = dual[24:36, :]

    @pl.when(rb == 0)
    def _():
        begin_tile(
            dual[pl.ds(t * AR, AR), :], dual[pl.ds(pl.multiple_of(8 + t * SR, 8), SR), :], a_buf, s_buf, col_buf
        )

    sweep_block(w_ref, t, rb, p_ref, c_ref, out_ref, a_buf, s_buf, r_buf, col_buf, False)
    keep_sums(t, rb, r_buf, col_buf, sums)

    @pl.when((t == 1) & (rb == NRB - 1))
    def _():
        data = sums[...]
        for j in range(XZ):
            msg[j * TS : (j + 1) * TS, :] = data


def scatter(ids, yc, rec, size, acc_a, acc_s):
    acc_a[...] = jnp.zeros_like(acc_a)
    acc_s[...] = jnp.zeros_like(acc_s)
    for j in range(XZ):
        dev = j * YC + yc
        for k in range(2):
            a = ids[dev * 4 + k]
            a = pl.multiple_of(jnp.where(a < 0, DEV, a) * 8, 8)
            acc_a[pl.ds(a, AR), :] += rec[j * size + AR * k : j * size + AR * (k + 1), :]
            s = ids[dev * 4 + 2 + k]
            s = pl.multiple_of(jnp.where(s < 0, DEV, s) * 8, 8)
            acc_s[pl.ds(s, SR), :] += rec[j * size + 8 + SR * k : j * size + 8 + SR * (k + 1), :]
        if size == MSG:
            d = pl.multiple_of(dev * 8, 8)
            acc_s[pl.ds(d, SR), :] += rec[j * size + 24 : j * size + 32, :]
            acc_a[pl.ds(d, AR), :] += rec[j * size + 32 : j * size + 36, :]


def users_kernel(ids, me, rec, out, acc_a, acc_s):
    scatter(ids, me[1], rec, MSG, acc_a, acc_s)
    for q in range(YC):
        dev = me[0] * YC + q
        o = q * MSG
        for k in range(2):
            a = ids[dev * 4 + k]
            a = pl.multiple_of(jnp.where(a < 0, DEV, a) * 8, 8)
            out[o + AR * k : o + AR * (k + 1), :] = acc_a[pl.ds(a, AR), :]
            s = ids[dev * 4 + 2 + k]
            s = pl.multiple_of(jnp.where(s < 0, DEV, s) * 8, 8)
            out[o + 8 + SR * k : o + 8 + SR * (k + 1), :] = acc_s[pl.ds(s, SR), :]
        d = pl.multiple_of(dev * 8, 8)
        out[o + 24 : o + 32, :] = acc_s[pl.ds(d, SR), :]
        out[o + 32 : o + 36, :] = acc_a[pl.ds(d, AR), :]


def owners_kernel(ids, me, rec, out, acc_a, acc_s):
    scatter(ids, me[1], rec, TS, acc_a, acc_s)
    for q in range(YC):
        d = pl.multiple_of((me[0] * YC + q) * 8, 8)
        o = q * (AR + SR)
        out[o : o + SR, :] = acc_s[pl.ds(d, SR), :]
        out[o + SR : o + SR + AR, :] = acc_a[pl.ds(d, AR), :]


def last_kernel(rec, own, limit, cap, adv_out, slot_out):
    n = AR + SR
    total = rec[0:n, :]
    for q in range(1, YC):
        total = total + rec[q * n : (q + 1) * n, :]
    slot_out[...] = jnp.maximum(own[0:SR, :] + (total[0:SR] - cap[...]) * (1.0 / 512), 0.0)
    adv_out[...] = jnp.maximum(own[SR:n, :] + (total[SR:n] - limit[...]) * (1.0 / 1024), 0.0)


def f32(*shape):
    return jax.ShapeDtypeStruct(shape, jnp.float32)


def sweep_scratch():
    return [
        pltpu.VMEM((512, L), jnp.float32),
        pltpu.VMEM((64, L), jnp.float32),
        pltpu.VMEM((RB, L), jnp.float32),
        pltpu.VMEM((64, L), jnp.float32),
        pltpu.VMEM((TS, L), jnp.float32),
    ]


def tile_spec(n):
    return pl.BlockSpec((1, RB, 1024), lambda t, rb: (t, rb, 0))


def exchange(x, groups):
    n = x.shape[0]
    return lax.all_to_all(x, "tiles", 0, 0, axis_index_groups=groups, tiled=True)


TABLE = [pltpu.VMEM(((DEV + 1) * 8, L), jnp.float32), pltpu.VMEM(((DEV + 1) * 8, L), jnp.float32)]


def body(primal_start, cost, mask, tile_adv, tile_slot, adv_dual, slot_dual, spend_limit, capacity):
    own_adv = adv_dual.reshape(AR, L)
    own_slot = slot_dual.reshape(SR, L)
    limit = spend_limit.reshape(AR, L)
    cap = capacity.reshape(SR, L)
    index = lax.axis_index("tiles")
    me = jnp.stack([index // YC, index % YC]).astype(jnp.int32)
    present = (tile_adv >= 0).astype(jnp.float32)
    weight = (mask.astype(jnp.float32) * present[:, None, None]).reshape(-1)

    ids_row = jnp.pad(jnp.concatenate([tile_adv, tile_slot]).astype(jnp.float32), (0, L - 4))
    message = jnp.concatenate([adv_dual.reshape(-1), slot_dual.reshape(-1), ids_row])
    table = exchange(jnp.broadcast_to(message[None, :], (DEV, REC * L)), None)
    ids = table[:, (REC - 1) * L : (REC - 1) * L + 4].astype(jnp.int32).reshape(-1)

    update, sums = pl.pallas_call(
        first_kernel,
        grid=(2, NRB),
        in_specs=[SMEM_WHOLE] * 3 + [VMEM_WHOLE] * 5 + [tile_spec(0), tile_spec(0)],
        out_specs=[tile_spec(0), VMEM_WHOLE],
        out_shape=[f32(2, 512, 1024), f32(XZ * MSG, L)],
        scratch_shapes=sweep_scratch(),
        name="first",
    )(tile_adv, tile_slot, weight, table.reshape(DEV * REC, L), own_adv, own_slot, limit, cap, primal_start, cost)

    part = exchange(sums.reshape(XZ, MSG * L), XZ_GROUPS)
    wanted = pl.pallas_call(
        users_kernel,
        in_specs=[SMEM_WHOLE] * 2 + [VMEM_WHOLE],
        out_specs=VMEM_WHOLE,
        out_shape=f32(YC * MSG, L),
        scratch_shapes=TABLE,
        name="users",
    )(ids, me, part.reshape(XZ * MSG, L))
    duals = exchange(wanted.reshape(YC, MSG * L), YC_GROUPS)

    primal, sums, own = pl.pallas_call(
        second_kernel,
        grid=(2, NRB),
        in_specs=[SMEM_WHOLE, VMEM_WHOLE, tile_spec(0), tile_spec(0)],
        out_specs=[tile_spec(0), VMEM_WHOLE, VMEM_WHOLE],
        out_shape=[f32(2, 512, 1024), f32(XZ * TS, L), f32(AR + SR, L)],
        scratch_shapes=sweep_scratch() + [pltpu.VMEM((MSG, L), jnp.float32)],
        name="second",
    )(weight, duals.reshape(YC * MSG, L), update, cost)

    part = exchange(sums.reshape(XZ, TS * L), XZ_GROUPS)
    wanted = pl.pallas_call(
        owners_kernel,
        in_specs=[SMEM_WHOLE] * 2 + [VMEM_WHOLE],
        out_specs=VMEM_WHOLE,
        out_shape=f32(YC * (AR + SR), L),
        scratch_shapes=TABLE,
        name="owners",
    )(ids, me, part.reshape(XZ * TS, L))
    last = exchange(wanted.reshape(YC, (AR + SR) * L), YC_GROUPS)

    adv_out, slot_out = pl.pallas_call(
        last_kernel,
        in_specs=[VMEM_WHOLE] * 4,
        out_specs=[VMEM_WHOLE] * 2,
        out_shape=[f32(AR, L), f32(SR, L)],
        name="last",
    )(last.reshape(YC * (AR + SR), L), own, limit, cap)
    return primal, adv_out.reshape(1, 512), slot_out.reshape(1, 1024)


def solution(mesh):
    return jax.shard_map(
        body,
        mesh=mesh,
        in_specs=(
            P("tiles", None, None),
            P("tiles", None, None),
            P("tiles", None, None),
            P("tiles"),
            P("tiles"),
            P("tiles", None),
            P("tiles", None),
            P("tiles", None),
            P("tiles", None),
        ),
        out_specs=(P("tiles", None, None), P("tiles", None), P("tiles", None)),
        check_vma=False,
    )
```

time: 471 us -> 102 us (0.22)
  waiting for transfers between devices: 291 us -> 20.9 us
  blocking collectives: 140 us -> 32.1 us
  Pallas kernels: 0 us -> 22.6 us
  starting transfers between devices: 0.08 us -> 14.7 us
  other arithmetic: 16.9 us -> 3.47 us
  between operations: 14.1 us -> 0.69 us
  matrix products: 7.18 us -> 0 us
  local copies, waits for them, and re-layouts: 0.13 us -> 5.63 us
    unnamed x4 -> x0, waiting for transfers between devices: 291 us -> none
    all_gather x4 -> x0, blocking collectives: 140 us -> none  [the longest x2 71.9 us: body(): lax.all_gather(adv_dual, 'tiles', axis=0, tiled=True)]
    all_to_all x0 -> x3, blocking collectives: none -> 32.1 us  [exchange(): lax.all_to_all(x, 'tiles', 0, 0, axis_index_groups=groups, tiled=True)]
    pallas_call x0 -> x5, Pallas kernels: none -> 22.6 us  [the longest x1 8.96 us: body(): pl.pallas_call(first_kernel, grid=(2, NRB), in_specs=[SMEM_WHOLE] * 3 + [...]
    all_to_all x0 -> x2, waiting for transfers between devices: none -> 20.9 us  [exchange(): lax.all_to_all(x, 'tiles', 0, 0, axis_index_groups=groups, tiled=True)]
    all_to_all x0 -> x2, starting transfers between devices: none -> 14.7 us  [exchange(): lax.all_to_all(x, 'tiles', 0, 0, axis_index_groups=groups, tiled=True)]
    reduce_sum x2 -> x0, other arithmetic: 11.4 us -> none  [the longest x1 6.39 us: body(): jnp.sum(extended, axis=1)]
    dot_general x8 -> x0, matrix products: 7.18 us -> none  [the longest x2 2.56 us: body(): jnp.dot(slot_onehot.T, jnp.sum(extended, axis=1), precision=highest)]
  transfers between devices with their start and end apart: 2 -> 2, of which waited for: 2 -> 2; matrix products, arithmetic and copies ran while one was open for 0% -> 5% of each run, Pallas kernels for 0% -> 0%
where the time goes in v1:
time: 102 us; the launch traced here: 100 us
  blocking collectives  32.1 us (31%)
  Pallas kernels  22.6 us (22%)
  waiting for transfers between devices  20.9 us (20%)
  starting transfers between devices  14.7 us (14%)
  local copies, waits for them, and re-layouts  5.63 us (6%)
  other arithmetic  3.47 us (3%)
    all_to_all x3, blocking collectives, exchange(): lax.all_to_all(x, 'tiles', 0, 0, axis_index_groups=groups, tiled=True)  32.1 us
    all_to_all x2, waiting for transfers between devices, exchange(): lax.all_to_all(x, 'tiles', 0, 0, axis_index_groups=groups, tiled=True)  20.9 us
    all_to_all x2, starting transfers between devices, exchange(): lax.all_to_all(x, 'tiles', 0, 0, axis_index_groups=groups, tiled=True)  14.7 us
    pallas_call x1, Pallas kernels, body(): pl.pallas_call(first_kernel, grid=(2, NRB), in_specs=[SMEM_WHOLE] * 3 + [...  8.96 us
    pallas_call x1, Pallas kernels, body(): pl.pallas_call(second_kernel, grid=(2, NRB), in_specs=[SMEM_WHOLE, VMEM_W...  8.5 us
    unnamed x5, local copies, waits for them, and re-layouts  2.82 us
  transfers between devices with their start and end apart: 2, of which 2 were waited for; matrix products, arithmetic and copies ran while one was open for 5% of the time, Pallas kernels for 0%

profile of v1, /device:TPU:0, one launch (start us, length us, event | category | flops | bytes accessed | tf_op | source)
XLA Modules:
  0.0 100.1 jit_solution(16528781428024469924)
XLA Ops:
  0.6 0.8 add_convert_fusion
  1.4 0.7 select_maximum_fusion
  2.1 1.3 %broadcast_in_dim.2 = f32[128,1,1664]{2,1,0:T(1,128)} broadcast(f32[1664]{0:T(1024)S(1)} %select_maximum_fusion), dimensions={2} | broadcast | bytes 858624 | tf_op jit(solution)/shard_map/broadcast_in_dim | solution.py:226
  3.4 11.2 %all-to-all-start = ((f32[128,1,1664]{2,1,0:T(1,128)}), f32[128,1,1664]{2,1,0:T(1,128)S(1)}, u32[]{:S(2)}, u32[]{:S(2)}) async-start(f32[128,1,1664]{2,1,0:T(1,128)} %broadcast_in_dim.2), calls=%async_computation | async-start | bytes 1703936 | tf_op jit(solution)/shard_map/all_to_all | solution.py:208
  14.6 0.7 compare_convert_fusion
  15.3 0.8 convert_multiply_fusion
  16.1 0.1 copy.13
  16.2 0.7 reshape.79.w_ref
  16.8 14.8 %all-to-all-done = f32[128,1,1664]{2,1,0:T(1,128)S(1)} async-done(((f32[128,1,1664]{2,1,0:T(1,128)}), f32[128,1,1664]{2,1,0:T(1,128)S(1)}, u32[]{:S(2)}, u32[]{:S(2)}) %all-to-all-start) | async-done | bytes 852000 | tf_op jit(solution)/shard_map/all_to_all | solution.py:208
  31.6 0.0 copy-start
  31.7 0.9 copy-done
  32.6 9.0 %first.1 = (f32[2,512,1024]{2,1,0:T(8,128)}, f32[576,128]{1,0:T(8,128)}) custom-call(s32[2]{0:T(128)} %adv_id.1, s32[2]{0:T(128)} %slot_id.1, f32[1024]{0:T(1024)} %reshape.79.w_ref, f32[1664,128]{1,0:T(8,128)} %bitcast.22, f32[4,128]{1,0:T(4,128)} %bitcast.39, f32[8,128]{1,0:T(8,128)} %bitcast.35, f32[4,128]{1,0:T(4,128)} %bitcast.36, f32[8,128]{1,0:T(8,128)} %bitcast.32, ...), custom_call_target="tpu_custom_call" | custom-call | tf_op jit(solution)/shard_map/first/pallas_call | solution.py:229
  41.5 3.5 %all-to-all-start.1 = ((f32[16,1,4608]{2,1,0:T(1,128)}), f32[16,1,4608]{2,1,0:T(1,128)S(1)}, u32[]{:S(2)}, u32[]{:S(2)}) async-start(f32[16,1,4608]{2,1,0:T(1,128)} %bitcast.28), calls=%async_computation.1 | async-start | bytes 589824 | tf_op jit(solution)/shard_map/all_to_all | solution.py:208
  45.1 0.6 pad_add_fusion.me
  45.6 1.2 %copy.20 = f32[128,1,1664]{2,0,1:T(8,128)S(1)} copy(f32[128,1,1664]{2,1,0:T(1,128)} %copy-done) | data formatting | bytes 1703936
  46.9 0.7 reshape.82.ids
  47.6 6.1 %all-to-all-done.1 = f32[16,1,4608]{2,1,0:T(1,128)S(1)} async-done(((f32[16,1,4608]{2,1,0:T(1,128)}), f32[16,1,4608]{2,1,0:T(1,128)S(1)}, u32[]{:S(2)}, u32[]{:S(2)}) %all-to-all-start.1) | async-done | bytes 294944 | tf_op jit(solution)/shard_map/all_to_all | solution.py:208
  53.7 0.0 copy-start.1
  53.7 0.7 copy-done.1
  54.4 1.9 %users.1 = f32[288,128]{1,0:T(8,128)} custom-call(s32[512]{0:T(512)} %reshape.82.ids, s32[2]{0:T(128)} %pad_add_fusion.me, f32[576,128]{1,0:T(8,128)} %bitcast.23), custom_call_target="tpu_custom_call" | custom-call | tf_op jit(solution)/shard_map/users/pallas_call | solution.py:240
  56.3 10.3 %all_to_all.45 = f32[8,1,4608]{2,1,0:T(1,128)} all-to-all(f32[8,1,4608]{2,1,0:T(1,128)} %bitcast.27), channel_id=1, replica_groups={{0,1,2,3,4,5,6,7},{8,9,10,11,12,13,14,15},{16,17,18,19,20,21,22,23},{24..., dimensions={0} | all-to-all | bytes 294912 | tf_op jit(solution)/shard_map/all_to_all | solution.py:208
  66.6 8.5 %second.1 = (f32[2,512,1024]{2,1,0:T(8,128)}, f32[384,128]{1,0:T(8,128)}, f32[12,128]{1,0:T(8,128)}) custom-call(f32[1024]{0:T(1024)} %reshape.79.w_ref, f32[288,128]{1,0:T(8,128)} %bitcast.26, f32[2,512,1024]{2,1,0:T(8,128)} %get-tuple-element.11.p_ref, bf16[2,512,1024]{2,1,0:T(8,128)(2,1)} %c_ref.3), custom_call_target="tpu_custom_call" | custom-call | tf_op jit(solution)/shard_map/second/pallas_call | solution.py:250
  75.1 12.4 %all_to_all.46 = f32[16,1,3072]{2,1,0:T(1,128)} all-to-all(f32[16,1,3072]{2,1,0:T(1,128)} %bitcast.29), channel_id=1, replica_groups={{0,8,16,24,32,40,48,56,64,72,80,88,96,104,112,120},{1,9,17,25,33,41,49,..., dimensions={0} | all-to-all | bytes 393216 | tf_op jit(solution)/shard_map/all_to_all | solution.py:208
  87.5 1.8 %owners.1 = f32[96,128]{1,0:T(8,128)} custom-call(s32[512]{0:T(512)} %reshape.82.ids, s32[2]{0:T(128)} %pad_add_fusion.me, f32[384,128]{1,0:T(8,128)} %bitcast.25), custom_call_target="tpu_custom_call" | custom-call | tf_op jit(solution)/shard_map/owners/pallas_call | solution.py:261
  89.2 9.5 %all_to_all.47 = f32[8,1,1536]{2,1,0:T(1,128)} all-to-all(f32[8,1,1536]{2,1,0:T(1,128)} %bitcast.31), channel_id=1, replica_groups={{0,1,2,3,4,5,6,7},{8,9,10,11,12,13,14,15},{16,17,18,19,20,21,22,23},{24..., dimensions={0} | all-to-all | bytes 98304 | tf_op jit(solution)/shard_map/all_to_all | solution.py:208
  98.7 1.4 %last.1 = (f32[4,128]{1,0:T(4,128)}, f32[8,128]{1,0:T(8,128)}) custom-call(f32[96,128]{1,0:T(8,128)} %bitcast.30, f32[12,128]{1,0:T(8,128)} %get-tuple-element.14.own, f32[4,128]{1,0:T(4,128)} %bitcast.37, f32[8,128]{1,0:T(8,128)} %bitcast.33), custom_call_target="tpu_custom_call" | custom-call | tf_op jit(solution)/shard_map/last/pallas_call | solution.py:271
  (1 shorter events, 0.0 us)
Async XLA Ops:
  3.4 28.2 %all-to-all-start = ((f32[128,1,1664]{2,1,0:T(1,128)}), f32[128,1,1664]{2,1,0:T(1,128)S(1)}, u32[]{:S(2)}, u32[]{:S(2)}) async-start(f32[128,1,1664]{2,1,0:T(1,128)} %broadcast_in_dim.2), calls=%async_computation | async-start | bytes 1703936 | tf_op jit(solution)/shard_map/all_to_all | solution.py:208
  31.6 0.9 copy-start
  41.5 12.2 %all-to-all-start.1 = ((f32[16,1,4608]{2,1,0:T(1,128)}), f32[16,1,4608]{2,1,0:T(1,128)S(1)}, u32[]{:S(2)}, u32[]{:S(2)}) async-start(f32[16,1,4608]{2,1,0:T(1,128)} %bitcast.28), calls=%async_computation.1 | async-start | bytes 589824 | tf_op jit(solution)/shard_map/all_to_all | solution.py:208
  53.7 0.7 copy-start.1

commit v2 on v0

v2 whole, which is shorter than its diff:
```python
import jax
import jax.numpy as jnp
from jax import lax
from jax.experimental import pallas as pl
from jax.experimental.pallas import tpu as pltpu
from jax.sharding import PartitionSpec as P

CHIPS = 64
BLOCKS = 128
L = 128
AR = 4
SR = 8
OWN = AR + SR + 1
REC = 2 * OWN
TS = 2 * (AR + SR)
MSG = TS + SR + AR
OUT = SR + AR
RB = 128
NRB = 4
BIG = 1e30

CORE_GROUPS = [[j * 2 + c for j in range(CHIPS)] for c in range(2)]
PARTNERS = [(i, i ^ 1) for i in range(2 * CHIPS)]

IN_VMEM = pl.BlockSpec(memory_space=pltpu.VMEM)
IN_SMEM = pl.BlockSpec(memory_space=pltpu.SMEM)


def own_kernel(adv_id, slot_id, adv, slot, limit, cap, mask_hbm, out, bias, bounds, ids, mask, sem):
    keep_mask = pltpu.make_async_copy(mask_hbm, mask, sem)
    keep_mask.start()
    lane = lax.broadcasted_iota(jnp.int32, (1, L), 1)
    row = jnp.zeros((1, L), jnp.int32)
    for k, v in enumerate((adv_id[0], adv_id[1], slot_id[0], slot_id[1])):
        row = jnp.where(lane == k, v, row)
        ids[k] = v
    out[0:AR, :] = adv[...]
    out[AR : AR + SR, :] = slot[...]
    out[AR + SR : OWN, :] = row.astype(jnp.float32)
    bias[0:SR, :] = slot[...] * 512.0 - cap[...]
    bias[SR:OUT, :] = adv[...] * 1024.0 - limit[...]
    bounds[0:SR, :] = cap[...]
    bounds[SR:OUT, :] = limit[...]
    keep_mask.wait()


def repeat_kernel(own, other, out):
    a = own[...]
    b = other[...]
    for j in range(CHIPS):
        out[j * REC : j * REC + OWN, :] = a
        out[j * REC + OWN : (j + 1) * REC, :] = b


def spread_half(row, buf):
    for b in range(NRB):
        block = jnp.broadcast_to(0.5 * row[b : b + 1, :], (L, L))
        buf[b * L : (b + 1) * L, :] = block.T


def tree(xs):
    while len(xs) > 1:
        xs = [xs[i] + xs[i + 1] for i in range(0, len(xs), 2)]
    return xs[0]


def write_sums(t, sums, r_buf, cols):
    for b in range(NRB):
        sums[t * AR + b : t * AR + b + 1, :] = jnp.sum(r_buf[b * L : (b + 1) * L, :].T, axis=0, keepdims=True)
    rows = [jnp.sum(c, axis=0, keepdims=True) for c in cols]
    sums[8 + t * SR : 8 + (t + 1) * SR, :] = jnp.concatenate(rows, axis=0)


def slot_rows(srow):
    return [jnp.broadcast_to(0.5 * srow[cb : cb + 1, :], (8, L)) for cb in range(SR)]


ZEROS = lambda: (jnp.zeros((8, L), jnp.float32),) * SR


def first_tile(t, alive, mask, arow, srow, p_ref, c_ref, out, usum, esum, a_buf, r_buf, e_buf, ready):
    spread_half(arow, a_buf)
    s = slot_rows(srow)

    def step(g, carry):
        ucols, ecols = list(carry[0]), list(carry[1])
        us = [[], []]
        es = [[], []]
        r0 = pl.multiple_of(g * 16, 16)
        for cb in range(SR):
            lanes = pl.ds(cb * L, L)
            c16 = 0.5 * c_ref[t, pl.ds(r0, 16), lanes].astype(jnp.float32)
            for h in range(2):
                rows = pl.ds(pl.multiple_of(r0 + 8 * h, 8), 8)
                here = (mask[t, cb, g * 2 + h] > 0) & alive
                p = jnp.minimum(p_ref[t, rows, lanes], jnp.where(here, 1.0, 0.0))
                hc = jnp.maximum(c16[8 * h : 8 * h + 8], jnp.where(here, -BIG, BIG))
                u = jnp.minimum(jnp.maximum(((p - hc) - a_buf[rows, :]) - s[cb], 0.0), 1.0)
                out[t, rows, lanes] = u - hc
                e = (u - p) + u
                us[h].append(u)
                es[h].append(e)
                ucols[cb] = ucols[cb] + u
                ecols[cb] = ecols[cb] + e
        for h in range(2):
            rows = pl.ds(pl.multiple_of(r0 + 8 * h, 8), 8)
            r_buf[rows, :] = tree(us[h])
            e_buf[rows, :] = tree(es[h])
        return tuple(ucols), tuple(ecols)

    ucols, ecols = ZEROS(), ZEROS()
    for b in range(NRB):
        ready(t, b)
        ucols, ecols = lax.fori_loop(b * 8, (b + 1) * 8, step, (ucols, ecols))
    write_sums(t, usum, r_buf, ucols)
    write_sums(t, esum, e_buf, ecols)


def first_kernel(own_ids, mask, rec, bias, p_hbm, c_hbm, out, usum, msg, ids, p_ref, c_ref, a_buf, r_buf, e_buf, esum, id_buf, p_sems, c_sems, sem):
    def fetch(t, b):
        rows = pl.ds(b * RB, RB)
        n = t * NRB + b
        return (
            pltpu.make_async_copy(p_hbm.at[t, rows, :], p_ref.at[t, rows, :], p_sems.at[n]),
            pltpu.make_async_copy(c_hbm.at[t, rows, :], c_ref.at[t, rows, :], c_sems.at[n]),
        )

    for t in range(2):
        for b in range(NRB):
            for copy in fetch(t, b):
                copy.start()

    def ready(t, b):
        for copy in fetch(t, b):
            copy.wait()

    core = lax.axis_index("tiles") & 1
    both = jnp.concatenate(
        [rec[pl.ds(OWN - 1, CHIPS, stride=REC), :], rec[pl.ds(REC - 1, CHIPS, stride=REC), :]], axis=0
    )
    id_buf[...] = both.T[0:8, :].astype(jnp.int32)
    keep_ids = pltpu.make_async_copy(id_buf, ids, sem)
    keep_ids.start()
    for t in range(2):
        alive = own_ids[t] >= 0
        a = jnp.maximum(own_ids[t], 0)
        a = (a >> 1) * REC + jnp.where((a & 1) == core, 0, OWN)
        s = jnp.maximum(own_ids[2 + t], 0)
        s = (s >> 1) * REC + jnp.where((s & 1) == core, AR, OWN + AR)
        arow, srow = rec[pl.ds(a, AR), :], rec[pl.ds(s, SR), :]
        first_tile(t, alive, mask, arow, srow, p_ref, c_ref, out, usum, esum, a_buf, r_buf, e_buf, ready)
    data = jnp.concatenate([esum[...], bias[...]], axis=0)
    for j in range(CHIPS):
        msg[j * MSG : (j + 1) * MSG, :] = data
    keep_ids.wait()


def users_kernel(ids, rec, mine, other, acc_a0, acc_a1, acc_s0, acc_s1):
    me = lax.axis_index("tiles")
    chip = me >> 1
    core = me & 1

    def at(i):
        return pl.multiple_of(jnp.where(i < 0, BLOCKS, i) * 8, 8)

    wanted = []
    for side, out, index in ((0, mine, me), (CHIPS, other, me ^ 1)):
        adv = [(ids[k, side + chip], AR * k) for k in range(2)] + [(index, TS + SR)]
        slot = [(ids[2 + k, side + chip], 8 + SR * k) for k in range(2)] + [(index, TS)]
        wanted.append((out, adv, slot))
    zero = jnp.zeros((8, L), jnp.float32)
    for _, adv, slot in wanted:
        for i, _ in adv:
            acc_a0[pl.ds(at(i), 8), :] = zero
            acc_a1[pl.ds(at(i), 8), :] = zero
        for i, _ in slot:
            acc_s0[pl.ds(at(i), 8), :] = zero
            acc_s1[pl.ds(at(i), 8), :] = zero
    for j in range(CHIPS):
        for k, acc in ((0, acc_a0), (1, acc_a1)):
            rows = pl.ds(at(ids[k, j]), AR)
            acc[rows, :] = acc[rows, :] + rec[j * MSG + AR * k : j * MSG + AR * (k + 1), :]
        for k, acc in ((0, acc_s0), (1, acc_s1)):
            rows = pl.ds(at(ids[2 + k, j]), SR)
            acc[rows, :] = acc[rows, :] + rec[j * MSG + 8 + SR * k : j * MSG + 8 + SR * (k + 1), :]
    for out, adv, slot in wanted:
        for i, o in adv:
            b = jnp.maximum(i, 0)
            bias = rec[pl.ds((b >> 1) * MSG + TS + SR, AR), :] * jnp.where((b & 1) == core, 1.0, 0.0)
            rows = pl.ds(at(i), AR)
            out[o : o + AR, :] = (acc_a0[rows, :] + acc_a1[rows, :]) + bias
        for i, o in slot:
            b = jnp.maximum(i, 0)
            bias = rec[pl.ds((b >> 1) * MSG + TS, SR), :] * jnp.where((b & 1) == core, 1.0, 0.0)
            rows = pl.ds(at(i), SR)
            out[o : o + SR, :] = (acc_s0[rows, :] + acc_s1[rows, :]) + bias


def second_tile(t, arow, srow, base, out, usum, a_buf, r_buf, done):
    spread_half(arow, a_buf)
    s = slot_rows(srow)

    def step(g, cols):
        rows = pl.ds(pl.multiple_of(g * 8, 8), 8)
        a = a_buf[rows, :]
        cols = list(cols)
        us = []
        for cb in range(SR):
            lanes = pl.ds(cb * L, L)
            u = jnp.minimum(jnp.maximum((base[t, rows, lanes] - a) - s[cb], 0.0), 1.0)
            out[t, rows, lanes] = u
            cols[cb] = cols[cb] + u
            us.append(u)
        r_buf[rows, :] = tree(us)
        return tuple(cols)

    cols = ZEROS()
    for b in range(NRB):
        cols = lax.fori_loop(b * 16, (b + 1) * 16, step, cols, unroll=4)
        done(t, b)
    write_sums(t, usum, r_buf, cols)


def second_kernel(mine, other, base, psum, primal, sums, own, out, usum, a_buf, r_buf, sems):
    def keep(t, b):
        rows = pl.ds(b * RB, RB)
        return pltpu.make_async_copy(out.at[t, rows, :], primal.at[t, rows, :], sems.at[t * NRB + b])

    total = mine[...] + other[...]
    adv = jnp.maximum(total[0:8] * (1.0 / 1024), 0.0)
    slot = jnp.maximum(total[8:32] * (1.0 / 512), 0.0)
    own[0:SR, :] = slot[16:24]
    own[SR:OUT, :] = jnp.maximum(total[32:36] * (1.0 / 1024), 0.0)
    for t in range(2):
        second_tile(
            t, adv[4 * t : 4 * t + 4], slot[8 * t : 8 * t + 8], base, out, usum, a_buf, r_buf, lambda t, b: keep(t, b).start()
        )
    sums[...] = 2.0 * usum[...] - psum[...]
    for t in range(2):
        for b in range(NRB):
            keep(t, b).wait()


def owners_kernel(ids, mine, other, out):
    me = lax.axis_index("tiles")
    chip = me >> 1
    core = me & 1
    out[...] = jnp.zeros_like(out)
    for side, rec in ((0, mine), (CHIPS, other)):
        for k in range(2):
            for i, o, n, src in (
                (ids[k, side + chip], SR, AR, AR * k),
                (ids[2 + k, side + chip], 0, SR, 8 + SR * k),
            ):

                @pl.when((i >= 0) & ((i & 1) == core))
                def _():
                    rows = pl.ds((i >> 1) * OUT + o, n)
                    out[rows, :] = out[rows, :] + rec[src : src + n, :]


def last_kernel(rec, own, bounds, adv_out, slot_out):
    n = 2 * OUT
    parts = [rec[g * n : (g + 1) * n, :] for g in range(CHIPS // 2)]
    total = tree(parts)
    total = total[0:OUT] + total[OUT:n]
    slot_out[...] = jnp.maximum(own[0:SR, :] + (total[0:SR] - bounds[0:SR, :]) * (1.0 / 512), 0.0)
    adv_out[...] = jnp.maximum(own[SR:OUT, :] + (total[SR:OUT] - bounds[SR:OUT, :]) * (1.0 / 1024), 0.0)


def f32(*shape):
    return jax.ShapeDtypeStruct(shape, jnp.float32)


def vmem(*shape):
    return pltpu.VMEM(shape, jnp.float32)


def in_vmem(x):
    return pltpu.with_memory_space_constraint(x, pltpu.VMEM)


def in_smem(x):
    return pltpu.with_memory_space_constraint(x, pltpu.SMEM)


def call(kernel, name, ins, outs, scratch=(), mib=4):
    return pl.pallas_call(
        kernel,
        in_specs=[s for _, s in ins],
        out_specs=[s for _, s in outs],
        out_shape=[o for o, _ in outs],
        scratch_shapes=list(scratch),
        compiler_params=pltpu.CompilerParams(vmem_limit_bytes=mib << 20),
        name=name,
    )(*[x for x, _ in ins])


def in_hbm(x):
    return pltpu.with_memory_space_constraint(x, pltpu.HBM)


def hbm_arg(x):
    return (in_hbm(x), pl.BlockSpec(memory_space=pl.ANY))


def smem_out(*shape):
    return (pltpu.SMEM(shape, jnp.int32), IN_SMEM)


def smem_arg(x):
    return (in_smem(x), IN_SMEM)


def vmem_arg(x):
    return (in_vmem(x), IN_VMEM)


def vmem_out(*shape):
    return (vmem(*shape), IN_VMEM)


def exchange(x, rows):
    x = x.reshape(CHIPS, rows * L)
    x = lax.all_to_all(x, "tiles", 0, 0, axis_index_groups=CORE_GROUPS, tiled=True)
    return vmem_arg(x.reshape(CHIPS * rows, L))


def swap(x):
    return lax.ppermute(x, "tiles", PARTNERS)


def body(primal_start, cost, mask, tile_adv, tile_slot, adv_dual, slot_dual, spend_limit, capacity):
    tile = (2, 512, 1024)
    own, bias, bounds, own_ids, here = call(
        own_kernel,
        "own",
        [(in_hbm(tile_adv), IN_SMEM), (in_hbm(tile_slot), IN_SMEM)]
        + [(in_hbm(x.reshape(-1, L)), IN_VMEM) for x in (adv_dual, slot_dual, spend_limit, capacity)]
        + [hbm_arg(mask.transpose(0, 2, 1))],
        [vmem_out(OWN, L), vmem_out(OUT, L), vmem_out(OUT, L), smem_out(4), smem_out(2, 8, 64)],
        [pltpu.SemaphoreType.DMA(())],
    )
    (message,) = call(repeat_kernel, "repeat", [vmem_arg(own), vmem_arg(swap(own))], [vmem_out(CHIPS * REC, L)])
    table = exchange(message, REC)

    base, usum, message, ids = call(
        first_kernel,
        "first",
        [smem_arg(own_ids), smem_arg(here), table, vmem_arg(bias), hbm_arg(primal_start), hbm_arg(cost)],
        [vmem_out(*tile), vmem_out(TS, L), vmem_out(CHIPS * MSG, L), smem_out(8, L)],
        [vmem(*tile), pltpu.VMEM(tile, jnp.bfloat16)]
        + [vmem(512, L)] * 3
        + [vmem(TS, L), pltpu.VMEM((8, L), jnp.int32)]
        + [pltpu.SemaphoreType.DMA((2 * NRB,))] * 2
        + [pltpu.SemaphoreType.DMA(())],
        8,
    )
    part = exchange(message, MSG)
    mine, other = call(
        users_kernel,
        "users",
        [smem_arg(ids), part],
        [vmem_out(MSG, L), vmem_out(MSG, L)],
        [vmem((BLOCKS + 1) * 8, L)] * 4,
    )

    primal, sums, own = call(
        second_kernel,
        "second",
        [vmem_arg(mine), vmem_arg(swap(other)), vmem_arg(base), vmem_arg(usum)],
        [(f32(*tile), pl.BlockSpec(memory_space=pl.ANY)), vmem_out(TS, L), vmem_out(OUT, L)],
        [vmem(*tile), vmem(TS, L), vmem(512, L), vmem(512, L), pltpu.SemaphoreType.DMA((2 * NRB,))],
        8,
    )
    (message,) = call(
        owners_kernel, "owners", [smem_arg(ids), vmem_arg(sums), vmem_arg(swap(sums))], [vmem_out(CHIPS * OUT, L)]
    )
    adv_out, slot_out = call(
        last_kernel,
        "last",
        [exchange(message, OUT), vmem_arg(own), vmem_arg(bounds)],
        [(f32(AR, L), IN_VMEM), (f32(SR, L), IN_VMEM)],
    )
    return primal, adv_out.reshape(1, 512), slot_out.reshape(1, 1024)


def solution(mesh):
    return jax.shard_map(
        body,
        mesh=mesh,
        in_specs=(
            P("tiles", None, None),
            P("tiles", None, None),
            P("tiles", None, None),
            P("tiles"),
            P("tiles"),
            P("tiles", None),
            P("tiles", None),
            P("tiles", None),
            P("tiles", None),
        ),
        out_specs=(P("tiles", None, None), P("tiles", None), P("tiles", None)),
        check_vma=False,
    )
```

time: 471 us -> 84 us (0.18)
  waiting for transfers between devices: 291 us -> 3.35 us
  blocking collectives: 140 us -> 68.5 us
  other arithmetic: 16.9 us -> 0 us
  between operations: 14.1 us -> 0.69 us
  Pallas kernels: 0 us -> 10.8 us
  matrix products: 7.18 us -> 0 us
    unnamed x4 -> x0, waiting for transfers between devices: 291 us -> none
    all_gather x4 -> x0, blocking collectives: 140 us -> none  [the longest x2 71.9 us: body(): lax.all_gather(adv_dual, 'tiles', axis=0, tiled=True)]
    all_to_all x0 -> x3, blocking collectives: none -> 68.5 us  [exchange(): lax.all_to_all(x, 'tiles', 0, 0, axis_index_groups=CORE_GROUPS, tiled=True)]
    reduce_sum x2 -> x0, other arithmetic: 11.4 us -> none  [the longest x1 6.39 us: body(): jnp.sum(extended, axis=1)]
    pallas_call x0 -> x7, Pallas kernels: none -> 10.8 us  [call(): pl.pallas_call(kernel, in_specs=[s for _, s in ins], out_specs=[s for _,...]
    dot_general x8 -> x0, matrix products: 7.18 us -> none  [the longest x2 2.56 us: body(): jnp.dot(slot_onehot.T, jnp.sum(extended, axis=1), precision=highest)]
  transfers between devices with their start and end apart: 2 -> 3, of which waited for: 2 -> 3; matrix products, arithmetic and copies ran while one was open for 0% -> 0% of each run, Pallas kernels for 0% -> 0%
where the time goes in v2:
time: 84 us; the launch traced here: 83.7 us
  blocking collectives  68.5 us (82%)
  Pallas kernels  10.8 us (13%)
  waiting for transfers between devices  3.35 us (4%)
    all_to_all x3, blocking collectives, exchange(): lax.all_to_all(x, 'tiles', 0, 0, axis_index_groups=CORE_GROUPS, tiled=True)  68.5 us
    pallas_call x7, Pallas kernels, call(): pl.pallas_call(kernel, in_specs=[s for _, s in ins], out_specs=[s for _,...  10.8 us
    ppermute x3, waiting for transfers between devices, swap(): return lax.ppermute(x, 'tiles', PARTNERS)  3.35 us
  transfers between devices with their start and end apart: 3, of which 3 were waited for; matrix products, arithmetic and copies ran while one was open for 0% of the time, Pallas kernels for 0%

profile of v2, /device:TPU:0, one launch (start us, length us, event | category | flops | bytes accessed | tf_op | source)
XLA Modules:
  0.0 83.7 jit_solution(17931357302158241892)
XLA Ops:
  0.6 1.6 %own.1 = (f32[13,128]{1,0:T(8,128)S(1)}, f32[12,128]{1,0:T(8,128)S(1)}, f32[12,128]{1,0:T(8,128)S(1)}, s32[4]{0:T(128)S(4)}, s32[2,8,64]{2,1,0:T(8,128)S(4)}) custom-call(s32[2]{0:T(128)} %adv_id.1, s32[2]{0:T(128)} %slot_id.1, f32[4,128]{1,0:T(4,128)} %bitcast.22, f32[8,128]{1,0:T(8,128)} %bitcast.20, f32[4,128]{1,0:T(4,128)} %bitcast.23, ...), custom_call_target="tpu_custom_call" | custom-call | tf_op jit(solution)/shard_map/own/pallas_call | solution.py:288
  2.2 0.1 collective-permute-start
  2.3 1.2 %collective-permute-done.other = f32[13,128]{1,0:T(8,128)S(1)} collective-permute-done((f32[13,128]{1,0:T(8,128)S(1)}, f32[13,128]{1,0:T(8,128)S(1)}, u32[]{:S(2)}, u32[]{:S(2)}) %collective-permute-start) | collective-permute-done | bytes 6688 | tf_op jit(solution)/shard_map/ppermute | solution.py:330
  3.5 0.1 repeat.1
  3.6 28.2 %all_to_all.27 = f32[64,1,3328]{2,1,0:T(1,128)S(1)} all-to-all(f32[64,1,3328]{2,1,0:T(1,128)S(1)} %bitcast.15), channel_id=1, replica_groups={{0,2,4,6,8,10,12,14,16,18,20,22,24,26,28,30,32,34,36,38,40,42,44,46,48,..., dimensions={0} | all-to-all | bytes 1703936 | tf_op jit(solution)/shard_map/all_to_all | solution.py:325
  31.8 5.6 %first.1 = (f32[2,512,1024]{2,1,0:T(8,128)S(1)}, f32[24,128]{1,0:T(8,128)S(1)}, f32[2304,128]{1,0:T(8,128)S(1)}, s32[8,128]{1,0:T(8,128)S(4)}) custom-call(s32[4]{0:T(128)S(4)} %get-tuple-element.19.own_ids, s32[2,8,64]{2,1,0:T(8,128)S(4)} %get-tuple-element.20.mask, f32[1664,128]{1,0:T(8,128)S(1)} %bitcast.14, f32[12,128]{1,0:T(8,128)S(1)} %get-tuple-element.22.bias, ...), custom_call_target="tpu_custom_call" | custom-call | tf_op jit(solution)/shard_map/first/pallas_call | solution.py:288
  37.4 23.6 %all_to_all.28 = f32[64,1,4608]{2,1,0:T(1,128)S(1)} all-to-all(f32[64,1,4608]{2,1,0:T(1,128)S(1)} %bitcast.18), channel_id=1, replica_groups={{0,2,4,6,8,10,12,14,16,18,20,22,24,26,28,30,32,34,36,38,40,42,44,46,48,..., dimensions={0} | all-to-all | bytes 2359296 | tf_op jit(solution)/shard_map/all_to_all | solution.py:325
  61.0 0.5 users.1
  61.4 0.1 collective-permute-start.1
  61.5 1.2 %collective-permute-done.1.other = f32[36,128]{1,0:T(8,128)S(1)} collective-permute-done((f32[36,128]{1,0:T(8,128)S(1)}, f32[36,128]{1,0:T(8,128)S(1)}, u32[]{:S(2)}, u32[]{:S(2)}) %collective-permute-start.1) | collective-permute-done | bytes 18464 | tf_op jit(solution)/shard_map/ppermute | solution.py:330
  62.7 2.3 %second.1 = (f32[2,512,1024]{2,1,0:T(8,128)}, f32[24,128]{1,0:T(8,128)S(1)}, f32[12,128]{1,0:T(8,128)S(1)}) custom-call(f32[36,128]{1,0:T(8,128)S(1)} %get-tuple-element.25.mine, f32[36,128]{1,0:T(8,128)S(1)} %collective-permute-done.1.other, f32[2,512,1024]{2,1,0:T(8,128)S(1)} %get-tuple-element.27.base, f32[24,128]{1,0:T(8,128)S(1)} %get-tuple-element.28.psum), custom_call_target="tpu_custom_call" | custom-call | tf_op jit(solution)/shard_map/second/pallas_call | solution.py:288
  65.0 0.2 collective-permute-start.2
  65.3 1.0 %collective-permute-done.2.other = f32[24,128]{1,0:T(8,128)S(1)} collective-permute-done((f32[24,128]{1,0:T(8,128)S(1)}, f32[24,128]{1,0:T(8,128)S(1)}, u32[]{:S(2)}, u32[]{:S(2)}) %collective-permute-start.2) | collective-permute-done | bytes 12320 | tf_op jit(solution)/shard_map/ppermute | solution.py:330
  66.3 0.1 owners.1
  66.4 16.7 %all_to_all.29 = f32[64,1,1536]{2,1,0:T(1,128)S(1)} all-to-all(f32[64,1,1536]{2,1,0:T(1,128)S(1)} %bitcast.17), channel_id=1, replica_groups={{0,2,4,6,8,10,12,14,16,18,20,22,24,26,28,30,32,34,36,38,40,42,44,46,48,..., dimensions={0} | all-to-all | bytes 786432 | tf_op jit(solution)/shard_map/all_to_all | solution.py:325
  83.1 0.6 last.1
Async XLA Ops:
  2.2 1.3 %collective-permute-start = (f32[13,128]{1,0:T(8,128)S(1)}, f32[13,128]{1,0:T(8,128)S(1)}, u32[]{:S(2)}, u32[]{:S(2)}) collective-permute-start(f32[13,128]{1,0:T(8,128)S(1)} %get-tuple-element.21.own), channel_id=1, source_target_pairs={{0,1},{1,0},{2,3},{3,2},{4,5},{5,4},{6,7},{7,6},{8,9},{9,8},{10,11... | collective-permute-start | bytes 19976 | tf_op jit(solution)/shard_map/ppermute | solution.py:330
  61.4 1.3 %collective-permute-start.1 = (f32[36,128]{1,0:T(8,128)S(1)}, f32[36,128]{1,0:T(8,128)S(1)}, u32[]{:S(2)}, u32[]{:S(2)}) collective-permute-start(f32[36,128]{1,0:T(8,128)S(1)} %get-tuple-element.26), channel_id=1, source_target_pairs={{0,1},{1,0},{2,3},{3,2},{4,5},{5,4},{6,7},{7,6},{8,9},{9,8},{10,11... | collective-permute-start | bytes 55304 | tf_op jit(solution)/shard_map/ppermute | solution.py:330
  65.0 1.3 %collective-permute-start.2 = (f32[24,128]{1,0:T(8,128)S(1)}, f32[24,128]{1,0:T(8,128)S(1)}, u32[]{:S(2)}, u32[]{:S(2)}) collective-permute-start(f32[24,128]{1,0:T(8,128)S(1)} %get-tuple-element.30.mine), channel_id=1, source_target_pairs={{0,1},{1,0},{2,3},{3,2},{4,5},{5,4},{6,7},{7,6},{8,9},{9,8},{10,11... | collective-permute-start | bytes 36872 | tf_op jit(solution)/shard_map/ppermute | solution.py:330

commit v3 on v2

--- a/solution.py
+++ b/solution.py
@@ -11,13 +11,14 @@
 AR = 4
 SR = 8
 OWN = AR + SR + 1
-REC = 2 * OWN
+SEL = 2 * (AR + SR) + 8
 TS = 2 * (AR + SR)
 MSG = TS + SR + AR
 OUT = SR + AR
 RB = 128
 NRB = 4
 BIG = 1e30
+AHEAD = 3
 
 CORE_GROUPS = [[j * 2 + c for j in range(CHIPS)] for c in range(2)]
 PARTNERS = [(i, i ^ 1) for i in range(2 * CHIPS)]
@@ -26,17 +27,18 @@
 IN_SMEM = pl.BlockSpec(memory_space=pltpu.SMEM)
 
 
-def own_kernel(adv_id, slot_id, adv, slot, limit, cap, mask_hbm, out, bias, bounds, ids, mask, sem):
+def own_kernel(adv_id, slot_id, adv, slot, limit, cap, mask_hbm, out, bias, bounds, row_ids, ids, mask, sem):
     keep_mask = pltpu.make_async_copy(mask_hbm, mask, sem)
     keep_mask.start()
-    lane = lax.broadcasted_iota(jnp.int32, (1, L), 1)
-    row = jnp.zeros((1, L), jnp.int32)
+    lane = lax.broadcasted_iota(jnp.int32, (8, L), 1)
+    row = jnp.zeros((8, L), jnp.int32)
     for k, v in enumerate((adv_id[0], adv_id[1], slot_id[0], slot_id[1])):
         row = jnp.where(lane == k, v, row)
         ids[k] = v
-    out[0:AR, :] = adv[...]
-    out[AR : AR + SR, :] = slot[...]
-    out[AR + SR : OWN, :] = row.astype(jnp.float32)
+    row_ids[...] = row
+    data = jnp.concatenate([slot[...], adv[...], row[0:1].astype(jnp.float32)], axis=0)
+    for j in range(CHIPS):
+        out[j * OWN : (j + 1) * OWN, :] = data
     bias[0:SR, :] = slot[...] * 512.0 - cap[...]
     bias[SR:OUT, :] = adv[...] * 1024.0 - limit[...]
     bounds[0:SR, :] = cap[...]
@@ -44,12 +46,20 @@
     keep_mask.wait()
 
 
-def repeat_kernel(own, other, out):
-    a = own[...]
-    b = other[...]
-    for j in range(CHIPS):
-        out[j * REC : j * REC + OWN, :] = a
-        out[j * REC + OWN : (j + 1) * REC, :] = b
+def rows_of(rec, i, slot):
+    at = (jnp.maximum(i, 0) >> 1) * OWN
+    return rec[pl.ds(at, SR), :] if slot else rec[pl.ds(at + SR, AR), :]
+
+
+def pick_kernel(partner_ids, rec, out):
+    lane = lax.broadcasted_iota(jnp.int32, (1, L), 1)
+    row = partner_ids[0:1, :]
+    wanted = [jnp.max(jnp.where(lane == k, row, -1)) for k in range(4)]
+    for k in range(2):
+        out[AR * k : AR * (k + 1), :] = rows_of(rec, wanted[k], False)
+        out[8 + SR * k : 8 + SR * (k + 1), :] = rows_of(rec, wanted[2 + k], True)
+    ids = rec[pl.ds(OWN - 1, CHIPS, stride=OWN), :]
+    out[TS:SEL, :] = jnp.concatenate([ids, ids], axis=0).T[0:8, :]
 
 
 def spread_half(row, buf):
@@ -78,14 +88,14 @@
 ZEROS = lambda: (jnp.zeros((8, L), jnp.float32),) * SR
 
 
-def first_tile(t, alive, mask, arow, srow, p_ref, c_ref, out, usum, esum, a_buf, r_buf, e_buf, ready):
+def first_tile(t, alive, mask, arow, srow, p_ref, c_ref, out, usum, psum, a_buf, r_buf, q_buf, ready):
     spread_half(arow, a_buf)
     s = slot_rows(srow)
 
     def step(g, carry):
-        ucols, ecols = list(carry[0]), list(carry[1])
+        ucols, pcols = list(carry[0]), list(carry[1])
         us = [[], []]
-        es = [[], []]
+        ps = [[], []]
         r0 = pl.multiple_of(g * 16, 16)
         for cb in range(SR):
             lanes = pl.ds(cb * L, L)
@@ -97,59 +107,56 @@
                 hc = jnp.maximum(c16[8 * h : 8 * h + 8], jnp.where(here, -BIG, BIG))
                 u = jnp.minimum(jnp.maximum(((p - hc) - a_buf[rows, :]) - s[cb], 0.0), 1.0)
                 out[t, rows, lanes] = u - hc
-                e = (u - p) + u
                 us[h].append(u)
-                es[h].append(e)
+                ps[h].append(p)
                 ucols[cb] = ucols[cb] + u
-                ecols[cb] = ecols[cb] + e
+                pcols[cb] = pcols[cb] + p
         for h in range(2):
             rows = pl.ds(pl.multiple_of(r0 + 8 * h, 8), 8)
             r_buf[rows, :] = tree(us[h])
-            e_buf[rows, :] = tree(es[h])
-        return tuple(ucols), tuple(ecols)
-
-    ucols, ecols = ZEROS(), ZEROS()
+            q_buf[rows, :] = tree(ps[h])
+        return tuple(ucols), tuple(pcols)
+
+    ucols, pcols = ZEROS(), ZEROS()
     for b in range(NRB):
-        ready(t, b)
-        ucols, ecols = lax.fori_loop(b * 8, (b + 1) * 8, step, (ucols, ecols))
+        ready(t * NRB + b)
+        ucols, pcols = lax.fori_loop(b * 8, (b + 1) * 8, step, (ucols, pcols))
     write_sums(t, usum, r_buf, ucols)
-    write_sums(t, esum, e_buf, ecols)
-
-
-def first_kernel(own_ids, mask, rec, bias, p_hbm, c_hbm, out, usum, msg, ids, p_ref, c_ref, a_buf, r_buf, e_buf, esum, id_buf, p_sems, c_sems, sem):
-    def fetch(t, b):
+    write_sums(t, psum, q_buf, pcols)
+
+
+def first_kernel(own_ids, mask, rec, mine, other, bias, p_hbm, c_hbm, out, usum, msg, ids, p_ref, c_ref, a_buf, r_buf, q_buf, psum, id_buf, p_sems, c_sems, sem):
+    def fetch(n):
+        t, b = divmod(n, NRB)
         rows = pl.ds(b * RB, RB)
-        n = t * NRB + b
         return (
             pltpu.make_async_copy(p_hbm.at[t, rows, :], p_ref.at[t, rows, :], p_sems.at[n]),
             pltpu.make_async_copy(c_hbm.at[t, rows, :], c_ref.at[t, rows, :], c_sems.at[n]),
         )
 
-    for t in range(2):
-        for b in range(NRB):
-            for copy in fetch(t, b):
-                copy.start()
-
-    def ready(t, b):
-        for copy in fetch(t, b):
+    def start(n):
+        for copy in fetch(n):
+            copy.start()
+
+    def ready(n):
+        if n + AHEAD < 2 * NRB:
+            start(n + AHEAD)
+        for copy in fetch(n):
             copy.wait()
 
+    for n in range(AHEAD):
+        start(n)
     core = lax.axis_index("tiles") & 1
-    both = jnp.concatenate(
-        [rec[pl.ds(OWN - 1, CHIPS, stride=REC), :], rec[pl.ds(REC - 1, CHIPS, stride=REC), :]], axis=0
-    )
-    id_buf[...] = both.T[0:8, :].astype(jnp.int32)
+    id_buf[0:4, :] = mine[TS : TS + 4, :].astype(jnp.int32)
+    id_buf[4:8, :] = other[TS : TS + 4, :].astype(jnp.int32)
     keep_ids = pltpu.make_async_copy(id_buf, ids, sem)
     keep_ids.start()
     for t in range(2):
-        alive = own_ids[t] >= 0
-        a = jnp.maximum(own_ids[t], 0)
-        a = (a >> 1) * REC + jnp.where((a & 1) == core, 0, OWN)
-        s = jnp.maximum(own_ids[2 + t], 0)
-        s = (s >> 1) * REC + jnp.where((s & 1) == core, AR, OWN + AR)
-        arow, srow = rec[pl.ds(a, AR), :], rec[pl.ds(s, SR), :]
-        first_tile(t, alive, mask, arow, srow, p_ref, c_ref, out, usum, esum, a_buf, r_buf, e_buf, ready)
-    data = jnp.concatenate([esum[...], bias[...]], axis=0)
+        a, s = own_ids[t], own_ids[2 + t]
+        arow = jnp.where((a & 1) == core, rows_of(rec, a, False), other[AR * t : AR * (t + 1), :])
+        srow = jnp.where((s & 1) == core, rows_of(rec, s, True), other[8 + SR * t : 8 + SR * (t + 1), :])
+        first_tile(t, a >= 0, mask, arow, srow, p_ref, c_ref, out, usum, psum, a_buf, r_buf, q_buf, ready)
+    data = jnp.concatenate([2.0 * usum[...] - psum[...], bias[...]], axis=0)
     for j in range(CHIPS):
         msg[j * MSG : (j + 1) * MSG, :] = data
     keep_ids.wait()
@@ -164,9 +171,9 @@
         return pl.multiple_of(jnp.where(i < 0, BLOCKS, i) * 8, 8)
 
     wanted = []
-    for side, out, index in ((0, mine, me), (CHIPS, other, me ^ 1)):
-        adv = [(ids[k, side + chip], AR * k) for k in range(2)] + [(index, TS + SR)]
-        slot = [(ids[2 + k, side + chip], 8 + SR * k) for k in range(2)] + [(index, TS)]
+    for side, out, index in ((0, mine, me), (4, other, me ^ 1)):
+        adv = [(ids[side + k, chip], AR * k) for k in range(2)] + [(index, TS + SR)]
+        slot = [(ids[side + 2 + k, chip], 8 + SR * k) for k in range(2)] + [(index, TS)]
         wanted.append((out, adv, slot))
     zero = jnp.zeros((8, L), jnp.float32)
     for _, adv, slot in wanted:
@@ -246,11 +253,11 @@
     chip = me >> 1
     core = me & 1
     out[...] = jnp.zeros_like(out)
-    for side, rec in ((0, mine), (CHIPS, other)):
+    for side, rec in ((0, mine), (4, other)):
         for k in range(2):
             for i, o, n, src in (
-                (ids[k, side + chip], SR, AR, AR * k),
-                (ids[2 + k, side + chip], 0, SR, 8 + SR * k),
+                (ids[side + k, chip], SR, AR, AR * k),
+                (ids[side + 2 + k, chip], 0, SR, 8 + SR * k),
             ):
 
                 @pl.when((i >= 0) & ((i & 1) == core))
@@ -332,22 +339,23 @@
 
 def body(primal_start, cost, mask, tile_adv, tile_slot, adv_dual, slot_dual, spend_limit, capacity):
     tile = (2, 512, 1024)
-    own, bias, bounds, own_ids, here = call(
+    message, bias, bounds, row_ids, own_ids, here = call(
         own_kernel,
         "own",
         [(in_hbm(tile_adv), IN_SMEM), (in_hbm(tile_slot), IN_SMEM)]
         + [(in_hbm(x.reshape(-1, L)), IN_VMEM) for x in (adv_dual, slot_dual, spend_limit, capacity)]
         + [hbm_arg(mask.transpose(0, 2, 1))],
-        [vmem_out(OWN, L), vmem_out(OUT, L), vmem_out(OUT, L), smem_out(4), smem_out(2, 8, 64)],
+        [vmem_out(CHIPS * OWN, L), vmem_out(OUT, L), vmem_out(OUT, L)]
+        + [(pltpu.VMEM((8, L), jnp.int32), IN_VMEM), smem_out(4), smem_out(2, 8, 64)],
         [pltpu.SemaphoreType.DMA(())],
     )
-    (message,) = call(repeat_kernel, "repeat", [vmem_arg(own), vmem_arg(swap(own))], [vmem_out(CHIPS * REC, L)])
-    table = exchange(message, REC)
+    table = exchange(message, OWN)
+    (picked,) = call(pick_kernel, "pick", [vmem_arg(swap(row_ids)), table], [vmem_out(SEL, L)])
 
     base, usum, message, ids = call(
         first_kernel,
         "first",
-        [smem_arg(own_ids), smem_arg(here), table, vmem_arg(bias), hbm_arg(primal_start), hbm_arg(cost)],
+        [smem_arg(own_ids), smem_arg(here), table, vmem_arg(picked), vmem_arg(swap(picked)), vmem_arg(bias)] + [hbm_arg(primal_start), hbm_arg(cost)],
         [vmem_out(*tile), vmem_out(TS, L), vmem_out(CHIPS * MSG, L), smem_out(8, L)],
         [vmem(*tile), pltpu.VMEM(tile, jnp.bfloat16)]
         + [vmem(512, L)] * 3

time: 84 us -> 81.7 us (0.973)
  blocking collectives: 68.5 us -> 41.7 us
  waiting for transfers between devices: 3.35 us -> 15.4 us
  starting transfers between devices: 0.41 us -> 12 us
    all_to_all x3 -> x2, blocking collectives: 68.5 us -> 41.7 us  [exchange(): lax.all_to_all(x, 'tiles', 0, 0, axis_index_groups=CORE_GROUPS, tiled=True)]
    all_to_all x0 -> x1, starting transfers between devices: none -> 11.5 us  [exchange(): lax.all_to_all(x, 'tiles', 0, 0, axis_index_groups=CORE_GROUPS, tiled=True)]
    all_to_all x0 -> x1, waiting for transfers between devices: none -> 10.9 us  [exchange(): lax.all_to_all(x, 'tiles', 0, 0, axis_index_groups=CORE_GROUPS, tiled=True)]
    ppermute x3 -> x4, waiting for transfers between devices: 3.35 us -> 4.51 us  [swap(): return lax.ppermute(x, 'tiles', PARTNERS)]
  transfers between devices with their start and end apart: 3 -> 5, of which waited for: 3 -> 5; matrix products, arithmetic and copies ran while one was open for 0% -> 0% of each run, Pallas kernels for 0% -> 0%
where the time goes in v3:
time: 81.7 us; the launch traced here: 81.4 us
  blocking collectives  41.7 us (51%)
  waiting for transfers between devices  15.4 us (19%)
  starting transfers between devices  12 us (15%)
  Pallas kernels  11.6 us (14%)
    all_to_all x2, blocking collectives, exchange(): lax.all_to_all(x, 'tiles', 0, 0, axis_index_groups=CORE_GROUPS, tiled=True)  41.7 us
    pallas_call x7, Pallas kernels, call(): pl.pallas_call(kernel, in_specs=[s for _, s in ins], out_specs=[s for _,...  11.6 us
    all_to_all x1, starting transfers between devices, exchange(): lax.all_to_all(x, 'tiles', 0, 0, axis_index_groups=CORE_GROUPS, tiled=True)  11.5 us
    all_to_all x1, waiting for transfers between devices, exchange(): lax.all_to_all(x, 'tiles', 0, 0, axis_index_groups=CORE_GROUPS, tiled=True)  10.9 us
    ppermute x4, waiting for transfers between devices, swap(): return lax.ppermute(x, 'tiles', PARTNERS)  4.51 us
  transfers between devices with their start and end apart: 5, of which 5 were waited for; matrix products, arithmetic and copies ran while one was open for 0% of the time, Pallas kernels for 0%

profile of v3, /device:TPU:0, one launch (start us, length us, event | category | flops | bytes accessed | tf_op | source)
XLA Modules:
  0.0 81.4 jit_solution(5161487367348142662)
XLA Ops:
  0.6 2.4 %own.1 = (f32[832,128]{1,0:T(8,128)}, f32[12,128]{1,0:T(8,128)S(1)}, f32[12,128]{1,0:T(8,128)S(1)}, s32[8,128]{1,0:T(8,128)S(1)}, s32[4]{0:T(128)S(4)}, /*index=5*/s32[2,8,64]{2,1,0:T(8,128)S(4)}) custom-call(s32[2]{0:T(128)} %adv_id.1, s32[2]{0:T(128)} %slot_id.1, f32[4,128]{1,0:T(4,128)} %bitcast.22, f32[8,128]{1,0:T(8,128)} %bitcast.20, ...), custom_call_target="tpu_custom_call" | custom-call | tf_op jit(solution)/shard_map/own/pallas_call | solution.py:295
  3.0 11.5 %all-to-all-start = ((f32[64,1,1664]{2,1,0:T(1,128)}), f32[64,1,1664]{2,1,0:T(1,128)S(1)}, u32[]{:S(2)}, u32[]{:S(2)}) async-start(f32[64,1,1664]{2,1,0:T(1,128)} %bitcast.5), calls=%async_computation | async-start | bytes 851968 | tf_op jit(solution)/shard_map/all_to_all | solution.py:332
  14.6 0.1 collective-permute-start
  14.6 1.2 %collective-permute-done.partner_ids = s32[8,128]{1,0:T(8,128)S(1)} collective-permute-done((s32[8,128]{1,0:T(8,128)S(1)}, s32[8,128]{1,0:T(8,128)S(1)}, u32[]{:S(2)}, u32[]{:S(2)}) %collective-permute-start) | collective-permute-done | bytes 4128 | tf_op jit(solution)/shard_map/ppermute | solution.py:337
  15.8 10.9 %all-to-all-done = f32[64,1,1664]{2,1,0:T(1,128)S(1)} async-done(((f32[64,1,1664]{2,1,0:T(1,128)}), f32[64,1,1664]{2,1,0:T(1,128)S(1)}, u32[]{:S(2)}, u32[]{:S(2)}) %all-to-all-start) | async-done | bytes 426016 | tf_op jit(solution)/shard_map/all_to_all | solution.py:332
  26.7 0.2 pick.1.mine
  26.9 0.1 collective-permute-start.1
  27.0 1.2 %collective-permute-done.1.other = f32[32,128]{1,0:T(8,128)S(1)} collective-permute-done((f32[32,128]{1,0:T(8,128)S(1)}, f32[32,128]{1,0:T(8,128)S(1)}, u32[]{:S(2)}, u32[]{:S(2)}) %collective-permute-start.1) | collective-permute-done | bytes 16416 | tf_op jit(solution)/shard_map/ppermute | solution.py:337
  28.1 5.5 %first.1 = (f32[2,512,1024]{2,1,0:T(8,128)S(1)}, f32[24,128]{1,0:T(8,128)S(1)}, f32[2304,128]{1,0:T(8,128)S(1)}, s32[8,128]{1,0:T(8,128)S(4)}) custom-call(s32[4]{0:T(128)S(4)} %get-tuple-element.20.own_ids, s32[2,8,64]{2,1,0:T(8,128)S(4)} %get-tuple-element.21.mask, f32[832,128]{1,0:T(8,128)S(1)} %bitcast.15, f32[32,128]{1,0:T(8,128)S(1)} %pick.1.mine, ...), custom_call_target="tpu_custom_call" | custom-call | tf_op jit(solution)/shard_map/first/pallas_call | solution.py:295
  33.6 25.1 %all_to_all.27 = f32[64,1,4608]{2,1,0:T(1,128)S(1)} all-to-all(f32[64,1,4608]{2,1,0:T(1,128)S(1)} %bitcast.18), channel_id=1, replica_groups={{0,2,4,6,8,10,12,14,16,18,20,22,24,26,28,30,32,34,36,38,40,42,44,46,48,..., dimensions={0} | all-to-all | bytes 2359296 | tf_op jit(solution)/shard_map/all_to_all | solution.py:332
  58.8 0.5 users.1
  59.2 0.1 collective-permute-start.2
  59.3 1.2 %collective-permute-done.2.other = f32[36,128]{1,0:T(8,128)S(1)} collective-permute-done((f32[36,128]{1,0:T(8,128)S(1)}, f32[36,128]{1,0:T(8,128)S(1)}, u32[]{:S(2)}, u32[]{:S(2)}) %collective-permute-start.2) | collective-permute-done | bytes 18464 | tf_op jit(solution)/shard_map/ppermute | solution.py:337
  60.5 2.3 %second.1 = (f32[2,512,1024]{2,1,0:T(8,128)}, f32[24,128]{1,0:T(8,128)S(1)}, f32[12,128]{1,0:T(8,128)S(1)}) custom-call(f32[36,128]{1,0:T(8,128)S(1)} %get-tuple-element.27.mine, f32[36,128]{1,0:T(8,128)S(1)} %collective-permute-done.2.other, f32[2,512,1024]{2,1,0:T(8,128)S(1)} %get-tuple-element.29.base, f32[24,128]{1,0:T(8,128)S(1)} %get-tuple-element.30.psum), custom_call_target="tpu_custom_call" | custom-call | tf_op jit(solution)/shard_map/second/pallas_call | solution.py:295
  62.8 0.2 collective-permute-start.3
  63.1 1.0 %collective-permute-done.3.other = f32[24,128]{1,0:T(8,128)S(1)} collective-permute-done((f32[24,128]{1,0:T(8,128)S(1)}, f32[24,128]{1,0:T(8,128)S(1)}, u32[]{:S(2)}, u32[]{:S(2)}) %collective-permute-start.3) | collective-permute-done | bytes 12320 | tf_op jit(solution)/shard_map/ppermute | solution.py:337
  64.1 0.1 owners.1
  64.2 16.6 %all_to_all.28 = f32[64,1,1536]{2,1,0:T(1,128)S(1)} all-to-all(f32[64,1,1536]{2,1,0:T(1,128)S(1)} %bitcast.17), channel_id=1, replica_groups={{0,2,4,6,8,10,12,14,16,18,20,22,24,26,28,30,32,34,36,38,40,42,44,46,48,..., dimensions={0} | all-to-all | bytes 786432 | tf_op jit(solution)/shard_map/all_to_all | solution.py:332
  80.8 0.6 last.1
Async XLA Ops:
  3.0 23.7 %all-to-all-start = ((f32[64,1,1664]{2,1,0:T(1,128)}), f32[64,1,1664]{2,1,0:T(1,128)S(1)}, u32[]{:S(2)}, u32[]{:S(2)}) async-start(f32[64,1,1664]{2,1,0:T(1,128)} %bitcast.5), calls=%async_computation | async-start | bytes 851968 | tf_op jit(solution)/shard_map/all_to_all | solution.py:332
  14.6 1.2 %collective-permute-start = (s32[8,128]{1,0:T(8,128)S(1)}, s32[8,128]{1,0:T(8,128)S(1)}, u32[]{:S(2)}, u32[]{:S(2)}) collective-permute-start(s32[8,128]{1,0:T(8,128)S(1)} %get-tuple-element.23), channel_id=1, source_target_pairs={{0,1},{1,0},{2,3},{3,2},{4,5},{5,4},{6,7},{7,6},{8,9},{9,8},{10,11... | collective-permute-start | bytes 12296 | tf_op jit(solution)/shard_map/ppermute | solution.py:337
  26.9 1.3 %collective-permute-start.1 = (f32[32,128]{1,0:T(8,128)S(1)}, f32[32,128]{1,0:T(8,128)S(1)}, u32[]{:S(2)}, u32[]{:S(2)}) collective-permute-start(f32[32,128]{1,0:T(8,128)S(1)} %pick.1.mine), channel_id=1, source_target_pairs={{0,1},{1,0},{2,3},{3,2},{4,5},{5,4},{6,7},{7,6},{8,9},{9,8},{10,11... | collective-permute-start | bytes 49160 | tf_op jit(solution)/shard_map/ppermute | solution.py:337
  59.2 1.3 %collective-permute-start.2 = (f32[36,128]{1,0:T(8,128)S(1)}, f32[36,128]{1,0:T(8,128)S(1)}, u32[]{:S(2)}, u32[]{:S(2)}) collective-permute-start(f32[36,128]{1,0:T(8,128)S(1)} %get-tuple-element.28), channel_id=1, source_target_pairs={{0,1},{1,0},{2,3},{3,2},{4,5},{5,4},{6,7},{7,6},{8,9},{9,8},{10,11... | collective-permute-start | bytes 55304 | tf_op jit(solution)/shard_map/ppermute | solution.py:337
  62.8 1.3 %collective-permute-start.3 = (f32[24,128]{1,0:T(8,128)S(1)}, f32[24,128]{1,0:T(8,128)S(1)}, u32[]{:S(2)}, u32[]{:S(2)}) collective-permute-start(f32[24,128]{1,0:T(8,128)S(1)} %get-tuple-element.32.mine), channel_id=1, source_target_pairs={{0,1},{1,0},{2,3},{3,2},{4,5},{5,4},{6,7},{7,6},{8,9},{9,8},{10,11... | collective-permute-start | bytes 36872 | tf_op jit(solution)/shard_map/ppermute | solution.py:337

commit v4 on v3

--- a/solution.py
+++ b/solution.py
@@ -20,8 +20,15 @@
 BIG = 1e30
 AHEAD = 3
 
+PLANE = 16
 CORE_GROUPS = [[j * 2 + c for j in range(CHIPS)] for c in range(2)]
+PLANE_GROUPS = [[(x * PLANE + j) * 2 + c for j in range(PLANE)] for x in range(4) for c in range(2)]
 PARTNERS = [(i, i ^ 1) for i in range(2 * CHIPS)]
+
+
+def along_x(d):
+    return [(i, (i + d * 2 * PLANE) % (2 * CHIPS)) for i in range(2 * CHIPS)]
+
 
 IN_VMEM = pl.BlockSpec(memory_space=pltpu.VMEM)
 IN_SMEM = pl.BlockSpec(memory_space=pltpu.SMEM)
@@ -51,7 +58,8 @@
     return rec[pl.ds(at, SR), :] if slot else rec[pl.ds(at + SR, AR), :]
 
 
-def pick_kernel(partner_ids, rec, out):
+def pick_kernel(partner_ids, rec, _, out):
+
     lane = lax.broadcasted_iota(jnp.int32, (1, L), 1)
     row = partner_ids[0:1, :]
     wanted = [jnp.max(jnp.where(lane == k, row, -1)) for k in range(4)]
@@ -88,64 +96,91 @@
 ZEROS = lambda: (jnp.zeros((8, L), jnp.float32),) * SR
 
 
-def first_tile(t, alive, mask, arow, srow, p_ref, c_ref, out, usum, psum, a_buf, r_buf, q_buf, ready):
+def prepare_kernel(own_ids, mask, p_ref, c_ref, hc, psum, r_buf, col_buf):
+    t = pl.program_id(0)
+    rb = pl.program_id(1)
+
+    @pl.when(rb == 0)
+    def _():
+        col_buf[...] = jnp.zeros_like(col_buf)
+
+    alive = own_ids[t] >= 0
+
+    def step(g, cols):
+        r0 = pl.multiple_of(g * 16, 16)
+        cols = list(cols)
+        ps = [[], []]
+        for cb in range(SR):
+            lanes = pl.ds(cb * L, L)
+            c16 = 0.5 * c_ref[0, pl.ds(r0, 16), lanes].astype(jnp.float32)
+            halves = []
+            for h in range(2):
+                here = (mask[t, cb, rb * 16 + g * 2 + h] > 0) & alive
+                rows = pl.ds(pl.multiple_of(r0 + 8 * h, 8), 8)
+                p = jnp.minimum(p_ref[0, rows, lanes], jnp.where(here, 1.0, 0.0))
+                halves.append(jnp.maximum(c16[8 * h : 8 * h + 8], jnp.where(here, -BIG, BIG)))
+                ps[h].append(p)
+                cols[cb] = cols[cb] + p
+            hc[t, pl.ds(pl.multiple_of(rb * RB + r0, 16), 16), lanes] = jnp.concatenate(halves, axis=0).astype(jnp.bfloat16)
+        for h in range(2):
+            r_buf[pl.ds(pl.multiple_of(r0 + 8 * h, 8), 8), :] = tree(ps[h])
+        return tuple(cols)
+
+    cols = tuple(col_buf[pl.ds(cb * 8, 8), :] for cb in range(SR))
+    cols = lax.fori_loop(0, RB // 16, step, cols)
+    for cb in range(SR):
+        col_buf[pl.ds(cb * 8, 8), :] = cols[cb]
+    psum[pl.ds(t * AR + rb, 1), :] = jnp.sum(r_buf[...].T, axis=0, keepdims=True)
+
+    @pl.when(rb == NRB - 1)
+    def _():
+        rows = [jnp.sum(cols[cb], axis=0, keepdims=True) for cb in range(SR)]
+        psum[pl.ds(pl.multiple_of(8 + t * SR, 8), SR), :] = jnp.concatenate(rows, axis=0)
+
+
+def first_tile(t, arow, srow, p_ref, hc_ref, out, usum, a_buf, r_buf, ready):
     spread_half(arow, a_buf)
     s = slot_rows(srow)
 
-    def step(g, carry):
-        ucols, pcols = list(carry[0]), list(carry[1])
+    def step(g, cols):
+        cols = list(cols)
         us = [[], []]
-        ps = [[], []]
         r0 = pl.multiple_of(g * 16, 16)
+        a = [a_buf[pl.ds(pl.multiple_of(r0 + 8 * h, 8), 8), :] for h in range(2)]
         for cb in range(SR):
             lanes = pl.ds(cb * L, L)
-            c16 = 0.5 * c_ref[t, pl.ds(r0, 16), lanes].astype(jnp.float32)
+            c16 = hc_ref[t, pl.ds(r0, 16), lanes].astype(jnp.float32)
             for h in range(2):
                 rows = pl.ds(pl.multiple_of(r0 + 8 * h, 8), 8)
-                here = (mask[t, cb, g * 2 + h] > 0) & alive
-                p = jnp.minimum(p_ref[t, rows, lanes], jnp.where(here, 1.0, 0.0))
-                hc = jnp.maximum(c16[8 * h : 8 * h + 8], jnp.where(here, -BIG, BIG))
-                u = jnp.minimum(jnp.maximum(((p - hc) - a_buf[rows, :]) - s[cb], 0.0), 1.0)
+                hc = c16[8 * h : 8 * h + 8]
+                u = jnp.minimum(jnp.maximum(((p_ref[t, rows, lanes] - hc) - a[h]) - s[cb], 0.0), 1.0)
                 out[t, rows, lanes] = u - hc
                 us[h].append(u)
-                ps[h].append(p)
-                ucols[cb] = ucols[cb] + u
-                pcols[cb] = pcols[cb] + p
+                cols[cb] = cols[cb] + u
         for h in range(2):
-            rows = pl.ds(pl.multiple_of(r0 + 8 * h, 8), 8)
-            r_buf[rows, :] = tree(us[h])
-            q_buf[rows, :] = tree(ps[h])
-        return tuple(ucols), tuple(pcols)
-
-    ucols, pcols = ZEROS(), ZEROS()
+            r_buf[pl.ds(pl.multiple_of(r0 + 8 * h, 8), 8), :] = tree(us[h])
+        return tuple(cols)
+
+    cols = ZEROS()
     for b in range(NRB):
         ready(t * NRB + b)
-        ucols, pcols = lax.fori_loop(b * 8, (b + 1) * 8, step, (ucols, pcols))
-    write_sums(t, usum, r_buf, ucols)
-    write_sums(t, psum, q_buf, pcols)
-
-
-def first_kernel(own_ids, mask, rec, mine, other, bias, p_hbm, c_hbm, out, usum, msg, ids, p_ref, c_ref, a_buf, r_buf, q_buf, psum, id_buf, p_sems, c_sems, sem):
+        cols = lax.fori_loop(b * 8, (b + 1) * 8, step, cols, unroll=2)
+    write_sums(t, usum, r_buf, cols)
+
+
+def first_kernel(own_ids, rec, mine, other, bias, psum, hc_ref, p_hbm, out, usum, msg, ids, p_ref, a_buf, r_buf, id_buf, p_sems, sem):
     def fetch(n):
         t, b = divmod(n, NRB)
         rows = pl.ds(b * RB, RB)
-        return (
-            pltpu.make_async_copy(p_hbm.at[t, rows, :], p_ref.at[t, rows, :], p_sems.at[n]),
-            pltpu.make_async_copy(c_hbm.at[t, rows, :], c_ref.at[t, rows, :], c_sems.at[n]),
-        )
-
-    def start(n):
-        for copy in fetch(n):
-            copy.start()
+        return pltpu.make_async_copy(p_hbm.at[t, rows, :], p_ref.at[t, rows, :], p_sems.at[n])
 
     def ready(n):
         if n + AHEAD < 2 * NRB:
-            start(n + AHEAD)
-        for copy in fetch(n):
-            copy.wait()
+            fetch(n + AHEAD).start()
+        fetch(n).wait()
 
     for n in range(AHEAD):
-        start(n)
+        fetch(n).start()
     core = lax.axis_index("tiles") & 1
     id_buf[0:4, :] = mine[TS : TS + 4, :].astype(jnp.int32)
     id_buf[4:8, :] = other[TS : TS + 4, :].astype(jnp.int32)
@@ -155,26 +190,31 @@
         a, s = own_ids[t], own_ids[2 + t]
         arow = jnp.where((a & 1) == core, rows_of(rec, a, False), other[AR * t : AR * (t + 1), :])
         srow = jnp.where((s & 1) == core, rows_of(rec, s, True), other[8 + SR * t : 8 + SR * (t + 1), :])
-        first_tile(t, a >= 0, mask, arow, srow, p_ref, c_ref, out, usum, psum, a_buf, r_buf, q_buf, ready)
+        first_tile(t, arow, srow, p_ref, hc_ref, out, usum, a_buf, r_buf, ready)
     data = jnp.concatenate([2.0 * usum[...] - psum[...], bias[...]], axis=0)
-    for j in range(CHIPS):
+    for j in range(PLANE):
         msg[j * MSG : (j + 1) * MSG, :] = data
     keep_ids.wait()
 
 
-def users_kernel(ids, rec, mine, other, acc_a0, acc_a1, acc_s0, acc_s1):
+def users_kernel(ids, rec, out0, out1, out2, out3, acc_a0, acc_a1, acc_s0, acc_s1):
     me = lax.axis_index("tiles")
     chip = me >> 1
     core = me & 1
+    x = chip >> 4
 
     def at(i):
         return pl.multiple_of(jnp.where(i < 0, BLOCKS, i) * 8, 8)
 
     wanted = []
-    for side, out, index in ((0, mine, me), (4, other, me ^ 1)):
-        adv = [(ids[side + k, chip], AR * k) for k in range(2)] + [(index, TS + SR)]
-        slot = [(ids[side + 2 + k, chip], 8 + SR * k) for k in range(2)] + [(index, TS)]
-        wanted.append((out, adv, slot))
+    for d, out in enumerate((out0, out1, out2, out3)):
+        there = (((x + d) & 3) << 4) | (chip & 15)
+        for side in range(2):
+            o = side * MSG
+            index = there * 2 + (core ^ side)
+            adv = [(ids[4 * side + k, there], o + AR * k) for k in range(2)] + [(index, o + TS + SR)]
+            slot = [(ids[4 * side + 2 + k, there], o + 8 + SR * k) for k in range(2)] + [(index, o + TS)]
+            wanted.append((out, adv, slot))
     zero = jnp.zeros((8, L), jnp.float32)
     for _, adv, slot in wanted:
         for i, _ in adv:
@@ -183,24 +223,33 @@
         for i, _ in slot:
             acc_s0[pl.ds(at(i), 8), :] = zero
             acc_s1[pl.ds(at(i), 8), :] = zero
-    for j in range(CHIPS):
+    for j in range(PLANE):
+        source = (x << 4) | j
         for k, acc in ((0, acc_a0), (1, acc_a1)):
-            rows = pl.ds(at(ids[k, j]), AR)
+            rows = pl.ds(at(ids[k, source]), AR)
             acc[rows, :] = acc[rows, :] + rec[j * MSG + AR * k : j * MSG + AR * (k + 1), :]
         for k, acc in ((0, acc_s0), (1, acc_s1)):
-            rows = pl.ds(at(ids[2 + k, j]), SR)
+            rows = pl.ds(at(ids[2 + k, source]), SR)
             acc[rows, :] = acc[rows, :] + rec[j * MSG + 8 + SR * k : j * MSG + 8 + SR * (k + 1), :]
+
+    def bias(i, o, n):
+        b = jnp.maximum(i, 0)
+        here = ((b & 1) == core) & ((b >> 5) == x)
+        return rec[pl.ds(((b >> 1) & 15) * MSG + o, n), :] * jnp.where(here, 1.0, 0.0)
+
     for out, adv, slot in wanted:
         for i, o in adv:
-            b = jnp.maximum(i, 0)
-            bias = rec[pl.ds((b >> 1) * MSG + TS + SR, AR), :] * jnp.where((b & 1) == core, 1.0, 0.0)
             rows = pl.ds(at(i), AR)
-            out[o : o + AR, :] = (acc_a0[rows, :] + acc_a1[rows, :]) + bias
+            out[o : o + AR, :] = (acc_a0[rows, :] + acc_a1[rows, :]) + bias(i, TS + SR, AR)
         for i, o in slot:
-            b = jnp.maximum(i, 0)
-            bias = rec[pl.ds((b >> 1) * MSG + TS, SR), :] * jnp.where((b & 1) == core, 1.0, 0.0)
             rows = pl.ds(at(i), SR)
-            out[o : o + SR, :] = (acc_s0[rows, :] + acc_s1[rows, :]) + bias
+            out[o : o + SR, :] = (acc_s0[rows, :] + acc_s1[rows, :]) + bias(i, TS, SR)
+
+
+def join_kernel(a, b, c, d, mine, other):
+    total = (a[...] + b[...]) + (c[...] + d[...])
+    mine[...] = total[0:MSG]
+    other[...] = total[MSG:]
 
 
 def second_tile(t, arow, srow, base, out, usum, a_buf, r_buf, done):
@@ -327,10 +376,10 @@
     return (vmem(*shape), IN_VMEM)
 
 
-def exchange(x, rows):
-    x = x.reshape(CHIPS, rows * L)
-    x = lax.all_to_all(x, "tiles", 0, 0, axis_index_groups=CORE_GROUPS, tiled=True)
-    return vmem_arg(x.reshape(CHIPS * rows, L))
+def exchange(x, groups, rows):
+    n = len(groups[0])
+    x = lax.all_to_all(x.reshape(n, rows * L), "tiles", 0, 0, axis_index_groups=groups, tiled=True)
+    return vmem_arg(x.reshape(n * rows, L))
 
 
 def swap(x):
@@ -349,29 +398,33 @@
         + [(pltpu.VMEM((8, L), jnp.int32), IN_VMEM), smem_out(4), smem_out(2, 8, 64)],
         [pltpu.SemaphoreType.DMA(())],
     )
-    table = exchange(message, OWN)
-    (picked,) = call(pick_kernel, "pick", [vmem_arg(swap(row_ids)), table], [vmem_out(SEL, L)])
-
+    table = exchange(message, CORE_GROUPS, OWN)
+    block = pl.BlockSpec((1, RB, 1024), lambda t, rb: (t, rb, 0))
+    hc, psum = pl.pallas_call(
+        prepare_kernel,
+        grid=(2, NRB),
+        in_specs=[IN_SMEM, IN_SMEM, block, block],
+        out_specs=[IN_VMEM, IN_VMEM],
+        out_shape=[pltpu.VMEM(tile, jnp.bfloat16), vmem(TS, L)],
+        scratch_shapes=[vmem(RB, L), vmem(64, L)],
+        compiler_params=pltpu.CompilerParams(vmem_limit_bytes=4 << 20),
+        name="prepare",
+    )(in_smem(own_ids), in_smem(here), in_hbm(primal_start), in_hbm(cost))
+    (picked,) = call(pick_kernel, "pick", [vmem_arg(swap(row_ids)), table, vmem_arg(psum)], [vmem_out(SEL, L)])
     base, usum, message, ids = call(
         first_kernel,
         "first",
-        [smem_arg(own_ids), smem_arg(here), table, vmem_arg(picked), vmem_arg(swap(picked)), vmem_arg(bias)] + [hbm_arg(primal_start), hbm_arg(cost)],
-        [vmem_out(*tile), vmem_out(TS, L), vmem_out(CHIPS * MSG, L), smem_out(8, L)],
-        [vmem(*tile), pltpu.VMEM(tile, jnp.bfloat16)]
-        + [vmem(512, L)] * 3
-        + [vmem(TS, L), pltpu.VMEM((8, L), jnp.int32)]
-        + [pltpu.SemaphoreType.DMA((2 * NRB,))] * 2
-        + [pltpu.SemaphoreType.DMA(())],
+        [smem_arg(own_ids), table, vmem_arg(picked), vmem_arg(swap(picked)), vmem_arg(bias), vmem_arg(psum), vmem_arg(hc)]
+        + [hbm_arg(primal_start)],
+        [vmem_out(*tile), vmem_out(TS, L), vmem_out(PLANE * MSG, L), smem_out(8, L)],
+        [vmem(*tile), vmem(512, L), vmem(512, L), pltpu.VMEM((8, L), jnp.int32)]
+        + [pltpu.SemaphoreType.DMA((2 * NRB,)), pltpu.SemaphoreType.DMA(())],
         8,
     )
-    part = exchange(message, MSG)
-    mine, other = call(
-        users_kernel,
-        "users",
-        [smem_arg(ids), part],
-        [vmem_out(MSG, L), vmem_out(MSG, L)],
-        [vmem((BLOCKS + 1) * 8, L)] * 4,
-    )
+    part = exchange(message, PLANE_GROUPS, MSG)
+    parts = call(users_kernel, "users", [smem_arg(ids), part], [vmem_out(2 * MSG, L)] * 4, [vmem((BLOCKS + 1) * 8, L)] * 4)
+    parts = [parts[0]] + [lax.ppermute(parts[d], "tiles", along_x(d)) for d in range(1, 4)]
+    mine, other = call(join_kernel, "join", [vmem_arg(v) for v in parts], [vmem_out(MSG, L)] * 2)
 
     primal, sums, own = call(
         second_kernel,
@@ -387,7 +440,7 @@
     adv_out, slot_out = call(
         last_kernel,
         "last",
-        [exchange(message, OUT), vmem_arg(own), vmem_arg(bounds)],
+        [exchange(message, CORE_GROUPS, OUT), vmem_arg(own), vmem_arg(bounds)],
         [(f32(AR, L), IN_VMEM), (f32(SR, L), IN_VMEM)],
     )
     return primal, adv_out.reshape(1, 512), slot_out.reshape(1, 1024)

time: 81.7 us -> 76.5 us (0.936)
  blocking collectives: 41.7 us -> 30.3 us
  starting transfers between devices: 12 us -> 17.7 us
  Pallas kernels: 11.6 us -> 17.2 us
  waiting for transfers between devices: 15.4 us -> 10.1 us
    all_to_all x2, blocking collectives: 41.7 us -> 30.3 us  [exchange(): lax.all_to_all(x.reshape(n, rows * L), 'tiles', 0, 0, axis_index_groups=g...]
    pallas_call x0 -> x1, Pallas kernels: none -> 7.84 us  [body(): pl.pallas_call(prepare_kernel, grid=(2, NRB), in_specs=[IN_SMEM, IN_SMEM,...]
    all_to_all x1, waiting for transfers between devices: 10.9 us -> 4.16 us  [exchange(): lax.all_to_all(x.reshape(n, rows * L), 'tiles', 0, 0, axis_index_groups=g...]
    ppermute x0 -> x3, starting transfers between devices: none -> 5.64 us  [body(): lax.ppermute(parts[d], 'tiles', along_x(d))]
    ppermute x0 -> x3, waiting for transfers between devices: none -> 2.6 us  [body(): lax.ppermute(parts[d], 'tiles', along_x(d))]
    pallas_call x7 -> x8, Pallas kernels: 11.6 us -> 9.34 us  [call(): pl.pallas_call(kernel, in_specs=[s for _, s in ins], out_specs=[s for _,...]
    ppermute x4, waiting for transfers between devices: 4.51 us -> 3.36 us  [swap(): return lax.ppermute(x, 'tiles', PARTNERS)]
  transfers between devices with their start and end apart: 5 -> 8, of which waited for: 5 -> 6; matrix products, arithmetic and copies ran while one was open for 0% -> 0% of each run, Pallas kernels for 0% -> 10%
where the time goes in v4:
time: 76.5 us; the launch traced here: 76 us
  blocking collectives  30.3 us (40%)
  starting transfers between devices  17.7 us (23%)
  Pallas kernels  17.2 us (22%)
  waiting for transfers between devices  10.1 us (13%)
    all_to_all x2, blocking collectives, exchange(): lax.all_to_all(x.reshape(n, rows * L), 'tiles', 0, 0, axis_index_groups=g...  30.3 us
    all_to_all x1, starting transfers between devices, exchange(): lax.all_to_all(x.reshape(n, rows * L), 'tiles', 0, 0, axis_index_groups=g...  11.5 us
    pallas_call x8, Pallas kernels, call(): pl.pallas_call(kernel, in_specs=[s for _, s in ins], out_specs=[s for _,...  9.34 us
    pallas_call x1, Pallas kernels, body(): pl.pallas_call(prepare_kernel, grid=(2, NRB), in_specs=[IN_SMEM, IN_SMEM,...  7.84 us
    ppermute x3, starting transfers between devices, body(): lax.ppermute(parts[d], 'tiles', along_x(d))  5.64 us
    all_to_all x1, waiting for transfers between devices, exchange(): lax.all_to_all(x.reshape(n, rows * L), 'tiles', 0, 0, axis_index_groups=g...  4.16 us
    ppermute x4, waiting for transfers between devices, swap(): return lax.ppermute(x, 'tiles', PARTNERS)  3.36 us
    ppermute x3, waiting for transfers between devices, body(): lax.ppermute(parts[d], 'tiles', along_x(d))  2.6 us
  transfers between devices with their start and end apart: 8, of which 6 were waited for; matrix products, arithmetic and copies ran while one was open for 0% of the time, Pallas kernels for 10%

profile of v4, /device:TPU:0, one launch (start us, length us, event | category | flops | bytes accessed | tf_op | source)
XLA Modules:
  0.0 76.0 jit_solution(9004247554035827332)
XLA Ops:
  0.6 2.4 %own.1 = (f32[832,128]{1,0:T(8,128)}, f32[12,128]{1,0:T(8,128)S(1)}, f32[12,128]{1,0:T(8,128)S(1)}, s32[8,128]{1,0:T(8,128)S(1)}, s32[4]{0:T(128)S(4)}, /*index=5*/s32[2,8,64]{2,1,0:T(8,128)S(4)}) custom-call(s32[2]{0:T(128)} %adv_id.1, s32[2]{0:T(128)} %slot_id.1, f32[4,128]{1,0:T(4,128)} %bitcast.22, f32[8,128]{1,0:T(8,128)} %bitcast.20, ...), custom_call_target="tpu_custom_call" | custom-call | tf_op jit(solution)/shard_map/own/pallas_call | solution.py:344
  3.0 11.5 %all-to-all-start = ((f32[64,1,1664]{2,1,0:T(1,128)}), f32[64,1,1664]{2,1,0:T(1,128)S(1)}, u32[]{:S(2)}, u32[]{:S(2)}) async-start(f32[64,1,1664]{2,1,0:T(1,128)} %bitcast.5), calls=%async_computation | async-start | bytes 851968 | tf_op jit(solution)/shard_map/all_to_all | solution.py:381
  14.6 0.1 collective-permute-start
  14.6 7.8 %prepare.1 = (bf16[2,512,1024]{2,1,0:T(8,128)(2,1)S(1)}, f32[24,128]{1,0:T(8,128)S(1)}) custom-call(s32[4]{0:T(128)S(4)} %get-tuple-element.26.own_ids, s32[2,8,64]{2,1,0:T(8,128)S(4)} %get-tuple-element.29.mask, f32[2,512,1024]{2,1,0:T(8,128)} %p_hbm.1, bf16[2,512,1024]{2,1,0:T(8,128)(2,1)} %c_ref.1), custom_call_target="tpu_custom_call" | custom-call | tf_op jit(solution)/shard_map/prepare/pallas_call | solution.py:403
  22.5 0.0 collective-permute-done.partner_ids
  22.5 4.2 %all-to-all-done = f32[64,1,1664]{2,1,0:T(1,128)S(1)} async-done(((f32[64,1,1664]{2,1,0:T(1,128)}), f32[64,1,1664]{2,1,0:T(1,128)S(1)}, u32[]{:S(2)}, u32[]{:S(2)}) %all-to-all-start) | async-done | bytes 426016 | tf_op jit(solution)/shard_map/all_to_all | solution.py:381
  26.7 0.2 pick.1.mine
  26.9 0.1 collective-permute-start.1
  27.0 1.2 %collective-permute-done.1.other = f32[32,128]{1,0:T(8,128)S(1)} collective-permute-done((f32[32,128]{1,0:T(8,128)S(1)}, f32[32,128]{1,0:T(8,128)S(1)}, u32[]{:S(2)}, u32[]{:S(2)}) %collective-permute-start.1) | collective-permute-done | bytes 16416 | tf_op jit(solution)/shard_map/ppermute | solution.py:386
  28.1 3.3 %first.1 = (f32[2,512,1024]{2,1,0:T(8,128)S(1)}, f32[24,128]{1,0:T(8,128)S(1)}, f32[576,128]{1,0:T(8,128)S(1)}, s32[8,128]{1,0:T(8,128)S(4)}) custom-call(s32[4]{0:T(128)S(4)} %get-tuple-element.26.own_ids, f32[832,128]{1,0:T(8,128)S(1)} %bitcast.14, f32[32,128]{1,0:T(8,128)S(1)} %pick.1.mine, f32[32,128]{1,0:T(8,128)S(1)} %collective-permute-done.1.other, ...), custom_call_target="tpu_custom_call" | custom-call | tf_op jit(solution)/shard_map/first/pallas_call | solution.py:344
  31.5 12.4 %all_to_all.27 = f32[16,1,4608]{2,1,0:T(1,128)S(1)} all-to-all(f32[16,1,4608]{2,1,0:T(1,128)S(1)} %bitcast.18), channel_id=1, replica_groups={{0,2,4,6,8,10,12,14,16,18,20,22,24,26,28,30},{1,3,5,7,9,11,13,15,17,19,..., dimensions={0} | all-to-all | bytes 589824 | tf_op jit(solution)/shard_map/all_to_all | solution.py:381
  43.9 0.4 users.1
  44.3 1.4 %collective-permute-start.2 = (f32[72,128]{1,0:T(8,128)S(1)}, f32[72,128]{1,0:T(8,128)S(1)}, u32[]{:S(2)}, u32[]{:S(2)}) collective-permute-start(f32[72,128]{1,0:T(8,128)S(1)} %get-tuple-element.36), channel_id=1, source_target_pairs={{0,32},{1,33},{2,34},{3,35},{4,36},{5,37},{6,38},{7,39},{8,40},{9,... | collective-permute-start | bytes 110600 | tf_op jit(solution)/shard_map/ppermute | solution.py:426
  45.7 2.9 %collective-permute-start.3 = (f32[72,128]{1,0:T(8,128)S(1)}, f32[72,128]{1,0:T(8,128)S(1)}, u32[]{:S(2)}, u32[]{:S(2)}) collective-permute-start(f32[72,128]{1,0:T(8,128)S(1)} %get-tuple-element.37), channel_id=1, source_target_pairs={{0,64},{1,65},{2,66},{3,67},{4,68},{5,69},{6,70},{7,71},{8,72},{9,... | collective-permute-start | bytes 110600 | tf_op jit(solution)/shard_map/ppermute | solution.py:426
  48.6 1.4 %collective-permute-start.4 = (f32[72,128]{1,0:T(8,128)S(1)}, f32[72,128]{1,0:T(8,128)S(1)}, u32[]{:S(2)}, u32[]{:S(2)}) collective-permute-start(f32[72,128]{1,0:T(8,128)S(1)} %get-tuple-element.38), channel_id=1, source_target_pairs={{0,96},{1,97},{2,98},{3,99},{4,100},{5,101},{6,102},{7,103},{8,104... | collective-permute-start | bytes 110600 | tf_op jit(solution)/shard_map/ppermute | solution.py:426
  49.9 0.0 collective-permute-done.2.b
  49.9 1.2 %collective-permute-done.3.c = f32[72,128]{1,0:T(8,128)S(1)} collective-permute-done((f32[72,128]{1,0:T(8,128)S(1)}, f32[72,128]{1,0:T(8,128)S(1)}, u32[]{:S(2)}, u32[]{:S(2)}) %collective-permute-start.3) | collective-permute-done | bytes 36896 | tf_op jit(solution)/shard_map/ppermute | solution.py:426
  51.1 1.4 %collective-permute-done.4.d = f32[72,128]{1,0:T(8,128)S(1)} collective-permute-done((f32[72,128]{1,0:T(8,128)S(1)}, f32[72,128]{1,0:T(8,128)S(1)}, u32[]{:S(2)}, u32[]{:S(2)}) %collective-permute-start.4) | collective-permute-done | bytes 36896 | tf_op jit(solution)/shard_map/ppermute | solution.py:426
  52.5 0.1 collective-permute-start.5
  52.6 1.2 %collective-permute-done.5.other = f32[36,128]{1,0:T(8,128)S(1)} collective-permute-done((f32[36,128]{1,0:T(8,128)S(1)}, f32[36,128]{1,0:T(8,128)S(1)}, u32[]{:S(2)}, u32[]{:S(2)}) %collective-permute-start.5) | collective-permute-done | bytes 18464 | tf_op jit(solution)/shard_map/ppermute | solution.py:386
  53.8 2.3 %second.1 = (f32[2,512,1024]{2,1,0:T(8,128)}, f32[24,128]{1,0:T(8,128)S(1)}, f32[12,128]{1,0:T(8,128)S(1)}) custom-call(f32[36,128]{1,0:T(8,128)S(1)} %get-tuple-element.39.mine, f32[36,128]{1,0:T(8,128)S(1)} %collective-permute-done.5.other, f32[2,512,1024]{2,1,0:T(8,128)S(1)} %get-tuple-element.41.base, f32[24,128]{1,0:T(8,128)S(1)} %get-tuple-element.42.psum), custom_call_target="tpu_custom_call" | custom-call | tf_op jit(solution)/shard_map/second/pallas_call | solution.py:344
  56.1 0.2 collective-permute-start.6
  56.4 1.0 %collective-permute-done.6.other = f32[24,128]{1,0:T(8,128)S(1)} collective-permute-done((f32[24,128]{1,0:T(8,128)S(1)}, f32[24,128]{1,0:T(8,128)S(1)}, u32[]{:S(2)}, u32[]{:S(2)}) %collective-permute-start.6) | collective-permute-done | bytes 12320 | tf_op jit(solution)/shard_map/ppermute | solution.py:386
  57.4 0.1 owners.1
  57.5 17.9 %all_to_all.28 = f32[64,1,1536]{2,1,0:T(1,128)S(1)} all-to-all(f32[64,1,1536]{2,1,0:T(1,128)S(1)} %bitcast.16), channel_id=1, replica_groups={{0,2,4,6,8,10,12,14,16,18,20,22,24,26,28,30,32,34,36,38,40,42,44,46,48,..., dimensions={0} | all-to-all | bytes 786432 | tf_op jit(solution)/shard_map/all_to_all | solution.py:381
  75.3 0.6 last.1
  (1 shorter events, 0.0 us)
Async XLA Ops:
  3.0 23.7 %all-to-all-start = ((f32[64,1,1664]{2,1,0:T(1,128)}), f32[64,1,1664]{2,1,0:T(1,128)S(1)}, u32[]{:S(2)}, u32[]{:S(2)}) async-start(f32[64,1,1664]{2,1,0:T(1,128)} %bitcast.5), calls=%async_computation | async-start | bytes 851968 | tf_op jit(solution)/shard_map/all_to_all | solution.py:381
  14.6 7.9 %collective-permute-start = (s32[8,128]{1,0:T(8,128)S(1)}, s32[8,128]{1,0:T(8,128)S(1)}, u32[]{:S(2)}, u32[]{:S(2)}) collective-permute-start(s32[8,128]{1,0:T(8,128)S(1)} %get-tuple-element.28), channel_id=1, source_target_pairs={{0,1},{1,0},{2,3},{3,2},{4,5},{5,4},{6,7},{7,6},{8,9},{9,8},{10,11... | collective-permute-start | bytes 12296 | tf_op jit(solution)/shard_map/ppermute | solution.py:386
  26.9 1.3 %collective-permute-start.1 = (f32[32,128]{1,0:T(8,128)S(1)}, f32[32,128]{1,0:T(8,128)S(1)}, u32[]{:S(2)}, u32[]{:S(2)}) collective-permute-start(f32[32,128]{1,0:T(8,128)S(1)} %pick.1.mine), channel_id=1, source_target_pairs={{0,1},{1,0},{2,3},{3,2},{4,5},{5,4},{6,7},{7,6},{8,9},{9,8},{10,11... | collective-permute-start | bytes 49160 | tf_op jit(solution)/shard_map/ppermute | solution.py:386
  44.3 5.6 %collective-permute-start.2 = (f32[72,128]{1,0:T(8,128)S(1)}, f32[72,128]{1,0:T(8,128)S(1)}, u32[]{:S(2)}, u32[]{:S(2)}) collective-permute-start(f32[72,128]{1,0:T(8,128)S(1)} %get-tuple-element.36), channel_id=1, source_target_pairs={{0,32},{1,33},{2,34},{3,35},{4,36},{5,37},{6,38},{7,39},{8,40},{9,... | collective-permute-start | bytes 110600 | tf_op jit(solution)/shard_map/ppermute | solution.py:426
  45.7 5.5 %collective-permute-start.3 = (f32[72,128]{1,0:T(8,128)S(1)}, f32[72,128]{1,0:T(8,128)S(1)}, u32[]{:S(2)}, u32[]{:S(2)}) collective-permute-start(f32[72,128]{1,0:T(8,128)S(1)} %get-tuple-element.37), channel_id=1, source_target_pairs={{0,64},{1,65},{2,66},{3,67},{4,68},{5,69},{6,70},{7,71},{8,72},{9,... | collective-permute-start | bytes 110600 | tf_op jit(solution)/shard_map/ppermute | solution.py:426
  48.6 4.0 %collective-permute-start.4 = (f32[72,128]{1,0:T(8,128)S(1)}, f32[72,128]{1,0:T(8,128)S(1)}, u32[]{:S(2)}, u32[]{:S(2)}) collective-permute-start(f32[72,128]{1,0:T(8,128)S(1)} %get-tuple-element.38), channel_id=1, source_target_pairs={{0,96},{1,97},{2,98},{3,99},{4,100},{5,101},{6,102},{7,103},{8,104... | collective-permute-start | bytes 110600 | tf_op jit(solution)/shard_map/ppermute | solution.py:426
  52.5 1.3 %collective-permute-start.5 = (f32[36,128]{1,0:T(8,128)S(1)}, f32[36,128]{1,0:T(8,128)S(1)}, u32[]{:S(2)}, u32[]{:S(2)}) collective-permute-start(f32[36,128]{1,0:T(8,128)S(1)} %get-tuple-element.40), channel_id=1, source_target_pairs={{0,1},{1,0},{2,3},{3,2},{4,5},{5,4},{6,7},{7,6},{8,9},{9,8},{10,11... | collective-permute-start | bytes 55304 | tf_op jit(solution)/shard_map/ppermute | solution.py:386
  56.1 1.3 %collective-permute-start.6 = (f32[24,128]{1,0:T(8,128)S(1)}, f32[24,128]{1,0:T(8,128)S(1)}, u32[]{:S(2)}, u32[]{:S(2)}) collective-permute-start(f32[24,128]{1,0:T(8,128)S(1)} %get-tuple-element.44.mine), channel_id=1, source_target_pairs={{0,1},{1,0},{2,3},{3,2},{4,5},{5,4},{6,7},{7,6},{8,9},{9,8},{10,11... | collective-permute-start | bytes 36872 | tf_op jit(solution)/shard_map/ppermute | solution.py:386

commit v5 on v4

--- a/solution.py
+++ b/solution.py
@@ -18,7 +18,6 @@
 RB = 128
 NRB = 4
 BIG = 1e30
-AHEAD = 3
 
 PLANE = 16
 CORE_GROUPS = [[j * 2 + c for j in range(CHIPS)] for c in range(2)]
@@ -104,7 +103,7 @@
     def _():
         col_buf[...] = jnp.zeros_like(col_buf)
 
-    alive = own_ids[t] >= 0
+    alive = jnp.where(own_ids[t] >= 0, 1, 0)
 
     def step(g, cols):
         r0 = pl.multiple_of(g * 16, 16)
@@ -115,10 +114,10 @@
             c16 = 0.5 * c_ref[0, pl.ds(r0, 16), lanes].astype(jnp.float32)
             halves = []
             for h in range(2):
-                here = (mask[t, cb, rb * 16 + g * 2 + h] > 0) & alive
+                here = jnp.full((8, L), mask[t, cb, rb * 16 + g * 2 + h] * alive, jnp.int32) > 0
                 rows = pl.ds(pl.multiple_of(r0 + 8 * h, 8), 8)
-                p = jnp.minimum(p_ref[0, rows, lanes], jnp.where(here, 1.0, 0.0))
-                halves.append(jnp.maximum(c16[8 * h : 8 * h + 8], jnp.where(here, -BIG, BIG)))
+                p = jnp.where(here, p_ref[0, rows, lanes], 0.0)
+                halves.append(jnp.where(here, c16[8 * h : 8 * h + 8], BIG))
                 ps[h].append(p)
                 cols[cb] = cols[cb] + p
             hc[t, pl.ds(pl.multiple_of(rb * RB + r0, 16), 16), lanes] = jnp.concatenate(halves, axis=0).astype(jnp.bfloat16)
@@ -136,6 +135,12 @@
     def _():
         rows = [jnp.sum(cols[cb], axis=0, keepdims=True) for cb in range(SR)]
         psum[pl.ds(pl.multiple_of(8 + t * SR, 8), SR), :] = jnp.concatenate(rows, axis=0)
+
+
+def load_kernel(p_hbm, _, out, sem):
+    copy = pltpu.make_async_copy(p_hbm.at[0], out, sem)
+    copy.start()
+    copy.wait()
 
 
 def first_tile(t, arow, srow, p_ref, hc_ref, out, usum, a_buf, r_buf, ready):
@@ -153,7 +158,7 @@
             for h in range(2):
                 rows = pl.ds(pl.multiple_of(r0 + 8 * h, 8), 8)
                 hc = c16[8 * h : 8 * h + 8]
-                u = jnp.minimum(jnp.maximum(((p_ref[t, rows, lanes] - hc) - a[h]) - s[cb], 0.0), 1.0)
+                u = jnp.minimum(jnp.maximum(((p_ref[rows, lanes] - hc) - a[h]) - s[cb], 0.0), 1.0)
                 out[t, rows, lanes] = u - hc
                 us[h].append(u)
                 cols[cb] = cols[cb] + u
@@ -163,24 +168,18 @@
 
     cols = ZEROS()
     for b in range(NRB):
-        ready(t * NRB + b)
+        ready(b)
         cols = lax.fori_loop(b * 8, (b + 1) * 8, step, cols, unroll=2)
     write_sums(t, usum, r_buf, cols)
 
 
-def first_kernel(own_ids, rec, mine, other, bias, psum, hc_ref, p_hbm, out, usum, msg, ids, p_ref, a_buf, r_buf, id_buf, p_sems, sem):
-    def fetch(n):
-        t, b = divmod(n, NRB)
+def first_kernel(own_ids, rec, mine, other, bias, psum, hc_ref, p0_ref, p_hbm, out, usum, msg, ids, p1_ref, a_buf, r_buf, id_buf, p_sems, sem):
+    def fetch(b):
         rows = pl.ds(b * RB, RB)
-        return pltpu.make_async_copy(p_hbm.at[t, rows, :], p_ref.at[t, rows, :], p_sems.at[n])
-
-    def ready(n):
-        if n + AHEAD < 2 * NRB:
-            fetch(n + AHEAD).start()
-        fetch(n).wait()
-
-    for n in range(AHEAD):
-        fetch(n).start()
+        return pltpu.make_async_copy(p_hbm.at[1, rows, :], p1_ref.at[rows, :], p_sems.at[b])
+
+    for b in range(NRB):
+        fetch(b).start()
     core = lax.axis_index("tiles") & 1
     id_buf[0:4, :] = mine[TS : TS + 4, :].astype(jnp.int32)
     id_buf[4:8, :] = other[TS : TS + 4, :].astype(jnp.int32)
@@ -190,66 +189,80 @@
         a, s = own_ids[t], own_ids[2 + t]
         arow = jnp.where((a & 1) == core, rows_of(rec, a, False), other[AR * t : AR * (t + 1), :])
         srow = jnp.where((s & 1) == core, rows_of(rec, s, True), other[8 + SR * t : 8 + SR * (t + 1), :])
-        first_tile(t, arow, srow, p_ref, hc_ref, out, usum, a_buf, r_buf, ready)
-    data = jnp.concatenate([2.0 * usum[...] - psum[...], bias[...]], axis=0)
-    for j in range(PLANE):
-        msg[j * MSG : (j + 1) * MSG, :] = data
+        first_tile(
+            t,
+            arow,
+            srow,
+            (p0_ref, p1_ref)[t],
+            hc_ref,
+            out,
+            usum,
+            a_buf,
+            r_buf,
+            (lambda b: None, lambda b: fetch(b).wait())[t],
+        )
+    msg[0:TS, :] = 2.0 * usum[...] - psum[...]
+    msg[TS:MSG, :] = bias[...]
     keep_ids.wait()
 
 
-def users_kernel(ids, rec, out0, out1, out2, out3, acc_a0, acc_a1, acc_s0, acc_s1):
+def pair_kernel(a, b, out):
+    out[0:MSG, :] = a[...]
+    out[MSG:, :] = b[...]
+
+
+def users_kernel(ids, rec0, rec1, rec2, rec3, out, rec, acc_a0, acc_a1, acc_s0, acc_s1):
     me = lax.axis_index("tiles")
     chip = me >> 1
     core = me & 1
     x = chip >> 4
+    line = chip & 15
+    both = 2 * MSG
 
     def at(i):
         return pl.multiple_of(jnp.where(i < 0, BLOCKS, i) * 8, 8)
 
     wanted = []
-    for d, out in enumerate((out0, out1, out2, out3)):
-        there = (((x + d) & 3) << 4) | (chip & 15)
-        for side in range(2):
-            o = side * MSG
-            index = there * 2 + (core ^ side)
-            adv = [(ids[4 * side + k, there], o + AR * k) for k in range(2)] + [(index, o + TS + SR)]
-            slot = [(ids[4 * side + 2 + k, there], o + 8 + SR * k) for k in range(2)] + [(index, o + TS)]
-            wanted.append((out, adv, slot))
+    for j in range(PLANE):
+        there = (x << 4) | j
+        o = j * MSG
+        index = there * 2 + core
+        adv = [(ids[k, there], o + AR * k) for k in range(2)] + [(index, o + TS + SR)]
+        slot = [(ids[2 + k, there], o + 8 + SR * k) for k in range(2)] + [(index, o + TS)]
+        wanted.append((adv, slot))
     zero = jnp.zeros((8, L), jnp.float32)
-    for _, adv, slot in wanted:
+    for adv, slot in wanted:
         for i, _ in adv:
             acc_a0[pl.ds(at(i), 8), :] = zero
             acc_a1[pl.ds(at(i), 8), :] = zero
         for i, _ in slot:
             acc_s0[pl.ds(at(i), 8), :] = zero
             acc_s1[pl.ds(at(i), 8), :] = zero
-    for j in range(PLANE):
-        source = (x << 4) | j
-        for k, acc in ((0, acc_a0), (1, acc_a1)):
-            rows = pl.ds(at(ids[k, source]), AR)
-            acc[rows, :] = acc[rows, :] + rec[j * MSG + AR * k : j * MSG + AR * (k + 1), :]
-        for k, acc in ((0, acc_s0), (1, acc_s1)):
-            rows = pl.ds(at(ids[2 + k, source]), SR)
-            acc[rows, :] = acc[rows, :] + rec[j * MSG + 8 + SR * k : j * MSG + 8 + SR * (k + 1), :]
+    for d, part in enumerate((rec0, rec1, rec2, rec3)):
+        rec[d * both : (d + 1) * both, :] = part[...]
+        source = (((x - d) & 3) << 4) | line
+        for side in range(2):
+            o = side * MSG
+            for k, acc in ((0, acc_a0), (1, acc_a1)):
+                rows = pl.ds(at(ids[4 * side + k, source]), AR)
+                acc[rows, :] = acc[rows, :] + part[o + AR * k : o + AR * (k + 1), :]
+            for k, acc in ((0, acc_s0), (1, acc_s1)):
+                rows = pl.ds(at(ids[4 * side + 2 + k, source]), SR)
+                acc[rows, :] = acc[rows, :] + part[o + 8 + SR * k : o + 8 + SR * (k + 1), :]
 
     def bias(i, o, n):
         b = jnp.maximum(i, 0)
-        here = ((b & 1) == core) & ((b >> 5) == x)
-        return rec[pl.ds(((b >> 1) & 15) * MSG + o, n), :] * jnp.where(here, 1.0, 0.0)
-
-    for out, adv, slot in wanted:
+        here = ((b >> 1) & 15) == line
+        row = ((x - (b >> 5)) & 3) * both + ((b & 1) ^ core) * MSG + o
+        return rec[pl.ds(row, n), :] * jnp.where(here, 1.0, 0.0)
+
+    for adv, slot in wanted:
         for i, o in adv:
             rows = pl.ds(at(i), AR)
             out[o : o + AR, :] = (acc_a0[rows, :] + acc_a1[rows, :]) + bias(i, TS + SR, AR)
         for i, o in slot:
             rows = pl.ds(at(i), SR)
             out[o : o + SR, :] = (acc_s0[rows, :] + acc_s1[rows, :]) + bias(i, TS, SR)
-
-
-def join_kernel(a, b, c, d, mine, other):
-    total = (a[...] + b[...]) + (c[...] + d[...])
-    mine[...] = total[0:MSG]
-    other[...] = total[MSG:]
 
 
 def second_tile(t, arow, srow, base, out, usum, a_buf, r_buf, done):
@@ -277,12 +290,12 @@
     write_sums(t, usum, r_buf, cols)
 
 
-def second_kernel(mine, other, base, psum, primal, sums, own, out, usum, a_buf, r_buf, sems):
+def second_kernel(rec, base, psum, primal, sums, own, out, usum, a_buf, r_buf, sems):
     def keep(t, b):
         rows = pl.ds(b * RB, RB)
         return pltpu.make_async_copy(out.at[t, rows, :], primal.at[t, rows, :], sems.at[t * NRB + b])
 
-    total = mine[...] + other[...]
+    total = tree([rec[j * MSG : (j + 1) * MSG, :] for j in range(PLANE)])
     adv = jnp.maximum(total[0:8] * (1.0 / 1024), 0.0)
     slot = jnp.maximum(total[8:32] * (1.0 / 512), 0.0)
     own[0:SR, :] = slot[16:24]
@@ -411,25 +424,36 @@
         name="prepare",
     )(in_smem(own_ids), in_smem(here), in_hbm(primal_start), in_hbm(cost))
     (picked,) = call(pick_kernel, "pick", [vmem_arg(swap(row_ids)), table, vmem_arg(psum)], [vmem_out(SEL, L)])
+    (start,) = call(
+        load_kernel,
+        "load",
+        [hbm_arg(primal_start), vmem_arg(picked)],
+        [vmem_out(*tile[1:])],
+        [pltpu.SemaphoreType.DMA(())],
+    )
     base, usum, message, ids = call(
         first_kernel,
         "first",
         [smem_arg(own_ids), table, vmem_arg(picked), vmem_arg(swap(picked)), vmem_arg(bias), vmem_arg(psum), vmem_arg(hc)]
-        + [hbm_arg(primal_start)],
-        [vmem_out(*tile), vmem_out(TS, L), vmem_out(PLANE * MSG, L), smem_out(8, L)],
-        [vmem(*tile), vmem(512, L), vmem(512, L), pltpu.VMEM((8, L), jnp.int32)]
-        + [pltpu.SemaphoreType.DMA((2 * NRB,)), pltpu.SemaphoreType.DMA(())],
+        + [vmem_arg(start), hbm_arg(primal_start)],
+        [vmem_out(*tile), vmem_out(TS, L), vmem_out(MSG, L), smem_out(8, L)],
+        [vmem(*tile[1:]), vmem(512, L), vmem(512, L), pltpu.VMEM((8, L), jnp.int32)]
+        + [pltpu.SemaphoreType.DMA((NRB,)), pltpu.SemaphoreType.DMA(())],
         8,
     )
-    part = exchange(message, PLANE_GROUPS, MSG)
-    parts = call(users_kernel, "users", [smem_arg(ids), part], [vmem_out(2 * MSG, L)] * 4, [vmem((BLOCKS + 1) * 8, L)] * 4)
-    parts = [parts[0]] + [lax.ppermute(parts[d], "tiles", along_x(d)) for d in range(1, 4)]
-    mine, other = call(join_kernel, "join", [vmem_arg(v) for v in parts], [vmem_out(MSG, L)] * 2)
-
+    (both,) = call(pair_kernel, "pair", [vmem_arg(message), vmem_arg(swap(message))], [vmem_out(2 * MSG, L)])
+    parts = [vmem_arg(both)] + [vmem_arg(lax.ppermute(both, "tiles", along_x(d))) for d in range(1, 4)]
+    (message,) = call(
+        users_kernel,
+        "users",
+        [smem_arg(ids)] + parts,
+        [vmem_out(PLANE * MSG, L)],
+        [vmem(8 * MSG, L)] + [vmem((BLOCKS + 1) * 8, L)] * 4,
+    )
     primal, sums, own = call(
         second_kernel,
         "second",
-        [vmem_arg(mine), vmem_arg(swap(other)), vmem_arg(base), vmem_arg(usum)],
+        [exchange(message, PLANE_GROUPS, MSG), vmem_arg(base), vmem_arg(usum)],
         [(f32(*tile), pl.BlockSpec(memory_space=pl.ANY)), vmem_out(TS, L), vmem_out(OUT, L)],
         [vmem(*tile), vmem(TS, L), vmem(512, L), vmem(512, L), pltpu.SemaphoreType.DMA((2 * NRB,))],
         8,

time: 76.5 us -> 74.5 us (0.974)
  starting transfers between devices: 17.7 us -> 15 us
  waiting for transfers between devices: 10.1 us -> 11.8 us
  blocking collectives: 30.3 us -> 29.1 us
    ppermute x3, starting transfers between devices: 5.64 us -> 2.66 us  [body(): lax.ppermute(both, 'tiles', along_x(d))]
    ppermute x3, waiting for transfers between devices: 2.6 us -> 5.16 us  [body(): lax.ppermute(both, 'tiles', along_x(d))]
    ppermute x4, waiting for transfers between devices: 3.36 us -> 2.01 us  [swap(): return lax.ppermute(x, 'tiles', PARTNERS)]
    all_to_all x2, blocking collectives: 30.3 us -> 29.1 us  [exchange(): lax.all_to_all(x.reshape(n, rows * L), 'tiles', 0, 0, axis_index_groups=g...]
    pallas_call x8 -> x9, Pallas kernels: 9.34 us -> 9.89 us  [call(): pl.pallas_call(kernel, in_specs=[s for _, s in ins], out_specs=[s for _,...]
  transfers between devices with their start and end apart: 8 -> 8, of which waited for: 6 -> 6; matrix products, arithmetic and copies ran while one was open for 0% -> 0% of each run, Pallas kernels for 10% -> 12%
where the time goes in v5:
time: 74.5 us; the launch traced here: 74 us
  blocking collectives  29.1 us (39%)
  Pallas kernels  17.2 us (23%)
  starting transfers between devices  15 us (20%)
  waiting for transfers between devices  11.8 us (16%)
  between operations  0.75 us (1%)
    all_to_all x2, blocking collectives, exchange(): lax.all_to_all(x.reshape(n, rows * L), 'tiles', 0, 0, axis_index_groups=g...  29.1 us
    all_to_all x1, starting transfers between devices, exchange(): lax.all_to_all(x.reshape(n, rows * L), 'tiles', 0, 0, axis_index_groups=g...  11.5 us
    pallas_call x9, Pallas kernels, call(): pl.pallas_call(kernel, in_specs=[s for _, s in ins], out_specs=[s for _,...  9.89 us
    pallas_call x1, Pallas kernels, body(): pl.pallas_call(prepare_kernel, grid=(2, NRB), in_specs=[IN_SMEM, IN_SMEM,...  7.35 us
    ppermute x3, waiting for transfers between devices, body(): lax.ppermute(both, 'tiles', along_x(d))  5.16 us
    all_to_all x1, waiting for transfers between devices, exchange(): lax.all_to_all(x.reshape(n, rows * L), 'tiles', 0, 0, axis_index_groups=g...  4.65 us
    ppermute x3, starting transfers between devices, body(): lax.ppermute(both, 'tiles', along_x(d))  2.66 us
    ppermute x4, waiting for transfers between devices, swap(): return lax.ppermute(x, 'tiles', PARTNERS)  2.01 us
  transfers between devices with their start and end apart: 8, of which 6 were waited for; matrix products, arithmetic and copies ran while one was open for 0% of the time, Pallas kernels for 12%

profile of v5, /device:TPU:0, one launch (start us, length us, event | category | flops | bytes accessed | tf_op | source)
XLA Modules:
  0.0 74.0 jit_solution(5937196239071543430)
XLA Ops:
  0.6 2.4 %own.1 = (f32[832,128]{1,0:T(8,128)}, f32[12,128]{1,0:T(8,128)S(1)}, f32[12,128]{1,0:T(8,128)S(1)}, s32[8,128]{1,0:T(8,128)S(1)}, s32[4]{0:T(128)S(4)}, /*index=5*/s32[2,8,64]{2,1,0:T(8,128)S(4)}) custom-call(s32[2]{0:T(128)} %adv_id.1, s32[2]{0:T(128)} %slot_id.1, f32[4,128]{1,0:T(4,128)} %bitcast.22, f32[8,128]{1,0:T(8,128)} %bitcast.20, ...), custom_call_target="tpu_custom_call" | custom-call | tf_op jit(solution)/shard_map/own/pallas_call | solution.py:357
  3.0 11.5 %all-to-all-start = ((f32[64,1,1664]{2,1,0:T(1,128)}), f32[64,1,1664]{2,1,0:T(1,128)S(1)}, u32[]{:S(2)}, u32[]{:S(2)}) async-start(f32[64,1,1664]{2,1,0:T(1,128)} %bitcast.5), calls=%async_computation | async-start | bytes 851968 | tf_op jit(solution)/shard_map/all_to_all | solution.py:394
  14.6 0.1 collective-permute-start
  14.6 7.3 %prepare.1 = (bf16[2,512,1024]{2,1,0:T(8,128)(2,1)S(1)}, f32[24,128]{1,0:T(8,128)S(1)}) custom-call(s32[4]{0:T(128)S(4)} %get-tuple-element.20.own_ids, s32[2,8,64]{2,1,0:T(8,128)S(4)} %get-tuple-element.23.mask, f32[2,512,1024]{2,1,0:T(8,128)} %p_hbm.3, bf16[2,512,1024]{2,1,0:T(8,128)(2,1)} %c_ref.1), custom_call_target="tpu_custom_call" | custom-call | tf_op jit(solution)/shard_map/prepare/pallas_call | solution.py:416
  22.0 0.0 collective-permute-done.partner_ids
  22.0 4.7 %all-to-all-done = f32[64,1,1664]{2,1,0:T(1,128)S(1)} async-done(((f32[64,1,1664]{2,1,0:T(1,128)}), f32[64,1,1664]{2,1,0:T(1,128)S(1)}, u32[]{:S(2)}, u32[]{:S(2)}) %all-to-all-start) | async-done | bytes 426016 | tf_op jit(solution)/shard_map/all_to_all | solution.py:394
  26.7 0.2 pick.1._.mine
  26.9 0.1 collective-permute-start.1
  27.0 1.6 %load.1.p0_ref = f32[512,1024]{1,0:T(8,128)S(1)} custom-call(f32[2,512,1024]{2,1,0:T(8,128)} %p_hbm.3, f32[32,128]{1,0:T(8,128)S(1)} %pick.1._.mine), custom_call_target="tpu_custom_call" | custom-call | tf_op jit(solution)/shard_map/load/pallas_call | solution.py:357
  28.6 0.0 collective-permute-done.1.other
  28.6 2.0 %first.1 = (f32[2,512,1024]{2,1,0:T(8,128)S(1)}, f32[24,128]{1,0:T(8,128)S(1)}, f32[36,128]{1,0:T(8,128)S(1)}, s32[8,128]{1,0:T(8,128)S(4)}) custom-call(s32[4]{0:T(128)S(4)} %get-tuple-element.20.own_ids, f32[832,128]{1,0:T(8,128)S(1)} %bitcast.14, f32[32,128]{1,0:T(8,128)S(1)} %pick.1._.mine, f32[32,128]{1,0:T(8,128)S(1)} %collective-permute-done.1.other, ...), custom_call_target="tpu_custom_call" | custom-call | tf_op jit(solution)/shard_map/first/pallas_call | solution.py:357
  30.6 0.6 collective-permute-start.2
  31.2 0.8 %collective-permute-done.2.b = f32[36,128]{1,0:T(8,128)S(1)} collective-permute-done((f32[36,128]{1,0:T(8,128)S(1)}, f32[36,128]{1,0:T(8,128)S(1)}, u32[]{:S(2)}, u32[]{:S(2)}) %collective-permute-start.2) | collective-permute-done | bytes 18464 | tf_op jit(solution)/shard_map/ppermute | solution.py:399
  32.0 1.0 %collective-permute-start.5 = (f32[72,128]{1,0:T(8,128)S(1)}, f32[72,128]{1,0:T(8,128)S(1)}, u32[]{:S(2)}, u32[]{:S(2)}) collective-permute-start(f32[72,128]{1,0:T(8,128)S(1)} %pair.1.rec0), channel_id=1, source_target_pairs={{0,96},{1,97},{2,98},{3,99},{4,100},{5,101},{6,102},{7,103},{8,104... | collective-permute-start | bytes 110600 | tf_op jit(solution)/shard_map/ppermute | solution.py:445
  33.0 1.7 %collective-permute-start.4 = (f32[72,128]{1,0:T(8,128)S(1)}, f32[72,128]{1,0:T(8,128)S(1)}, u32[]{:S(2)}, u32[]{:S(2)}) collective-permute-start(f32[72,128]{1,0:T(8,128)S(1)} %pair.1.rec0), channel_id=1, source_target_pairs={{0,64},{1,65},{2,66},{3,67},{4,68},{5,69},{6,70},{7,71},{8,72},{9,... | collective-permute-start | bytes 110600 | tf_op jit(solution)/shard_map/ppermute | solution.py:445
  34.7 0.0 collective-permute-start.3
  34.7 1.5 %collective-permute-done.5.rec3 = f32[72,128]{1,0:T(8,128)S(1)} collective-permute-done((f32[72,128]{1,0:T(8,128)S(1)}, f32[72,128]{1,0:T(8,128)S(1)}, u32[]{:S(2)}, u32[]{:S(2)}) %collective-permute-start.5) | collective-permute-done | bytes 36896 | tf_op jit(solution)/shard_map/ppermute | solution.py:445
  36.2 2.3 %collective-permute-done.4.rec2 = f32[72,128]{1,0:T(8,128)S(1)} collective-permute-done((f32[72,128]{1,0:T(8,128)S(1)}, f32[72,128]{1,0:T(8,128)S(1)}, u32[]{:S(2)}, u32[]{:S(2)}) %collective-permute-start.4) | collective-permute-done | bytes 36896 | tf_op jit(solution)/shard_map/ppermute | solution.py:445
  38.5 1.4 %collective-permute-done.3.rec1 = f32[72,128]{1,0:T(8,128)S(1)} collective-permute-done((f32[72,128]{1,0:T(8,128)S(1)}, f32[72,128]{1,0:T(8,128)S(1)}, u32[]{:S(2)}, u32[]{:S(2)}) %collective-permute-start.3) | collective-permute-done | bytes 36896 | tf_op jit(solution)/shard_map/ppermute | solution.py:445
  39.9 0.7 users.1
  40.5 12.2 %all_to_all.27 = f32[16,1,4608]{2,1,0:T(1,128)S(1)} all-to-all(f32[16,1,4608]{2,1,0:T(1,128)S(1)} %bitcast.18), channel_id=1, replica_groups={{0,2,4,6,8,10,12,14,16,18,20,22,24,26,28,30},{1,3,5,7,9,11,13,15,17,19,..., dimensions={0} | all-to-all | bytes 589824 | tf_op jit(solution)/shard_map/all_to_all | solution.py:394
  52.7 2.3 %second.1 = (f32[2,512,1024]{2,1,0:T(8,128)}, f32[24,128]{1,0:T(8,128)S(1)}, f32[12,128]{1,0:T(8,128)S(1)}) custom-call(f32[576,128]{1,0:T(8,128)S(1)} %bitcast.17, f32[2,512,1024]{2,1,0:T(8,128)S(1)} %get-tuple-element.29.base, f32[24,128]{1,0:T(8,128)S(1)} %get-tuple-element.30.psum), custom_call_target="tpu_custom_call" | custom-call | tf_op jit(solution)/shard_map/second/pallas_call | solution.py:357
  55.0 0.1 collective-permute-start.6
  55.1 1.2 %collective-permute-done.6.other = f32[24,128]{1,0:T(8,128)S(1)} collective-permute-done((f32[24,128]{1,0:T(8,128)S(1)}, f32[24,128]{1,0:T(8,128)S(1)}, u32[]{:S(2)}, u32[]{:S(2)}) %collective-permute-start.6) | collective-permute-done | bytes 12320 | tf_op jit(solution)/shard_map/ppermute | solution.py:399
  56.3 0.1 owners.1
  56.4 16.9 %all_to_all.28 = f32[64,1,1536]{2,1,0:T(1,128)S(1)} all-to-all(f32[64,1,1536]{2,1,0:T(1,128)S(1)} %bitcast.16), channel_id=1, replica_groups={{0,2,4,6,8,10,12,14,16,18,20,22,24,26,28,30,32,34,36,38,40,42,44,46,48,..., dimensions={0} | all-to-all | bytes 786432 | tf_op jit(solution)/shard_map/all_to_all | solution.py:394
  73.3 0.6 last.1
  (1 shorter events, 0.0 us)
Async XLA Ops:
  3.0 23.7 %all-to-all-start = ((f32[64,1,1664]{2,1,0:T(1,128)}), f32[64,1,1664]{2,1,0:T(1,128)S(1)}, u32[]{:S(2)}, u32[]{:S(2)}) async-start(f32[64,1,1664]{2,1,0:T(1,128)} %bitcast.5), calls=%async_computation | async-start | bytes 851968 | tf_op jit(solution)/shard_map/all_to_all | solution.py:394
  14.6 7.5 %collective-permute-start = (s32[8,128]{1,0:T(8,128)S(1)}, s32[8,128]{1,0:T(8,128)S(1)}, u32[]{:S(2)}, u32[]{:S(2)}) collective-permute-start(s32[8,128]{1,0:T(8,128)S(1)} %get-tuple-element.22), channel_id=1, source_target_pairs={{0,1},{1,0},{2,3},{3,2},{4,5},{5,4},{6,7},{7,6},{8,9},{9,8},{10,11... | collective-permute-start | bytes 12296 | tf_op jit(solution)/shard_map/ppermute | solution.py:399
  26.9 1.7 %collective-permute-start.1 = (f32[32,128]{1,0:T(8,128)S(1)}, f32[32,128]{1,0:T(8,128)S(1)}, u32[]{:S(2)}, u32[]{:S(2)}) collective-permute-start(f32[32,128]{1,0:T(8,128)S(1)} %pick.1._.mine), channel_id=1, source_target_pairs={{0,1},{1,0},{2,3},{3,2},{4,5},{5,4},{6,7},{7,6},{8,9},{9,8},{10,11... | collective-permute-start | bytes 49160 | tf_op jit(solution)/shard_map/ppermute | solution.py:399
  30.6 1.4 %collective-permute-start.2 = (f32[36,128]{1,0:T(8,128)S(1)}, f32[36,128]{1,0:T(8,128)S(1)}, u32[]{:S(2)}, u32[]{:S(2)}) collective-permute-start(f32[36,128]{1,0:T(8,128)S(1)} %get-tuple-element.28.a), channel_id=1, source_target_pairs={{0,1},{1,0},{2,3},{3,2},{4,5},{5,4},{6,7},{7,6},{8,9},{9,8},{10,11... | collective-permute-start | bytes 55304 | tf_op jit(solution)/shard_map/ppermute | solution.py:399
  32.0 4.1 %collective-permute-start.5 = (f32[72,128]{1,0:T(8,128)S(1)}, f32[72,128]{1,0:T(8,128)S(1)}, u32[]{:S(2)}, u32[]{:S(2)}) collective-permute-start(f32[72,128]{1,0:T(8,128)S(1)} %pair.1.rec0), channel_id=1, source_target_pairs={{0,96},{1,97},{2,98},{3,99},{4,100},{5,101},{6,102},{7,103},{8,104... | collective-permute-start | bytes 110600 | tf_op jit(solution)/shard_map/ppermute | solution.py:445
  33.0 5.5 %collective-permute-start.4 = (f32[72,128]{1,0:T(8,128)S(1)}, f32[72,128]{1,0:T(8,128)S(1)}, u32[]{:S(2)}, u32[]{:S(2)}) collective-permute-start(f32[72,128]{1,0:T(8,128)S(1)} %pair.1.rec0), channel_id=1, source_target_pairs={{0,64},{1,65},{2,66},{3,67},{4,68},{5,69},{6,70},{7,71},{8,72},{9,... | collective-permute-start | bytes 110600 | tf_op jit(solution)/shard_map/ppermute | solution.py:445
  34.7 5.2 %collective-permute-start.3 = (f32[72,128]{1,0:T(8,128)S(1)}, f32[72,128]{1,0:T(8,128)S(1)}, u32[]{:S(2)}, u32[]{:S(2)}) collective-permute-start(f32[72,128]{1,0:T(8,128)S(1)} %pair.1.rec0), channel_id=1, source_target_pairs={{0,32},{1,33},{2,34},{3,35},{4,36},{5,37},{6,38},{7,39},{8,40},{9,... | collective-permute-start | bytes 110600 | tf_op jit(solution)/shard_map/ppermute | solution.py:445
  55.0 1.3 %collective-permute-start.6 = (f32[24,128]{1,0:T(8,128)S(1)}, f32[24,128]{1,0:T(8,128)S(1)}, u32[]{:S(2)}, u32[]{:S(2)}) collective-permute-start(f32[24,128]{1,0:T(8,128)S(1)} %get-tuple-element.32.mine), channel_id=1, source_target_pairs={{0,1},{1,0},{2,3},{3,2},{4,5},{5,4},{6,7},{7,6},{8,9},{9,8},{10,11... | collective-permute-start | bytes 36872 | tf_op jit(solution)/shard_map/ppermute | solution.py:399

commit v6 on v5

--- a/solution.py
+++ b/solution.py
@@ -1,3 +1,5 @@
+import functools
+
 import jax
 import jax.numpy as jnp
 from jax import lax
@@ -18,6 +20,8 @@
 RB = 128
 NRB = 4
 BIG = 1e30
+HEAD = 256
+TAIL = 256
 
 PLANE = 16
 CORE_GROUPS = [[j * 2 + c for j in range(CHIPS)] for c in range(2)]
@@ -33,9 +37,7 @@
 IN_SMEM = pl.BlockSpec(memory_space=pltpu.SMEM)
 
 
-def own_kernel(adv_id, slot_id, adv, slot, limit, cap, mask_hbm, out, bias, bounds, row_ids, ids, mask, sem):
-    keep_mask = pltpu.make_async_copy(mask_hbm, mask, sem)
-    keep_mask.start()
+def own_kernel(adv_id, slot_id, adv, slot, limit, cap, out, bias, bounds, row_ids, ids):
     lane = lax.broadcasted_iota(jnp.int32, (8, L), 1)
     row = jnp.zeros((8, L), jnp.int32)
     for k, v in enumerate((adv_id[0], adv_id[1], slot_id[0], slot_id[1])):
@@ -49,7 +51,6 @@
     bias[SR:OUT, :] = adv[...] * 1024.0 - limit[...]
     bounds[0:SR, :] = cap[...]
     bounds[SR:OUT, :] = limit[...]
-    keep_mask.wait()
 
 
 def rows_of(rec, i, slot):
@@ -95,59 +96,61 @@
 ZEROS = lambda: (jnp.zeros((8, L), jnp.float32),) * SR
 
 
-def prepare_kernel(own_ids, mask, p_ref, c_ref, hc, psum, r_buf, col_buf):
-    t = pl.program_id(0)
-    rb = pl.program_id(1)
-
-    @pl.when(rb == 0)
-    def _():
-        col_buf[...] = jnp.zeros_like(col_buf)
-
-    alive = jnp.where(own_ids[t] >= 0, 1, 0)
-
-    def step(g, cols):
-        r0 = pl.multiple_of(g * 16, 16)
-        cols = list(cols)
-        ps = [[], []]
-        for cb in range(SR):
-            lanes = pl.ds(cb * L, L)
-            c16 = 0.5 * c_ref[0, pl.ds(r0, 16), lanes].astype(jnp.float32)
-            halves = []
+def prepare_kernel(own_ids, mask, p_hbm, c_hbm, hc, psum, p_ref, c_ref, r_buf, p_sems, c_sems):
+    def fetch(t, b):
+        rows = pl.ds(b * RB, RB)
+        n = t * NRB + b
+        return (
+            pltpu.make_async_copy(p_hbm.at[t, rows, :], p_ref.at[t, rows, :], p_sems.at[n]),
+            pltpu.make_async_copy(c_hbm.at[t, rows, :], c_ref.at[t, rows, :], c_sems.at[n]),
+        )
+
+    for t in range(2):
+        for b in range(NRB):
+            for copy in fetch(t, b):
+                copy.start()
+    for t in range(2):
+        alive = jnp.where(own_ids[t] >= 0, 1, 0)
+
+        def step(g, cols):
+            r0 = pl.multiple_of(g * 16, 16)
+            cols = list(cols)
+            ps = [[], []]
+            for cb in range(SR):
+                lanes = pl.ds(cb * L, L)
+                c16 = 0.5 * c_ref[t, pl.ds(r0, 16), lanes].astype(jnp.float32)
+                halves = []
+                for h in range(2):
+                    here = jnp.full((8, L), mask[t, cb, g * 2 + h] * alive, jnp.int32) > 0
+                    rows = pl.ds(pl.multiple_of(r0 + 8 * h, 8), 8)
+                    p = jnp.where(here, p_ref[t, rows, lanes], 0.0)
+                    halves.append(jnp.where(here, c16[8 * h : 8 * h + 8], BIG))
+                    ps[h].append(p)
+                    cols[cb] = cols[cb] + p
+                hc[t, pl.ds(r0, 16), lanes] = jnp.concatenate(halves, axis=0).astype(jnp.bfloat16)
             for h in range(2):
-                here = jnp.full((8, L), mask[t, cb, rb * 16 + g * 2 + h] * alive, jnp.int32) > 0
-                rows = pl.ds(pl.multiple_of(r0 + 8 * h, 8), 8)
-                p = jnp.where(here, p_ref[0, rows, lanes], 0.0)
-                halves.append(jnp.where(here, c16[8 * h : 8 * h + 8], BIG))
-                ps[h].append(p)
-                cols[cb] = cols[cb] + p
-            hc[t, pl.ds(pl.multiple_of(rb * RB + r0, 16), 16), lanes] = jnp.concatenate(halves, axis=0).astype(jnp.bfloat16)
-        for h in range(2):
-            r_buf[pl.ds(pl.multiple_of(r0 + 8 * h, 8), 8), :] = tree(ps[h])
-        return tuple(cols)
-
-    cols = tuple(col_buf[pl.ds(cb * 8, 8), :] for cb in range(SR))
-    cols = lax.fori_loop(0, RB // 16, step, cols)
-    for cb in range(SR):
-        col_buf[pl.ds(cb * 8, 8), :] = cols[cb]
-    psum[pl.ds(t * AR + rb, 1), :] = jnp.sum(r_buf[...].T, axis=0, keepdims=True)
-
-    @pl.when(rb == NRB - 1)
-    def _():
-        rows = [jnp.sum(cols[cb], axis=0, keepdims=True) for cb in range(SR)]
-        psum[pl.ds(pl.multiple_of(8 + t * SR, 8), SR), :] = jnp.concatenate(rows, axis=0)
+                r_buf[pl.ds(pl.multiple_of(r0 + 8 * h, 8), 8), :] = tree(ps[h])
+            return tuple(cols)
+
+        cols = ZEROS()
+        for b in range(NRB):
+            for copy in fetch(t, b):
+                copy.wait()
+            cols = lax.fori_loop(b * 8, (b + 1) * 8, step, cols)
+        write_sums(t, psum, r_buf, cols)
 
 
 def load_kernel(p_hbm, _, out, sem):
-    copy = pltpu.make_async_copy(p_hbm.at[0], out, sem)
+    copy = pltpu.make_async_copy(p_hbm.at[0, pl.ds(0, HEAD), :], out, sem)
     copy.start()
     copy.wait()
 
 
-def first_tile(t, arow, srow, p_ref, hc_ref, out, usum, a_buf, r_buf, ready):
+def first_tile(t, arow, srow, sources, hc_ref, out, usum, a_buf, r_buf, ready):
     spread_half(arow, a_buf)
     s = slot_rows(srow)
 
-    def step(g, cols):
+    def step(p_ref, skip, g, cols):
         cols = list(cols)
         us = [[], []]
         r0 = pl.multiple_of(g * 16, 16)
@@ -158,7 +161,7 @@
             for h in range(2):
                 rows = pl.ds(pl.multiple_of(r0 + 8 * h, 8), 8)
                 hc = c16[8 * h : 8 * h + 8]
-                u = jnp.minimum(jnp.maximum(((p_ref[rows, lanes] - hc) - a[h]) - s[cb], 0.0), 1.0)
+                u = jnp.minimum(jnp.maximum(((p_ref[pl.ds(pl.multiple_of(r0 + 8 * h - skip, 8), 8), lanes] - hc) - a[h]) - s[cb], 0.0), 1.0)
                 out[t, rows, lanes] = u - hc
                 us[h].append(u)
                 cols[cb] = cols[cb] + u
@@ -169,17 +172,21 @@
     cols = ZEROS()
     for b in range(NRB):
         ready(b)
-        cols = lax.fori_loop(b * 8, (b + 1) * 8, step, cols, unroll=2)
+        cols = lax.fori_loop(b * 8, (b + 1) * 8, functools.partial(step, *sources[b]), cols, unroll=2)
     write_sums(t, usum, r_buf, cols)
 
 
-def first_kernel(own_ids, rec, mine, other, bias, psum, hc_ref, p0_ref, p_hbm, out, usum, msg, ids, p1_ref, a_buf, r_buf, id_buf, p_sems, sem):
-    def fetch(b):
-        rows = pl.ds(b * RB, RB)
-        return pltpu.make_async_copy(p_hbm.at[1, rows, :], p1_ref.at[rows, :], p_sems.at[b])
-
-    for b in range(NRB):
-        fetch(b).start()
+def first_kernel(own_ids, rec, mine, other, bias, psum, hc_ref, head, p_hbm, out, usum, msg, ids, p_ref, a_buf, r_buf, id_buf, p_sems, sem):
+    def fetch(t, b):
+        n = (t * NRB + b) * RB - HEAD
+        return pltpu.make_async_copy(p_hbm.at[t, pl.ds(b * RB, RB), :], p_ref.at[pl.ds(n, RB), :], p_sems.at[n // RB])
+
+    def ready(t, b):
+        if (t * NRB + b) * RB >= HEAD:
+            fetch(t, b).wait()
+
+    for n in range(HEAD // RB, 2 * NRB):
+        fetch(*divmod(n, NRB)).start()
     core = lax.axis_index("tiles") & 1
     id_buf[0:4, :] = mine[TS : TS + 4, :].astype(jnp.int32)
     id_buf[4:8, :] = other[TS : TS + 4, :].astype(jnp.int32)
@@ -189,18 +196,8 @@
         a, s = own_ids[t], own_ids[2 + t]
         arow = jnp.where((a & 1) == core, rows_of(rec, a, False), other[AR * t : AR * (t + 1), :])
         srow = jnp.where((s & 1) == core, rows_of(rec, s, True), other[8 + SR * t : 8 + SR * (t + 1), :])
-        first_tile(
-            t,
-            arow,
-            srow,
-            (p0_ref, p1_ref)[t],
-            hc_ref,
-            out,
-            usum,
-            a_buf,
-            r_buf,
-            (lambda b: None, lambda b: fetch(b).wait())[t],
-        )
+        sources = [(head, 0) if t * 512 + b * RB < HEAD else (p_ref, HEAD - t * 512) for b in range(NRB)]
+        first_tile(t, arow, srow, sources, hc_ref, out, usum, a_buf, r_buf, functools.partial(ready, t))
     msg[0:TS, :] = 2.0 * usum[...] - psum[...]
     msg[TS:MSG, :] = bias[...]
     keep_ids.wait()
@@ -265,11 +262,11 @@
             out[o : o + SR, :] = (acc_s0[rows, :] + acc_s1[rows, :]) + bias(i, TS, SR)
 
 
-def second_tile(t, arow, srow, base, out, usum, a_buf, r_buf, done):
+def second_tile(t, arow, srow, base, outs, usum, a_buf, r_buf, done):
     spread_half(arow, a_buf)
     s = slot_rows(srow)
 
-    def step(g, cols):
+    def step(out, skip, g, cols):
         rows = pl.ds(pl.multiple_of(g * 8, 8), 8)
         a = a_buf[rows, :]
         cols = list(cols)
@@ -277,7 +274,7 @@
         for cb in range(SR):
             lanes = pl.ds(cb * L, L)
             u = jnp.minimum(jnp.maximum((base[t, rows, lanes] - a) - s[cb], 0.0), 1.0)
-            out[t, rows, lanes] = u
+            out[pl.ds(pl.multiple_of(g * 8 - skip, 8), 8), lanes] = u
             cols[cb] = cols[cb] + u
             us.append(u)
         r_buf[rows, :] = tree(us)
@@ -285,15 +282,21 @@
 
     cols = ZEROS()
     for b in range(NRB):
-        cols = lax.fori_loop(b * 16, (b + 1) * 16, step, cols, unroll=4)
+        cols = lax.fori_loop(b * 16, (b + 1) * 16, functools.partial(step, *outs[b]), cols, unroll=4)
         done(t, b)
     write_sums(t, usum, r_buf, cols)
 
 
-def second_kernel(rec, base, psum, primal, sums, own, out, usum, a_buf, r_buf, sems):
+def second_kernel(rec, base, psum, primal, sums, own, tail, out, usum, a_buf, r_buf, sems):
+    early = 1024 - TAIL
+
     def keep(t, b):
-        rows = pl.ds(b * RB, RB)
-        return pltpu.make_async_copy(out.at[t, rows, :], primal.at[t, rows, :], sems.at[t * NRB + b])
+        n = t * NRB + b
+        return pltpu.make_async_copy(out.at[pl.ds(n * RB, RB), :], primal.at[t, pl.ds(b * RB, RB), :], sems.at[n])
+
+    def done(t, b):
+        if (t * NRB + b) * RB < early:
+            keep(t, b).start()
 
     total = tree([rec[j * MSG : (j + 1) * MSG, :] for j in range(PLANE)])
     adv = jnp.maximum(total[0:8] * (1.0 / 1024), 0.0)
@@ -301,16 +304,21 @@
     own[0:SR, :] = slot[16:24]
     own[SR:OUT, :] = jnp.maximum(total[32:36] * (1.0 / 1024), 0.0)
     for t in range(2):
-        second_tile(
-            t, adv[4 * t : 4 * t + 4], slot[8 * t : 8 * t + 8], base, out, usum, a_buf, r_buf, lambda t, b: keep(t, b).start()
-        )
+        outs = [(out, -t * 512) if t * 512 + b * RB < early else (tail, early - t * 512) for b in range(NRB)]
+        second_tile(t, adv[4 * t : 4 * t + 4], slot[8 * t : 8 * t + 8], base, outs, usum, a_buf, r_buf, done)
     sums[...] = 2.0 * usum[...] - psum[...]
-    for t in range(2):
-        for b in range(NRB):
-            keep(t, b).wait()
-
-
-def owners_kernel(ids, mine, other, out):
+    for n in range(early // RB):
+        keep(*divmod(n, NRB)).wait()
+
+
+def store_kernel(tail, _, primal, sem):
+    copy = pltpu.make_async_copy(tail, primal.at[1, pl.ds(512 - TAIL, TAIL), :], sem)
+    copy.start()
+    copy.wait()
+
+
+def owners_kernel(ids, mine, other, _, out):
+
     me = lax.axis_index("tiles")
     chip = me >> 1
     core = me & 1
@@ -353,7 +361,7 @@
     return pltpu.with_memory_space_constraint(x, pltpu.SMEM)
 
 
-def call(kernel, name, ins, outs, scratch=(), mib=4):
+def call(kernel, name, ins, outs, scratch=(), mib=4, aliases={}):
     return pl.pallas_call(
         kernel,
         in_specs=[s for _, s in ins],
@@ -361,6 +369,7 @@
         out_shape=[o for o, _ in outs],
         scratch_shapes=list(scratch),
         compiler_params=pltpu.CompilerParams(vmem_limit_bytes=mib << 20),
+        input_output_aliases=aliases,
         name=name,
     )(*[x for x, _ in ins])
 
@@ -401,34 +410,29 @@
 
 def body(primal_start, cost, mask, tile_adv, tile_slot, adv_dual, slot_dual, spend_limit, capacity):
     tile = (2, 512, 1024)
-    message, bias, bounds, row_ids, own_ids, here = call(
+    message, bias, bounds, row_ids, own_ids = call(
         own_kernel,
         "own",
         [(in_hbm(tile_adv), IN_SMEM), (in_hbm(tile_slot), IN_SMEM)]
-        + [(in_hbm(x.reshape(-1, L)), IN_VMEM) for x in (adv_dual, slot_dual, spend_limit, capacity)]
-        + [hbm_arg(mask.transpose(0, 2, 1))],
+        + [(in_hbm(x.reshape(-1, L)), IN_VMEM) for x in (adv_dual, slot_dual, spend_limit, capacity)],
         [vmem_out(CHIPS * OWN, L), vmem_out(OUT, L), vmem_out(OUT, L)]
-        + [(pltpu.VMEM((8, L), jnp.int32), IN_VMEM), smem_out(4), smem_out(2, 8, 64)],
-        [pltpu.SemaphoreType.DMA(())],
+        + [(pltpu.VMEM((8, L), jnp.int32), IN_VMEM), smem_out(4)],
     )
     table = exchange(message, CORE_GROUPS, OWN)
-    block = pl.BlockSpec((1, RB, 1024), lambda t, rb: (t, rb, 0))
-    hc, psum = pl.pallas_call(
+    hc, psum = call(
         prepare_kernel,
-        grid=(2, NRB),
-        in_specs=[IN_SMEM, IN_SMEM, block, block],
-        out_specs=[IN_VMEM, IN_VMEM],
-        out_shape=[pltpu.VMEM(tile, jnp.bfloat16), vmem(TS, L)],
-        scratch_shapes=[vmem(RB, L), vmem(64, L)],
-        compiler_params=pltpu.CompilerParams(vmem_limit_bytes=4 << 20),
-        name="prepare",
-    )(in_smem(own_ids), in_smem(here), in_hbm(primal_start), in_hbm(cost))
+        "prepare",
+        [smem_arg(own_ids), (in_hbm(mask.transpose(0, 2, 1)), IN_SMEM), hbm_arg(primal_start), hbm_arg(cost)],
+        [(pltpu.VMEM(tile, jnp.bfloat16), IN_VMEM), vmem_out(TS, L)],
+        [vmem(*tile), pltpu.VMEM(tile, jnp.bfloat16), vmem(512, L)] + [pltpu.SemaphoreType.DMA((2 * NRB,))] * 2,
+        8,
+    )
     (picked,) = call(pick_kernel, "pick", [vmem_arg(swap(row_ids)), table, vmem_arg(psum)], [vmem_out(SEL, L)])
     (start,) = call(
         load_kernel,
         "load",
         [hbm_arg(primal_start), vmem_arg(picked)],
-        [vmem_out(*tile[1:])],
+        [vmem_out(HEAD, 1024)],
         [pltpu.SemaphoreType.DMA(())],
     )
     base, usum, message, ids = call(
@@ -437,8 +441,8 @@
         [smem_arg(own_ids), table, vmem_arg(picked), vmem_arg(swap(picked)), vmem_arg(bias), vmem_arg(psum), vmem_arg(hc)]
         + [vmem_arg(start), hbm_arg(primal_start)],
         [vmem_out(*tile), vmem_out(TS, L), vmem_out(MSG, L), smem_out(8, L)],
-        [vmem(*tile[1:]), vmem(512, L), vmem(512, L), pltpu.VMEM((8, L), jnp.int32)]
-        + [pltpu.SemaphoreType.DMA((NRB,)), pltpu.SemaphoreType.DMA(())],
+        [vmem(1024 - HEAD, 1024), vmem(512, L), vmem(512, L), pltpu.VMEM((8, L), jnp.int32)]
+        + [pltpu.SemaphoreType.DMA((2 * NRB - HEAD // RB,)), pltpu.SemaphoreType.DMA(())],
         8,
     )
     (both,) = call(pair_kernel, "pair", [vmem_arg(message), vmem_arg(swap(message))], [vmem_out(2 * MSG, L)])
@@ -450,16 +454,28 @@
         [vmem_out(PLANE * MSG, L)],
         [vmem(8 * MSG, L)] + [vmem((BLOCKS + 1) * 8, L)] * 4,
     )
-    primal, sums, own = call(
+    primal, sums, own, tail = call(
         second_kernel,
         "second",
         [exchange(message, PLANE_GROUPS, MSG), vmem_arg(base), vmem_arg(usum)],
-        [(f32(*tile), pl.BlockSpec(memory_space=pl.ANY)), vmem_out(TS, L), vmem_out(OUT, L)],
-        [vmem(*tile), vmem(TS, L), vmem(512, L), vmem(512, L), pltpu.SemaphoreType.DMA((2 * NRB,))],
+        [(f32(*tile), pl.BlockSpec(memory_space=pl.ANY))] + [vmem_out(TS, L), vmem_out(OUT, L), vmem_out(TAIL, 1024)],
+        [vmem(1024 - TAIL, 1024), vmem(TS, L), vmem(512, L), vmem(512, L)]
+        + [pltpu.SemaphoreType.DMA((2 * NRB - TAIL // RB,))],
         8,
     )
+    (primal,) = call(
+        store_kernel,
+        "store",
+        [vmem_arg(tail), hbm_arg(primal)],
+        [(f32(*tile), pl.BlockSpec(memory_space=pl.ANY))],
+        [pltpu.SemaphoreType.DMA(())],
+        aliases={1: 0},
+    )
     (message,) = call(
-        owners_kernel, "owners", [smem_arg(ids), vmem_arg(sums), vmem_arg(swap(sums))], [vmem_out(CHIPS * OUT, L)]
+        owners_kernel,
+        "owners",
+        [smem_arg(ids), vmem_arg(sums), vmem_arg(swap(sums)), hbm_arg(primal)],
+        [vmem_out(CHIPS * OUT, L)],
     )
     adv_out, slot_out = call(
         last_kernel,

time: 74.5 us -> 72.6 us (0.974)
  Pallas kernels: 17.2 us -> 15 us
  waiting for transfers between devices: 11.8 us -> 13.1 us
    pallas_call x1 -> x0, Pallas kernels: 7.35 us -> none  [body(): pl.pallas_call(prepare_kernel, grid=(2, NRB), in_specs=[IN_SMEM, IN_SMEM,...]
    pallas_call x9 -> x11, Pallas kernels: 9.89 us -> 15 us  [call(): pl.pallas_call(kernel, in_specs=[s for _, s in ins], out_specs=[s for _,...]
    all_to_all x1, waiting for transfers between devices: 4.65 us -> 6.9 us  [exchange(): lax.all_to_all(x.reshape(n, rows * L), 'tiles', 0, 0, axis_index_groups=g...]
    ppermute x4, waiting for transfers between devices: 2.01 us -> 1.02 us  [swap(): return lax.ppermute(x, 'tiles', PARTNERS)]
  transfers between devices with their start and end apart: 8 -> 8, of which waited for: 6 -> 6; matrix products, arithmetic and copies ran while one was open for 0% -> 0% of each run, Pallas kernels for 12% -> 10%
where the time goes in v6:
time: 72.6 us; the launch traced here: 72.3 us
  blocking collectives  28.4 us (39%)
  Pallas kernels  15 us (21%)
  starting transfers between devices  15 us (21%)
  waiting for transfers between devices  13.1 us (18%)
  between operations  0.75 us (1%)
    all_to_all x2, blocking collectives, exchange(): lax.all_to_all(x.reshape(n, rows * L), 'tiles', 0, 0, axis_index_groups=g...  28.4 us
    pallas_call x11, Pallas kernels, call(): pl.pallas_call(kernel, in_specs=[s for _, s in ins], out_specs=[s for _,...  15 us
    all_to_all x1, starting transfers between devices, exchange(): lax.all_to_all(x.reshape(n, rows * L), 'tiles', 0, 0, axis_index_groups=g...  11.5 us
    all_to_all x1, waiting for transfers between devices, exchange(): lax.all_to_all(x.reshape(n, rows * L), 'tiles', 0, 0, axis_index_groups=g...  6.9 us
    ppermute x3, waiting for transfers between devices, body(): lax.ppermute(both, 'tiles', along_x(d))  5.16 us
    ppermute x3, starting transfers between devices, body(): lax.ppermute(both, 'tiles', along_x(d))  2.66 us
  transfers between devices with their start and end apart: 8, of which 6 were waited for; matrix products, arithmetic and copies ran while one was open for 0% of the time, Pallas kernels for 10%

profile of v6, /device:TPU:0, one launch (start us, length us, event | category | flops | bytes accessed | tf_op | source)
XLA Modules:
  0.0 72.3 jit_solution(17704953727849544470)
XLA Ops:
  0.6 1.6 %own.1 = (f32[832,128]{1,0:T(8,128)}, f32[12,128]{1,0:T(8,128)S(1)}, f32[12,128]{1,0:T(8,128)S(1)}, s32[8,128]{1,0:T(8,128)S(1)}, s32[4]{0:T(128)S(4)}) custom-call(s32[2]{0:T(128)} %adv_id.1, s32[2]{0:T(128)} %slot_id.1, f32[4,128]{1,0:T(4,128)} %bitcast.22, f32[8,128]{1,0:T(8,128)} %bitcast.20, f32[4,128]{1,0:T(4,128)} %bitcast.23, f32[8,128]{1,0:T(8,128)} %bitcast.21), custom_call_target="tpu_custom_call" | custom-call | tf_op jit(solution)/shard_map/own/pallas_call | solution.py:365
  2.2 11.5 %all-to-all-start = ((f32[64,1,1664]{2,1,0:T(1,128)}), f32[64,1,1664]{2,1,0:T(1,128)S(1)}, u32[]{:S(2)}, u32[]{:S(2)}) async-start(f32[64,1,1664]{2,1,0:T(1,128)} %bitcast.4), calls=%async_computation | async-start | bytes 851968 | tf_op jit(solution)/shard_map/all_to_all | solution.py:403
  13.8 0.1 collective-permute-start
  13.9 5.1 %prepare.1 = (bf16[2,512,1024]{2,1,0:T(8,128)(2,1)S(1)}, f32[24,128]{1,0:T(8,128)S(1)}) custom-call(s32[4]{0:T(128)S(4)} %get-tuple-element.20.own_ids, s32[2,8,64]{2,1,0:T(8,128)} %bitcast.19, f32[2,512,1024]{2,1,0:T(8,128)} %p_hbm.5, bf16[2,512,1024]{2,1,0:T(8,128)(2,1)} %c_hbm.1), custom_call_target="tpu_custom_call" | custom-call | tf_op jit(solution)/shard_map/prepare/pallas_call | solution.py:365
  19.0 0.0 collective-permute-done.partner_ids
  19.0 6.9 %all-to-all-done = f32[64,1,1664]{2,1,0:T(1,128)S(1)} async-done(((f32[64,1,1664]{2,1,0:T(1,128)}), f32[64,1,1664]{2,1,0:T(1,128)S(1)}, u32[]{:S(2)}, u32[]{:S(2)}) %all-to-all-start) | async-done | bytes 426016 | tf_op jit(solution)/shard_map/all_to_all | solution.py:403
  25.9 0.2 pick.1._.mine
  26.1 0.1 collective-permute-start.1
  26.2 1.2 %load.1.head = f32[256,1024]{1,0:T(8,128)S(1)} custom-call(f32[2,512,1024]{2,1,0:T(8,128)} %p_hbm.5, f32[32,128]{1,0:T(8,128)S(1)} %pick.1._.mine), custom_call_target="tpu_custom_call" | custom-call | tf_op jit(solution)/shard_map/load/pallas_call | solution.py:365
  27.4 0.0 collective-permute-done.1.other
  27.4 2.5 %first.1 = (f32[2,512,1024]{2,1,0:T(8,128)S(1)}, f32[24,128]{1,0:T(8,128)S(1)}, f32[36,128]{1,0:T(8,128)S(1)}, s32[8,128]{1,0:T(8,128)S(4)}) custom-call(s32[4]{0:T(128)S(4)} %get-tuple-element.20.own_ids, f32[832,128]{1,0:T(8,128)S(1)} %bitcast.14, f32[32,128]{1,0:T(8,128)S(1)} %pick.1._.mine, f32[32,128]{1,0:T(8,128)S(1)} %collective-permute-done.1.other, ...), custom_call_target="tpu_custom_call" | custom-call | tf_op jit(solution)/shard_map/first/pallas_call | solution.py:365
  30.0 0.6 collective-permute-start.2
  30.6 0.8 %collective-permute-done.2.b = f32[36,128]{1,0:T(8,128)S(1)} collective-permute-done((f32[36,128]{1,0:T(8,128)S(1)}, f32[36,128]{1,0:T(8,128)S(1)}, u32[]{:S(2)}, u32[]{:S(2)}) %collective-permute-start.2) | collective-permute-done | bytes 18464 | tf_op jit(solution)/shard_map/ppermute | solution.py:408
  31.4 1.0 %collective-permute-start.5 = (f32[72,128]{1,0:T(8,128)S(1)}, f32[72,128]{1,0:T(8,128)S(1)}, u32[]{:S(2)}, u32[]{:S(2)}) collective-permute-start(f32[72,128]{1,0:T(8,128)S(1)} %pair.1.rec0), channel_id=1, source_target_pairs={{0,96},{1,97},{2,98},{3,99},{4,100},{5,101},{6,102},{7,103},{8,104... | collective-permute-start | bytes 110600 | tf_op jit(solution)/shard_map/ppermute | solution.py:449
  32.4 1.7 %collective-permute-start.4 = (f32[72,128]{1,0:T(8,128)S(1)}, f32[72,128]{1,0:T(8,128)S(1)}, u32[]{:S(2)}, u32[]{:S(2)}) collective-permute-start(f32[72,128]{1,0:T(8,128)S(1)} %pair.1.rec0), channel_id=1, source_target_pairs={{0,64},{1,65},{2,66},{3,67},{4,68},{5,69},{6,70},{7,71},{8,72},{9,... | collective-permute-start | bytes 110600 | tf_op jit(solution)/shard_map/ppermute | solution.py:449
  34.1 0.0 collective-permute-start.3
  34.1 1.5 %collective-permute-done.5.rec3 = f32[72,128]{1,0:T(8,128)S(1)} collective-permute-done((f32[72,128]{1,0:T(8,128)S(1)}, f32[72,128]{1,0:T(8,128)S(1)}, u32[]{:S(2)}, u32[]{:S(2)}) %collective-permute-start.5) | collective-permute-done | bytes 36896 | tf_op jit(solution)/shard_map/ppermute | solution.py:449
  35.5 2.3 %collective-permute-done.4.rec2 = f32[72,128]{1,0:T(8,128)S(1)} collective-permute-done((f32[72,128]{1,0:T(8,128)S(1)}, f32[72,128]{1,0:T(8,128)S(1)}, u32[]{:S(2)}, u32[]{:S(2)}) %collective-permute-start.4) | collective-permute-done | bytes 36896 | tf_op jit(solution)/shard_map/ppermute | solution.py:449
  37.9 1.4 %collective-permute-done.3.rec1 = f32[72,128]{1,0:T(8,128)S(1)} collective-permute-done((f32[72,128]{1,0:T(8,128)S(1)}, f32[72,128]{1,0:T(8,128)S(1)}, u32[]{:S(2)}, u32[]{:S(2)}) %collective-permute-start.3) | collective-permute-done | bytes 36896 | tf_op jit(solution)/shard_map/ppermute | solution.py:449
  39.2 0.7 users.1
  39.9 12.0 %all_to_all.27 = f32[16,1,4608]{2,1,0:T(1,128)S(1)} all-to-all(f32[16,1,4608]{2,1,0:T(1,128)S(1)} %bitcast.18), channel_id=1, replica_groups={{0,2,4,6,8,10,12,14,16,18,20,22,24,26,28,30},{1,3,5,7,9,11,13,15,17,19,..., dimensions={0} | all-to-all | bytes 589824 | tf_op jit(solution)/shard_map/all_to_all | solution.py:403
  51.9 2.0 %second.1 = (f32[2,512,1024]{2,1,0:T(8,128)}, f32[24,128]{1,0:T(8,128)S(1)}, f32[12,128]{1,0:T(8,128)S(1)}, f32[256,1024]{1,0:T(8,128)S(1)}) custom-call(f32[576,128]{1,0:T(8,128)S(1)} %bitcast.17, f32[2,512,1024]{2,1,0:T(8,128)S(1)} %get-tuple-element.28.base, f32[24,128]{1,0:T(8,128)S(1)} %get-tuple-element.29.psum), custom_call_target="tpu_custom_call" | custom-call | tf_op jit(solution)/shard_map/second/pallas_call | solution.py:365
  53.9 0.1 collective-permute-start.6
  54.0 1.0 %store.1._ = f32[2,512,1024]{2,1,0:T(8,128)} custom-call(f32[256,1024]{1,0:T(8,128)S(1)} %get-tuple-element.30.tail, f32[2,512,1024]{2,1,0:T(8,128)} %get-tuple-element.31._), custom_call_target="tpu_custom_call", output_to_operand_aliasing={{}: (1, {})} | custom-call | tf_op jit(solution)/shard_map/store/pallas_call | solution.py:365
  55.0 0.2 collective-permute-done.6.other
  55.2 0.1 owners.1
  55.3 16.4 %all_to_all.28 = f32[64,1,1536]{2,1,0:T(1,128)S(1)} all-to-all(f32[64,1,1536]{2,1,0:T(1,128)S(1)} %bitcast.16), channel_id=1, replica_groups={{0,2,4,6,8,10,12,14,16,18,20,22,24,26,28,30,32,34,36,38,40,42,44,46,48,..., dimensions={0} | all-to-all | bytes 786432 | tf_op jit(solution)/shard_map/all_to_all | solution.py:403
  71.6 0.6 last.1
  (1 shorter events, 0.0 us)
Async XLA Ops:
  2.2 23.6 %all-to-all-start = ((f32[64,1,1664]{2,1,0:T(1,128)}), f32[64,1,1664]{2,1,0:T(1,128)S(1)}, u32[]{:S(2)}, u32[]{:S(2)}) async-start(f32[64,1,1664]{2,1,0:T(1,128)} %bitcast.4), calls=%async_computation | async-start | bytes 851968 | tf_op jit(solution)/shard_map/all_to_all | solution.py:403
  13.8 5.2 %collective-permute-start = (s32[8,128]{1,0:T(8,128)S(1)}, s32[8,128]{1,0:T(8,128)S(1)}, u32[]{:S(2)}, u32[]{:S(2)}) collective-permute-start(s32[8,128]{1,0:T(8,128)S(1)} %get-tuple-element.22), channel_id=1, source_target_pairs={{0,1},{1,0},{2,3},{3,2},{4,5},{5,4},{6,7},{7,6},{8,9},{9,8},{10,11... | collective-permute-start | bytes 12296 | tf_op jit(solution)/shard_map/ppermute | solution.py:408
  26.1 1.3 %collective-permute-start.1 = (f32[32,128]{1,0:T(8,128)S(1)}, f32[32,128]{1,0:T(8,128)S(1)}, u32[]{:S(2)}, u32[]{:S(2)}) collective-permute-start(f32[32,128]{1,0:T(8,128)S(1)} %pick.1._.mine), channel_id=1, source_target_pairs={{0,1},{1,0},{2,3},{3,2},{4,5},{5,4},{6,7},{7,6},{8,9},{9,8},{10,11... | collective-permute-start | bytes 49160 | tf_op jit(solution)/shard_map/ppermute | solution.py:408
  30.0 1.4 %collective-permute-start.2 = (f32[36,128]{1,0:T(8,128)S(1)}, f32[36,128]{1,0:T(8,128)S(1)}, u32[]{:S(2)}, u32[]{:S(2)}) collective-permute-start(f32[36,128]{1,0:T(8,128)S(1)} %get-tuple-element.27.a), channel_id=1, source_target_pairs={{0,1},{1,0},{2,3},{3,2},{4,5},{5,4},{6,7},{7,6},{8,9},{9,8},{10,11... | collective-permute-start | bytes 55304 | tf_op jit(solution)/shard_map/ppermute | solution.py:408
  31.4 4.1 %collective-permute-start.5 = (f32[72,128]{1,0:T(8,128)S(1)}, f32[72,128]{1,0:T(8,128)S(1)}, u32[]{:S(2)}, u32[]{:S(2)}) collective-permute-start(f32[72,128]{1,0:T(8,128)S(1)} %pair.1.rec0), channel_id=1, source_target_pairs={{0,96},{1,97},{2,98},{3,99},{4,100},{5,101},{6,102},{7,103},{8,104... | collective-permute-start | bytes 110600 | tf_op jit(solution)/shard_map/ppermute | solution.py:449
  32.4 5.5 %collective-permute-start.4 = (f32[72,128]{1,0:T(8,128)S(1)}, f32[72,128]{1,0:T(8,128)S(1)}, u32[]{:S(2)}, u32[]{:S(2)}) collective-permute-start(f32[72,128]{1,0:T(8,128)S(1)} %pair.1.rec0), channel_id=1, source_target_pairs={{0,64},{1,65},{2,66},{3,67},{4,68},{5,69},{6,70},{7,71},{8,72},{9,... | collective-permute-start | bytes 110600 | tf_op jit(solution)/shard_map/ppermute | solution.py:449
  34.1 5.2 %collective-permute-start.3 = (f32[72,128]{1,0:T(8,128)S(1)}, f32[72,128]{1,0:T(8,128)S(1)}, u32[]{:S(2)}, u32[]{:S(2)}) collective-permute-start(f32[72,128]{1,0:T(8,128)S(1)} %pair.1.rec0), channel_id=1, source_target_pairs={{0,32},{1,33},{2,34},{3,35},{4,36},{5,37},{6,38},{7,39},{8,40},{9,... | collective-permute-start | bytes 110600 | tf_op jit(solution)/shard_map/ppermute | solution.py:449
  53.9 1.3 %collective-permute-start.6 = (f32[24,128]{1,0:T(8,128)S(1)}, f32[24,128]{1,0:T(8,128)S(1)}, u32[]{:S(2)}, u32[]{:S(2)}) collective-permute-start(f32[24,128]{1,0:T(8,128)S(1)} %get-tuple-element.32.mine), channel_id=1, source_target_pairs={{0,1},{1,0},{2,3},{3,2},{4,5},{5,4},{6,7},{7,6},{8,9},{9,8},{10,11... | collective-permute-start | bytes 36872 | tf_op jit(solution)/shard_map/ppermute | solution.py:408

commit v7 on v6

--- a/solution.py
+++ b/solution.py
@@ -20,7 +20,8 @@
 RB = 128
 NRB = 4
 BIG = 1e30
-HEAD = 256
+HEAD = 128
+AHEAD = 2
 TAIL = 256
 
 PLANE = 16
@@ -96,12 +97,17 @@
 ZEROS = lambda: (jnp.zeros((8, L), jnp.float32),) * SR
 
 
-def prepare_kernel(own_ids, mask, p_hbm, c_hbm, hc, psum, p_ref, c_ref, r_buf, p_sems, c_sems):
+def prepare_kernel(own_ids, mask, p_hbm, c_hbm, hc, psum, head, p_rest, c_ref, r_buf, p_sems, c_sems):
+    def place(t, b):
+        n = (t * NRB + b) * RB
+        return (head, -t * 512) if n < HEAD else (p_rest, HEAD - t * 512)
+
     def fetch(t, b):
         rows = pl.ds(b * RB, RB)
         n = t * NRB + b
+        p_ref, skip = place(t, b)
         return (
-            pltpu.make_async_copy(p_hbm.at[t, rows, :], p_ref.at[t, rows, :], p_sems.at[n]),
+            pltpu.make_async_copy(p_hbm.at[t, rows, :], p_ref.at[pl.ds(b * RB - skip, RB), :], p_sems.at[n]),
             pltpu.make_async_copy(c_hbm.at[t, rows, :], c_ref.at[t, rows, :], c_sems.at[n]),
         )
 
@@ -112,7 +118,7 @@
     for t in range(2):
         alive = jnp.where(own_ids[t] >= 0, 1, 0)
 
-        def step(g, cols):
+        def step(p_ref, skip, g, cols):
             r0 = pl.multiple_of(g * 16, 16)
             cols = list(cols)
             ps = [[], []]
@@ -122,8 +128,8 @@
                 halves = []
                 for h in range(2):
                     here = jnp.full((8, L), mask[t, cb, g * 2 + h] * alive, jnp.int32) > 0
-                    rows = pl.ds(pl.multiple_of(r0 + 8 * h, 8), 8)
-                    p = jnp.where(here, p_ref[t, rows, lanes], 0.0)
+                    rows = pl.ds(pl.multiple_of(r0 + 8 * h - skip, 8), 8)
+                    p = jnp.where(here, p_ref[rows, lanes], 0.0)
                     halves.append(jnp.where(here, c16[8 * h : 8 * h + 8], BIG))
                     ps[h].append(p)
                     cols[cb] = cols[cb] + p
@@ -136,14 +142,8 @@
         for b in range(NRB):
             for copy in fetch(t, b):
                 copy.wait()
-            cols = lax.fori_loop(b * 8, (b + 1) * 8, step, cols)
+            cols = lax.fori_loop(b * 8, (b + 1) * 8, functools.partial(step, *place(t, b)), cols)
         write_sums(t, psum, r_buf, cols)
-
-
-def load_kernel(p_hbm, _, out, sem):
-    copy = pltpu.make_async_copy(p_hbm.at[0, pl.ds(0, HEAD), :], out, sem)
-    copy.start()
-    copy.wait()
 
 
 def first_tile(t, arow, srow, sources, hc_ref, out, usum, a_buf, r_buf, ready):
@@ -181,11 +181,16 @@
         n = (t * NRB + b) * RB - HEAD
         return pltpu.make_async_copy(p_hbm.at[t, pl.ds(b * RB, RB), :], p_ref.at[pl.ds(n, RB), :], p_sems.at[n // RB])
 
+    first = HEAD // RB
+
     def ready(t, b):
-        if (t * NRB + b) * RB >= HEAD:
+        n = t * NRB + b
+        if first + AHEAD <= n + AHEAD < 2 * NRB:
+            fetch(*divmod(n + AHEAD, NRB)).start()
+        if n >= first:
             fetch(t, b).wait()
 
-    for n in range(HEAD // RB, 2 * NRB):
+    for n in range(first, first + AHEAD):
         fetch(*divmod(n, NRB)).start()
     core = lax.axis_index("tiles") & 1
     id_buf[0:4, :] = mine[TS : TS + 4, :].astype(jnp.int32)
@@ -208,7 +213,27 @@
     out[MSG:, :] = b[...]
 
 
-def users_kernel(ids, rec0, rec1, rec2, rec3, out, rec, acc_a0, acc_a1, acc_s0, acc_s1):
+def flags_kernel(own_ids, mine, other, _, flags):
+    me = lax.axis_index("tiles")
+    core = me & 1
+    lane = lax.broadcasted_iota(jnp.int32, (4, L), 1)
+    row = lax.broadcasted_iota(jnp.int32, (4, L), 0)
+    place = lane * 4 + jnp.where(row < 2, core, 1 - core) * 2 + (row & 1)
+
+    def found(where):
+        return jnp.max(jnp.where(where & (lane < CHIPS), 1, 0))
+
+    for kind in range(2):
+        rows = pl.ds(TS + 2 * kind, 2)
+        ids = jnp.concatenate([mine[rows, :], other[rows, :]], axis=0).astype(jnp.int32)
+        for k in range(2):
+            i = own_ids[2 * kind + k]
+            earlier = found((ids == i) & (place < me * 2 + k))
+            flags[2 * kind + k] = jnp.where((i >= 0) & (earlier == 0), 1, 0)
+        flags[4 + kind] = 1 - found(ids == me)
+
+
+def users_kernel(ids, rec0, rec1, rec2, rec3, _, out, rec, acc_a0, acc_a1, acc_s0, acc_s1):
     me = lax.axis_index("tiles")
     chip = me >> 1
     core = me & 1
@@ -222,10 +247,9 @@
     wanted = []
     for j in range(PLANE):
         there = (x << 4) | j
-        o = j * MSG
-        index = there * 2 + core
-        adv = [(ids[k, there], o + AR * k) for k in range(2)] + [(index, o + TS + SR)]
-        slot = [(ids[2 + k, there], o + 8 + SR * k) for k in range(2)] + [(index, o + TS)]
+        o = j * TS
+        adv = [(ids[k, there], o + AR * k) for k in range(2)]
+        slot = [(ids[2 + k, there], o + 8 + SR * k) for k in range(2)]
         wanted.append((adv, slot))
     zero = jnp.zeros((8, L), jnp.float32)
     for adv, slot in wanted:
@@ -287,7 +311,7 @@
     write_sums(t, usum, r_buf, cols)
 
 
-def second_kernel(rec, base, psum, primal, sums, own, tail, out, usum, a_buf, r_buf, sems):
+def second_kernel(flags, rec, base, psum, primal, sums, tail, out, usum, a_buf, r_buf, sems):
     early = 1024 - TAIL
 
     def keep(t, b):
@@ -298,15 +322,16 @@
         if (t * NRB + b) * RB < early:
             keep(t, b).start()
 
-    total = tree([rec[j * MSG : (j + 1) * MSG, :] for j in range(PLANE)])
-    adv = jnp.maximum(total[0:8] * (1.0 / 1024), 0.0)
-    slot = jnp.maximum(total[8:32] * (1.0 / 512), 0.0)
-    own[0:SR, :] = slot[16:24]
-    own[SR:OUT, :] = jnp.maximum(total[32:36] * (1.0 / 1024), 0.0)
+    total = jnp.maximum(tree([rec[j * TS : (j + 1) * TS, :] for j in range(PLANE)]), 0.0)
+    adv = total[0:8] * (1.0 / 1024)
+    slot = total[8:24] * (1.0 / 512)
     for t in range(2):
         outs = [(out, -t * 512) if t * 512 + b * RB < early else (tail, early - t * 512) for b in range(NRB)]
         second_tile(t, adv[4 * t : 4 * t + 4], slot[8 * t : 8 * t + 8], base, outs, usum, a_buf, r_buf, done)
-    sums[...] = 2.0 * usum[...] - psum[...]
+    for k, (o, n) in enumerate(((0, AR), (AR, AR), (8, SR), (8 + SR, SR))):
+        rows = pl.ds(o, n)
+        named = total[o : o + n] * jnp.where(flags[k] > 0, 1.0, 0.0)
+        sums[rows, :] = named + (2.0 * usum[rows, :] - psum[rows, :])
     for n in range(early // RB):
         keep(*divmod(n, NRB)).wait()
 
@@ -336,13 +361,15 @@
                     out[rows, :] = out[rows, :] + rec[src : src + n, :]
 
 
-def last_kernel(rec, own, bounds, adv_out, slot_out):
+def last_kernel(flags, rec, bias, bounds, adv_out, slot_out):
     n = 2 * OUT
-    parts = [rec[g * n : (g + 1) * n, :] for g in range(CHIPS // 2)]
-    total = tree(parts)
+    total = tree([rec[g * n : (g + 1) * n, :] for g in range(CHIPS // 2)])
     total = total[0:OUT] + total[OUT:n]
-    slot_out[...] = jnp.maximum(own[0:SR, :] + (total[0:SR] - bounds[0:SR, :]) * (1.0 / 512), 0.0)
-    adv_out[...] = jnp.maximum(own[SR:OUT, :] + (total[SR:OUT] - bounds[SR:OUT, :]) * (1.0 / 1024), 0.0)
+    unnamed = jnp.maximum(bias[...], 0.0)
+    slot = total[0:SR] + unnamed[0:SR] * jnp.where(flags[5] > 0, 1.0, 0.0)
+    adv = total[SR:OUT] + unnamed[SR:OUT] * jnp.where(flags[4] > 0, 1.0, 0.0)
+    slot_out[...] = jnp.maximum((slot - bounds[0:SR, :]) * (1.0 / 512), 0.0)
+    adv_out[...] = jnp.maximum((adv - bounds[SR:OUT, :]) * (1.0 / 1024), 0.0)
 
 
 def f32(*shape):
@@ -419,27 +446,21 @@
         + [(pltpu.VMEM((8, L), jnp.int32), IN_VMEM), smem_out(4)],
     )
     table = exchange(message, CORE_GROUPS, OWN)
-    hc, psum = call(
+    hc, psum, head = call(
         prepare_kernel,
         "prepare",
         [smem_arg(own_ids), (in_hbm(mask.transpose(0, 2, 1)), IN_SMEM), hbm_arg(primal_start), hbm_arg(cost)],
-        [(pltpu.VMEM(tile, jnp.bfloat16), IN_VMEM), vmem_out(TS, L)],
-        [vmem(*tile), pltpu.VMEM(tile, jnp.bfloat16), vmem(512, L)] + [pltpu.SemaphoreType.DMA((2 * NRB,))] * 2,
+        [(pltpu.VMEM(tile, jnp.bfloat16), IN_VMEM), vmem_out(TS, L), vmem_out(HEAD, 1024)],
+        [vmem(1024 - HEAD, 1024), pltpu.VMEM(tile, jnp.bfloat16), vmem(512, L)] + [pltpu.SemaphoreType.DMA((2 * NRB,))] * 2,
         8,
     )
     (picked,) = call(pick_kernel, "pick", [vmem_arg(swap(row_ids)), table, vmem_arg(psum)], [vmem_out(SEL, L)])
-    (start,) = call(
-        load_kernel,
-        "load",
-        [hbm_arg(primal_start), vmem_arg(picked)],
-        [vmem_out(HEAD, 1024)],
-        [pltpu.SemaphoreType.DMA(())],
-    )
+    other = swap(picked)
     base, usum, message, ids = call(
         first_kernel,
         "first",
-        [smem_arg(own_ids), table, vmem_arg(picked), vmem_arg(swap(picked)), vmem_arg(bias), vmem_arg(psum), vmem_arg(hc)]
-        + [vmem_arg(start), hbm_arg(primal_start)],
+        [smem_arg(own_ids), table, vmem_arg(picked), vmem_arg(other), vmem_arg(bias), vmem_arg(psum), vmem_arg(hc)]
+        + [vmem_arg(head), hbm_arg(primal_start)],
         [vmem_out(*tile), vmem_out(TS, L), vmem_out(MSG, L), smem_out(8, L)],
         [vmem(1024 - HEAD, 1024), vmem(512, L), vmem(512, L), pltpu.VMEM((8, L), jnp.int32)]
         + [pltpu.SemaphoreType.DMA((2 * NRB - HEAD // RB,)), pltpu.SemaphoreType.DMA(())],
@@ -447,18 +468,24 @@
     )
     (both,) = call(pair_kernel, "pair", [vmem_arg(message), vmem_arg(swap(message))], [vmem_out(2 * MSG, L)])
     parts = [vmem_arg(both)] + [vmem_arg(lax.ppermute(both, "tiles", along_x(d))) for d in range(1, 4)]
+    (flags,) = call(
+        flags_kernel,
+        "flags",
+        [smem_arg(own_ids), vmem_arg(picked), vmem_arg(other), vmem_arg(both)],
+        [smem_out(6)],
+    )
     (message,) = call(
         users_kernel,
         "users",
-        [smem_arg(ids)] + parts,
-        [vmem_out(PLANE * MSG, L)],
+        [smem_arg(ids)] + parts + [smem_arg(flags)],
+        [vmem_out(PLANE * TS, L)],
         [vmem(8 * MSG, L)] + [vmem((BLOCKS + 1) * 8, L)] * 4,
     )
-    primal, sums, own, tail = call(
+    primal, sums, tail = call(
         second_kernel,
         "second",
-        [exchange(message, PLANE_GROUPS, MSG), vmem_arg(base), vmem_arg(usum)],
-        [(f32(*tile), pl.BlockSpec(memory_space=pl.ANY))] + [vmem_out(TS, L), vmem_out(OUT, L), vmem_out(TAIL, 1024)],
+        [smem_arg(flags), exchange(message, PLANE_GROUPS, TS), vmem_arg(base), vmem_arg(usum)],
+        [(f32(*tile), pl.BlockSpec(memory_space=pl.ANY))] + [vmem_out(TS, L), vmem_out(TAIL, 1024)],
         [vmem(1024 - TAIL, 1024), vmem(TS, L), vmem(512, L), vmem(512, L)]
         + [pltpu.SemaphoreType.DMA((2 * NRB - TAIL // RB,))],
         8,
@@ -480,7 +507,7 @@
     adv_out, slot_out = call(
         last_kernel,
         "last",
-        [exchange(message, CORE_GROUPS, OUT), vmem_arg(own), vmem_arg(bounds)],
+        [smem_arg(flags), exchange(message, CORE_GROUPS, OUT), vmem_arg(bias), vmem_arg(bounds)],
         [(f32(AR, L), IN_VMEM), (f32(SR, L), IN_VMEM)],
     )
     return primal, adv_out.reshape(1, 512), slot_out.reshape(1, 1024)

time: 72.6 us -> 73.2 us (level)
  waiting for transfers between devices: 13.1 us -> 14.2 us
    ppermute x4, waiting for transfers between devices: 1.02 us -> 2.37 us  [swap(): return lax.ppermute(x, 'tiles', PARTNERS)]
  transfers between devices with their start and end apart: 8 -> 8, of which waited for: 6 -> 7; matrix products, arithmetic and copies ran while one was open for 0% -> 0% of each run, Pallas kernels for 10% -> 9%
where the time goes in v7:
time: 73.2 us; the launch traced here: 72.7 us
  blocking collectives  27.9 us (38%)
  Pallas kernels  15.3 us (21%)
  starting transfers between devices  14.7 us (20%)
  waiting for transfers between devices  14.2 us (19%)
  between operations  0.74 us (1%)
    all_to_all x2, blocking collectives, exchange(): lax.all_to_all(x.reshape(n, rows * L), 'tiles', 0, 0, axis_index_groups=g...  27.9 us
    pallas_call x11, Pallas kernels, call(): pl.pallas_call(kernel, in_specs=[s for _, s in ins], out_specs=[s for _,...  15.3 us
    all_to_all x1, starting transfers between devices, exchange(): lax.all_to_all(x.reshape(n, rows * L), 'tiles', 0, 0, axis_index_groups=g...  11.5 us
    all_to_all x1, waiting for transfers between devices, exchange(): lax.all_to_all(x.reshape(n, rows * L), 'tiles', 0, 0, axis_index_groups=g...  6.86 us
    ppermute x3, waiting for transfers between devices, body(): lax.ppermute(both, 'tiles', along_x(d))  4.94 us
    ppermute x3, starting transfers between devices, body(): lax.ppermute(both, 'tiles', along_x(d))  2.66 us
    ppermute x4, waiting for transfers between devices, swap(): return lax.ppermute(x, 'tiles', PARTNERS)  2.37 us
  transfers between devices with their start and end apart: 8, of which 7 were waited for; matrix products, arithmetic and copies ran while one was open for 0% of the time, Pallas kernels for 9%

profile of v7, /device:TPU:0, one launch (start us, length us, event | category | flops | bytes accessed | tf_op | source)
XLA Modules:
  0.0 72.7 jit_solution(3824352234947821216)
XLA Ops:
  0.6 1.6 %own.1 = (f32[832,128]{1,0:T(8,128)}, f32[12,128]{1,0:T(8,128)S(1)}, f32[12,128]{1,0:T(8,128)S(1)}, s32[8,128]{1,0:T(8,128)S(1)}, s32[4]{0:T(128)S(4)}) custom-call(s32[2]{0:T(128)} %adv_id.1, s32[2]{0:T(128)} %slot_id.1, f32[4,128]{1,0:T(4,128)} %bitcast.22, f32[8,128]{1,0:T(8,128)} %bitcast.20, f32[4,128]{1,0:T(4,128)} %bitcast.23, f32[8,128]{1,0:T(8,128)} %bitcast.21), custom_call_target="tpu_custom_call" | custom-call | tf_op jit(solution)/shard_map/own/pallas_call | solution.py:392
  2.2 11.5 %all-to-all-start = ((f32[64,1,1664]{2,1,0:T(1,128)}), f32[64,1,1664]{2,1,0:T(1,128)S(1)}, u32[]{:S(2)}, u32[]{:S(2)}) async-start(f32[64,1,1664]{2,1,0:T(1,128)} %bitcast.4), calls=%async_computation | async-start | bytes 851968 | tf_op jit(solution)/shard_map/all_to_all | solution.py:430
  13.8 0.1 collective-permute-start
  13.9 5.1 %prepare.1 = (bf16[2,512,1024]{2,1,0:T(8,128)(2,1)S(1)}, f32[24,128]{1,0:T(8,128)S(1)}, f32[128,1024]{1,0:T(8,128)S(1)}) custom-call(s32[4]{0:T(128)S(4)} %get-tuple-element.20.own_ids, s32[2,8,64]{2,1,0:T(8,128)} %bitcast.19, f32[2,512,1024]{2,1,0:T(8,128)} %p_hbm.3, bf16[2,512,1024]{2,1,0:T(8,128)(2,1)} %c_hbm.1), custom_call_target="tpu_custom_call" | custom-call | tf_op jit(solution)/shard_map/prepare/pallas_call | solution.py:392
  19.0 0.0 collective-permute-done.partner_ids
  19.0 6.9 %all-to-all-done = f32[64,1,1664]{2,1,0:T(1,128)S(1)} async-done(((f32[64,1,1664]{2,1,0:T(1,128)}), f32[64,1,1664]{2,1,0:T(1,128)S(1)}, u32[]{:S(2)}, u32[]{:S(2)}) %all-to-all-start) | async-done | bytes 426016 | tf_op jit(solution)/shard_map/all_to_all | solution.py:430
  25.9 0.2 pick.1.mine
  26.1 0.1 collective-permute-start.1
  26.2 1.2 %collective-permute-done.1.other = f32[32,128]{1,0:T(8,128)S(1)} collective-permute-done((f32[32,128]{1,0:T(8,128)S(1)}, f32[32,128]{1,0:T(8,128)S(1)}, u32[]{:S(2)}, u32[]{:S(2)}) %collective-permute-start.1) | collective-permute-done | bytes 16416 | tf_op jit(solution)/shard_map/ppermute | solution.py:435
  27.4 3.9 %first.1 = (f32[2,512,1024]{2,1,0:T(8,128)S(1)}, f32[24,128]{1,0:T(8,128)S(1)}, f32[36,128]{1,0:T(8,128)S(1)}, s32[8,128]{1,0:T(8,128)S(4)}) custom-call(s32[4]{0:T(128)S(4)} %get-tuple-element.20.own_ids, f32[832,128]{1,0:T(8,128)S(1)} %bitcast.14, f32[32,128]{1,0:T(8,128)S(1)} %pick.1.mine, f32[32,128]{1,0:T(8,128)S(1)} %collective-permute-done.1.other, ...), custom_call_target="tpu_custom_call" | custom-call | tf_op jit(solution)/shard_map/first/pallas_call | solution.py:392
  31.3 0.2 collective-permute-start.2
  31.5 1.0 %collective-permute-done.2.b = f32[36,128]{1,0:T(8,128)S(1)} collective-permute-done((f32[36,128]{1,0:T(8,128)S(1)}, f32[36,128]{1,0:T(8,128)S(1)}, u32[]{:S(2)}, u32[]{:S(2)}) %collective-permute-start.2) | collective-permute-done | bytes 18464 | tf_op jit(solution)/shard_map/ppermute | solution.py:435
  32.6 1.0 %collective-permute-start.5 = (f32[72,128]{1,0:T(8,128)S(1)}, f32[72,128]{1,0:T(8,128)S(1)}, u32[]{:S(2)}, u32[]{:S(2)}) collective-permute-start(f32[72,128]{1,0:T(8,128)S(1)} %pair.1._.rec0), channel_id=1, source_target_pairs={{0,96},{1,97},{2,98},{3,99},{4,100},{5,101},{6,102},{7,103},{8,104... | collective-permute-start | bytes 110600 | tf_op jit(solution)/shard_map/ppermute | solution.py:470
  33.5 1.7 %collective-permute-start.4 = (f32[72,128]{1,0:T(8,128)S(1)}, f32[72,128]{1,0:T(8,128)S(1)}, u32[]{:S(2)}, u32[]{:S(2)}) collective-permute-start(f32[72,128]{1,0:T(8,128)S(1)} %pair.1._.rec0), channel_id=1, source_target_pairs={{0,64},{1,65},{2,66},{3,67},{4,68},{5,69},{6,70},{7,71},{8,72},{9,... | collective-permute-start | bytes 110600 | tf_op jit(solution)/shard_map/ppermute | solution.py:470
  35.2 0.0 collective-permute-start.3
  35.2 0.2 flags.1._
  35.5 1.1 %collective-permute-done.5.rec3 = f32[72,128]{1,0:T(8,128)S(1)} collective-permute-done((f32[72,128]{1,0:T(8,128)S(1)}, f32[72,128]{1,0:T(8,128)S(1)}, u32[]{:S(2)}, u32[]{:S(2)}) %collective-permute-start.5) | collective-permute-done | bytes 36896 | tf_op jit(solution)/shard_map/ppermute | solution.py:470
  36.5 2.6 %collective-permute-done.4.rec2 = f32[72,128]{1,0:T(8,128)S(1)} collective-permute-done((f32[72,128]{1,0:T(8,128)S(1)}, f32[72,128]{1,0:T(8,128)S(1)}, u32[]{:S(2)}, u32[]{:S(2)}) %collective-permute-start.4) | collective-permute-done | bytes 36896 | tf_op jit(solution)/shard_map/ppermute | solution.py:470
  39.1 1.3 %collective-permute-done.3.rec1 = f32[72,128]{1,0:T(8,128)S(1)} collective-permute-done((f32[72,128]{1,0:T(8,128)S(1)}, f32[72,128]{1,0:T(8,128)S(1)}, u32[]{:S(2)}, u32[]{:S(2)}) %collective-permute-start.3) | collective-permute-done | bytes 36896 | tf_op jit(solution)/shard_map/ppermute | solution.py:470
  40.4 0.5 users.1
  40.9 11.5 %all_to_all.27 = f32[16,1,3072]{2,1,0:T(1,128)S(1)} all-to-all(f32[16,1,3072]{2,1,0:T(1,128)S(1)} %bitcast.17), channel_id=1, replica_groups={{0,2,4,6,8,10,12,14,16,18,20,22,24,26,28,30},{1,3,5,7,9,11,13,15,17,19,..., dimensions={0} | all-to-all | bytes 393216 | tf_op jit(solution)/shard_map/all_to_all | solution.py:430
  52.4 2.0 %second.1 = (f32[2,512,1024]{2,1,0:T(8,128)}, f32[24,128]{1,0:T(8,128)S(1)}, f32[256,1024]{1,0:T(8,128)S(1)}) custom-call(s32[6]{0:T(128)S(4)} %flags.1._, f32[384,128]{1,0:T(8,128)S(1)} %bitcast.18, f32[2,512,1024]{2,1,0:T(8,128)S(1)} %get-tuple-element.29.base, f32[24,128]{1,0:T(8,128)S(1)} %get-tuple-element.30.psum), custom_call_target="tpu_custom_call" | custom-call | tf_op jit(solution)/shard_map/second/pallas_call | solution.py:392
  54.4 0.1 collective-permute-start.6
  54.5 1.0 %store.1._ = f32[2,512,1024]{2,1,0:T(8,128)} custom-call(f32[256,1024]{1,0:T(8,128)S(1)} %get-tuple-element.31.tail, f32[2,512,1024]{2,1,0:T(8,128)} %get-tuple-element.32._), custom_call_target="tpu_custom_call", output_to_operand_aliasing={{}: (1, {})} | custom-call | tf_op jit(solution)/shard_map/store/pallas_call | solution.py:392
  55.5 0.2 collective-permute-done.6.other
  55.7 0.1 owners.1
  55.8 16.4 %all_to_all.28 = f32[64,1,1536]{2,1,0:T(1,128)S(1)} all-to-all(f32[64,1,1536]{2,1,0:T(1,128)S(1)} %bitcast.16), channel_id=1, replica_groups={{0,2,4,6,8,10,12,14,16,18,20,22,24,26,28,30,32,34,36,38,40,42,44,46,48,..., dimensions={0} | all-to-all | bytes 786432 | tf_op jit(solution)/shard_map/all_to_all | solution.py:430
  72.1 0.6 last.1
  (1 shorter events, 0.0 us)
Async XLA Ops:
  2.2 23.6 %all-to-all-start = ((f32[64,1,1664]{2,1,0:T(1,128)}), f32[64,1,1664]{2,1,0:T(1,128)S(1)}, u32[]{:S(2)}, u32[]{:S(2)}) async-start(f32[64,1,1664]{2,1,0:T(1,128)} %bitcast.4), calls=%async_computation | async-start | bytes 851968 | tf_op jit(solution)/shard_map/all_to_all | solution.py:430
  13.8 5.2 %collective-permute-start = (s32[8,128]{1,0:T(8,128)S(1)}, s32[8,128]{1,0:T(8,128)S(1)}, u32[]{:S(2)}, u32[]{:S(2)}) collective-permute-start(s32[8,128]{1,0:T(8,128)S(1)} %get-tuple-element.21), channel_id=1, source_target_pairs={{0,1},{1,0},{2,3},{3,2},{4,5},{5,4},{6,7},{7,6},{8,9},{9,8},{10,11... | collective-permute-start | bytes 12296 | tf_op jit(solution)/shard_map/ppermute | solution.py:435
  26.1 1.3 %collective-permute-start.1 = (f32[32,128]{1,0:T(8,128)S(1)}, f32[32,128]{1,0:T(8,128)S(1)}, u32[]{:S(2)}, u32[]{:S(2)}) collective-permute-start(f32[32,128]{1,0:T(8,128)S(1)} %pick.1.mine), channel_id=1, source_target_pairs={{0,1},{1,0},{2,3},{3,2},{4,5},{5,4},{6,7},{7,6},{8,9},{9,8},{10,11... | collective-permute-start | bytes 49160 | tf_op jit(solution)/shard_map/ppermute | solution.py:435
  31.3 1.3 %collective-permute-start.2 = (f32[36,128]{1,0:T(8,128)S(1)}, f32[36,128]{1,0:T(8,128)S(1)}, u32[]{:S(2)}, u32[]{:S(2)}) collective-permute-start(f32[36,128]{1,0:T(8,128)S(1)} %get-tuple-element.27.a), channel_id=1, source_target_pairs={{0,1},{1,0},{2,3},{3,2},{4,5},{5,4},{6,7},{7,6},{8,9},{9,8},{10,11... | collective-permute-start | bytes 55304 | tf_op jit(solution)/shard_map/ppermute | solution.py:435
  32.6 4.0 %collective-permute-start.5 = (f32[72,128]{1,0:T(8,128)S(1)}, f32[72,128]{1,0:T(8,128)S(1)}, u32[]{:S(2)}, u32[]{:S(2)}) collective-permute-start(f32[72,128]{1,0:T(8,128)S(1)} %pair.1._.rec0), channel_id=1, source_target_pairs={{0,96},{1,97},{2,98},{3,99},{4,100},{5,101},{6,102},{7,103},{8,104... | collective-permute-start | bytes 110600 | tf_op jit(solution)/shard_map/ppermute | solution.py:470
  33.5 5.6 %collective-permute-start.4 = (f32[72,128]{1,0:T(8,128)S(1)}, f32[72,128]{1,0:T(8,128)S(1)}, u32[]{:S(2)}, u32[]{:S(2)}) collective-permute-start(f32[72,128]{1,0:T(8,128)S(1)} %pair.1._.rec0), channel_id=1, source_target_pairs={{0,64},{1,65},{2,66},{3,67},{4,68},{5,69},{6,70},{7,71},{8,72},{9,... | collective-permute-start | bytes 110600 | tf_op jit(solution)/shard_map/ppermute | solution.py:470
  35.2 5.2 %collective-permute-start.3 = (f32[72,128]{1,0:T(8,128)S(1)}, f32[72,128]{1,0:T(8,128)S(1)}, u32[]{:S(2)}, u32[]{:S(2)}) collective-permute-start(f32[72,128]{1,0:T(8,128)S(1)} %pair.1._.rec0), channel_id=1, source_target_pairs={{0,32},{1,33},{2,34},{3,35},{4,36},{5,37},{6,38},{7,39},{8,40},{9,... | collective-permute-start | bytes 110600 | tf_op jit(solution)/shard_map/ppermute | solution.py:470
  54.4 1.3 %collective-permute-start.6 = (f32[24,128]{1,0:T(8,128)S(1)}, f32[24,128]{1,0:T(8,128)S(1)}, u32[]{:S(2)}, u32[]{:S(2)}) collective-permute-start(f32[24,128]{1,0:T(8,128)S(1)} %get-tuple-element.33.mine), channel_id=1, source_target_pairs={{0,1},{1,0},{2,3},{3,2},{4,5},{5,4},{6,7},{7,6},{8,9},{9,8},{10,11... | collective-permute-start | bytes 36872 | tf_op jit(solution)/shard_map/ppermute | solution.py:435

commit v8 on v7

--- a/solution.py
+++ b/solution.py
@@ -21,7 +21,6 @@
 NRB = 4
 BIG = 1e30
 HEAD = 128
-AHEAD = 2
 TAIL = 256
 
 PLANE = 16
@@ -146,6 +145,12 @@
         write_sums(t, psum, r_buf, cols)
 
 
+def load_kernel(p_hbm, _, out, sem):
+    copy = pltpu.make_async_copy(p_hbm.at[0, pl.ds(HEAD, 512 - HEAD), :], out, sem)
+    copy.start()
+    copy.wait()
+
+
 def first_tile(t, arow, srow, sources, hc_ref, out, usum, a_buf, r_buf, ready):
     spread_half(arow, a_buf)
     s = slot_rows(srow)
@@ -176,22 +181,17 @@
     write_sums(t, usum, r_buf, cols)
 
 
-def first_kernel(own_ids, rec, mine, other, bias, psum, hc_ref, head, p_hbm, out, usum, msg, ids, p_ref, a_buf, r_buf, id_buf, p_sems, sem):
-    def fetch(t, b):
-        n = (t * NRB + b) * RB - HEAD
-        return pltpu.make_async_copy(p_hbm.at[t, pl.ds(b * RB, RB), :], p_ref.at[pl.ds(n, RB), :], p_sems.at[n // RB])
-
-    first = HEAD // RB
+def first_kernel(own_ids, rec, mine, other, bias, psum, hc_ref, head, rest, p_hbm, out, usum, msg, ids, p_ref, a_buf, r_buf, id_buf, p_sems, sem):
+    def fetch(b):
+        rows = pl.ds(b * RB, RB)
+        return pltpu.make_async_copy(p_hbm.at[1, rows, :], p_ref.at[rows, :], p_sems.at[b])
 
     def ready(t, b):
-        n = t * NRB + b
-        if first + AHEAD <= n + AHEAD < 2 * NRB:
-            fetch(*divmod(n + AHEAD, NRB)).start()
-        if n >= first:
-            fetch(t, b).wait()
-
-    for n in range(first, first + AHEAD):
-        fetch(*divmod(n, NRB)).start()
+        if t == 1:
+            fetch(b).wait()
+
+    for b in range(NRB):
+        fetch(b).start()
     core = lax.axis_index("tiles") & 1
     id_buf[0:4, :] = mine[TS : TS + 4, :].astype(jnp.int32)
     id_buf[4:8, :] = other[TS : TS + 4, :].astype(jnp.int32)
@@ -201,7 +201,7 @@
         a, s = own_ids[t], own_ids[2 + t]
         arow = jnp.where((a & 1) == core, rows_of(rec, a, False), other[AR * t : AR * (t + 1), :])
         srow = jnp.where((s & 1) == core, rows_of(rec, s, True), other[8 + SR * t : 8 + SR * (t + 1), :])
-        sources = [(head, 0) if t * 512 + b * RB < HEAD else (p_ref, HEAD - t * 512) for b in range(NRB)]
+        sources = [(p_ref, 0) if t else (head, 0) if b * RB < HEAD else (rest, HEAD) for b in range(NRB)]
         first_tile(t, arow, srow, sources, hc_ref, out, usum, a_buf, r_buf, functools.partial(ready, t))
     msg[0:TS, :] = 2.0 * usum[...] - psum[...]
     msg[TS:MSG, :] = bias[...]
@@ -456,14 +456,21 @@
     )
     (picked,) = call(pick_kernel, "pick", [vmem_arg(swap(row_ids)), table, vmem_arg(psum)], [vmem_out(SEL, L)])
     other = swap(picked)
+    (rest,) = call(
+        load_kernel,
+        "load",
+        [hbm_arg(primal_start), vmem_arg(picked)],
+        [vmem_out(512 - HEAD, 1024)],
+        [pltpu.SemaphoreType.DMA(())],
+    )
     base, usum, message, ids = call(
         first_kernel,
         "first",
         [smem_arg(own_ids), table, vmem_arg(picked), vmem_arg(other), vmem_arg(bias), vmem_arg(psum), vmem_arg(hc)]
-        + [vmem_arg(head), hbm_arg(primal_start)],
+        + [vmem_arg(head), vmem_arg(rest), hbm_arg(primal_start)],
         [vmem_out(*tile), vmem_out(TS, L), vmem_out(MSG, L), smem_out(8, L)],
-        [vmem(1024 - HEAD, 1024), vmem(512, L), vmem(512, L), pltpu.VMEM((8, L), jnp.int32)]
-        + [pltpu.SemaphoreType.DMA((2 * NRB - HEAD // RB,)), pltpu.SemaphoreType.DMA(())],
+        [vmem(512, 1024), vmem(512, L), vmem(512, L), pltpu.VMEM((8, L), jnp.int32)]
+        + [pltpu.SemaphoreType.DMA((NRB,)), pltpu.SemaphoreType.DMA(())],
         8,
     )
     (both,) = call(pair_kernel, "pair", [vmem_arg(message), vmem_arg(swap(message))], [vmem_out(2 * MSG, L)])

time: 73.2 us -> 71.6 us (0.978)
  waiting for transfers between devices: 14.2 us -> 12.8 us
    ppermute x4, waiting for transfers between devices: 2.37 us -> 1.02 us  [swap(): return lax.ppermute(x, 'tiles', PARTNERS)]
    pallas_call x11 -> x12, Pallas kernels: 15.3 us -> 14.8 us  [call(): pl.pallas_call(kernel, in_specs=[s for _, s in ins], out_specs=[s for _,...]
  transfers between devices with their start and end apart: 8 -> 8, of which waited for: 7 -> 6; matrix products, arithmetic and copies ran while one was open for 0% -> 0% of each run, Pallas kernels for 9% -> 11%
where the time goes in v8:
time: 71.6 us; the launch traced here: 71.2 us
  blocking collectives  27.9 us (39%)
  starting transfers between devices  15 us (21%)
  Pallas kernels  14.8 us (21%)
  waiting for transfers between devices  12.8 us (18%)
  between operations  0.76 us (1%)
    all_to_all x2, blocking collectives, exchange(): lax.all_to_all(x.reshape(n, rows * L), 'tiles', 0, 0, axis_index_groups=g...  27.9 us
    pallas_call x12, Pallas kernels, call(): pl.pallas_call(kernel, in_specs=[s for _, s in ins], out_specs=[s for _,...  14.8 us
    all_to_all x1, starting transfers between devices, exchange(): lax.all_to_all(x.reshape(n, rows * L), 'tiles', 0, 0, axis_index_groups=g...  11.5 us
    all_to_all x1, waiting for transfers between devices, exchange(): lax.all_to_all(x.reshape(n, rows * L), 'tiles', 0, 0, axis_index_groups=g...  6.86 us
    ppermute x3, waiting for transfers between devices, body(): lax.ppermute(both, 'tiles', along_x(d))  4.94 us
    ppermute x3, starting transfers between devices, body(): lax.ppermute(both, 'tiles', along_x(d))  2.66 us
  transfers between devices with their start and end apart: 8, of which 6 were waited for; matrix products, arithmetic and copies ran while one was open for 0% of the time, Pallas kernels for 11%

profile of v8, /device:TPU:0, one launch (start us, length us, event | category | flops | bytes accessed | tf_op | source)
XLA Modules:
  0.0 71.2 jit_solution(5559018669905614504)
XLA Ops:
  0.6 1.6 %own.1 = (f32[832,128]{1,0:T(8,128)}, f32[12,128]{1,0:T(8,128)S(1)}, f32[12,128]{1,0:T(8,128)S(1)}, s32[8,128]{1,0:T(8,128)S(1)}, s32[4]{0:T(128)S(4)}) custom-call(s32[2]{0:T(128)} %adv_id.1, s32[2]{0:T(128)} %slot_id.1, f32[4,128]{1,0:T(4,128)} %bitcast.22, f32[8,128]{1,0:T(8,128)} %bitcast.20, f32[4,128]{1,0:T(4,128)} %bitcast.23, f32[8,128]{1,0:T(8,128)} %bitcast.21), custom_call_target="tpu_custom_call" | custom-call | tf_op jit(solution)/shard_map/own/pallas_call | solution.py:392
  2.2 11.5 %all-to-all-start = ((f32[64,1,1664]{2,1,0:T(1,128)}), f32[64,1,1664]{2,1,0:T(1,128)S(1)}, u32[]{:S(2)}, u32[]{:S(2)}) async-start(f32[64,1,1664]{2,1,0:T(1,128)} %bitcast.4), calls=%async_computation | async-start | bytes 851968 | tf_op jit(solution)/shard_map/all_to_all | solution.py:430
  13.8 0.1 collective-permute-start
  13.9 5.1 %prepare.1 = (bf16[2,512,1024]{2,1,0:T(8,128)(2,1)S(1)}, f32[24,128]{1,0:T(8,128)S(1)}, f32[128,1024]{1,0:T(8,128)S(1)}) custom-call(s32[4]{0:T(128)S(4)} %get-tuple-element.20.own_ids, s32[2,8,64]{2,1,0:T(8,128)} %bitcast.19, f32[2,512,1024]{2,1,0:T(8,128)} %p_hbm.5, bf16[2,512,1024]{2,1,0:T(8,128)(2,1)} %c_hbm.1), custom_call_target="tpu_custom_call" | custom-call | tf_op jit(solution)/shard_map/prepare/pallas_call | solution.py:392
  19.0 0.0 collective-permute-done.partner_ids
  19.0 6.9 %all-to-all-done = f32[64,1,1664]{2,1,0:T(1,128)S(1)} async-done(((f32[64,1,1664]{2,1,0:T(1,128)}), f32[64,1,1664]{2,1,0:T(1,128)S(1)}, u32[]{:S(2)}, u32[]{:S(2)}) %all-to-all-start) | async-done | bytes 426016 | tf_op jit(solution)/shard_map/all_to_all | solution.py:430
  25.9 0.2 pick.1._.mine
  26.1 0.1 collective-permute-start.1
  26.2 1.4 %load.1.rest = f32[384,1024]{1,0:T(8,128)S(1)} custom-call(f32[2,512,1024]{2,1,0:T(8,128)} %p_hbm.5, f32[32,128]{1,0:T(8,128)S(1)} %pick.1._.mine), custom_call_target="tpu_custom_call" | custom-call | tf_op jit(solution)/shard_map/load/pallas_call | solution.py:392
  27.6 0.0 collective-permute-done.1.other
  27.6 2.0 %first.1 = (f32[2,512,1024]{2,1,0:T(8,128)S(1)}, f32[24,128]{1,0:T(8,128)S(1)}, f32[36,128]{1,0:T(8,128)S(1)}, s32[8,128]{1,0:T(8,128)S(4)}) custom-call(s32[4]{0:T(128)S(4)} %get-tuple-element.20.own_ids, f32[832,128]{1,0:T(8,128)S(1)} %bitcast.14, f32[32,128]{1,0:T(8,128)S(1)} %pick.1._.mine, f32[32,128]{1,0:T(8,128)S(1)} %collective-permute-done.1.other, ...), custom_call_target="tpu_custom_call" | custom-call | tf_op jit(solution)/shard_map/first/pallas_call | solution.py:392
  29.6 0.6 collective-permute-start.2
  30.2 0.8 %collective-permute-done.2.b = f32[36,128]{1,0:T(8,128)S(1)} collective-permute-done((f32[36,128]{1,0:T(8,128)S(1)}, f32[36,128]{1,0:T(8,128)S(1)}, u32[]{:S(2)}, u32[]{:S(2)}) %collective-permute-start.2) | collective-permute-done | bytes 18464 | tf_op jit(solution)/shard_map/ppermute | solution.py:435
  31.1 1.0 %collective-permute-start.5 = (f32[72,128]{1,0:T(8,128)S(1)}, f32[72,128]{1,0:T(8,128)S(1)}, u32[]{:S(2)}, u32[]{:S(2)}) collective-permute-start(f32[72,128]{1,0:T(8,128)S(1)} %pair.1._.rec0), channel_id=1, source_target_pairs={{0,96},{1,97},{2,98},{3,99},{4,100},{5,101},{6,102},{7,103},{8,104... | collective-permute-start | bytes 110600 | tf_op jit(solution)/shard_map/ppermute | solution.py:477
  32.0 1.7 %collective-permute-start.4 = (f32[72,128]{1,0:T(8,128)S(1)}, f32[72,128]{1,0:T(8,128)S(1)}, u32[]{:S(2)}, u32[]{:S(2)}) collective-permute-start(f32[72,128]{1,0:T(8,128)S(1)} %pair.1._.rec0), channel_id=1, source_target_pairs={{0,64},{1,65},{2,66},{3,67},{4,68},{5,69},{6,70},{7,71},{8,72},{9,... | collective-permute-start | bytes 110600 | tf_op jit(solution)/shard_map/ppermute | solution.py:477
  33.7 0.0 collective-permute-start.3
  33.7 0.2 flags.1._
  33.9 1.2 %collective-permute-done.5.rec3 = f32[72,128]{1,0:T(8,128)S(1)} collective-permute-done((f32[72,128]{1,0:T(8,128)S(1)}, f32[72,128]{1,0:T(8,128)S(1)}, u32[]{:S(2)}, u32[]{:S(2)}) %collective-permute-start.5) | collective-permute-done | bytes 36896 | tf_op jit(solution)/shard_map/ppermute | solution.py:477
  35.2 2.3 %collective-permute-done.4.rec2 = f32[72,128]{1,0:T(8,128)S(1)} collective-permute-done((f32[72,128]{1,0:T(8,128)S(1)}, f32[72,128]{1,0:T(8,128)S(1)}, u32[]{:S(2)}, u32[]{:S(2)}) %collective-permute-start.4) | collective-permute-done | bytes 36896 | tf_op jit(solution)/shard_map/ppermute | solution.py:477
  37.5 1.4 %collective-permute-done.3.rec1 = f32[72,128]{1,0:T(8,128)S(1)} collective-permute-done((f32[72,128]{1,0:T(8,128)S(1)}, f32[72,128]{1,0:T(8,128)S(1)}, u32[]{:S(2)}, u32[]{:S(2)}) %collective-permute-start.3) | collective-permute-done | bytes 36896 | tf_op jit(solution)/shard_map/ppermute | solution.py:477
  38.9 0.5 users.1
  39.4 11.5 %all_to_all.27 = f32[16,1,3072]{2,1,0:T(1,128)S(1)} all-to-all(f32[16,1,3072]{2,1,0:T(1,128)S(1)} %bitcast.17), channel_id=1, replica_groups={{0,2,4,6,8,10,12,14,16,18,20,22,24,26,28,30},{1,3,5,7,9,11,13,15,17,19,..., dimensions={0} | all-to-all | bytes 393216 | tf_op jit(solution)/shard_map/all_to_all | solution.py:430
  50.9 2.0 %second.1 = (f32[2,512,1024]{2,1,0:T(8,128)}, f32[24,128]{1,0:T(8,128)S(1)}, f32[256,1024]{1,0:T(8,128)S(1)}) custom-call(s32[6]{0:T(128)S(4)} %flags.1._, f32[384,128]{1,0:T(8,128)S(1)} %bitcast.18, f32[2,512,1024]{2,1,0:T(8,128)S(1)} %get-tuple-element.29.base, f32[24,128]{1,0:T(8,128)S(1)} %get-tuple-element.30.psum), custom_call_target="tpu_custom_call" | custom-call | tf_op jit(solution)/shard_map/second/pallas_call | solution.py:392
  52.9 0.1 collective-permute-start.6
  53.0 1.0 %store.1._ = f32[2,512,1024]{2,1,0:T(8,128)} custom-call(f32[256,1024]{1,0:T(8,128)S(1)} %get-tuple-element.31.tail, f32[2,512,1024]{2,1,0:T(8,128)} %get-tuple-element.32._), custom_call_target="tpu_custom_call", output_to_operand_aliasing={{}: (1, {})} | custom-call | tf_op jit(solution)/shard_map/store/pallas_call | solution.py:392
  54.0 0.2 collective-permute-done.6.other
  54.1 0.1 owners.1
  54.2 16.4 %all_to_all.28 = f32[64,1,1536]{2,1,0:T(1,128)S(1)} all-to-all(f32[64,1,1536]{2,1,0:T(1,128)S(1)} %bitcast.16), channel_id=1, replica_groups={{0,2,4,6,8,10,12,14,16,18,20,22,24,26,28,30,32,34,36,38,40,42,44,46,48,..., dimensions={0} | all-to-all | bytes 786432 | tf_op jit(solution)/shard_map/all_to_all | solution.py:430
  70.6 0.6 last.1
  (1 shorter events, 0.0 us)
Async XLA Ops:
  2.2 23.6 %all-to-all-start = ((f32[64,1,1664]{2,1,0:T(1,128)}), f32[64,1,1664]{2,1,0:T(1,128)S(1)}, u32[]{:S(2)}, u32[]{:S(2)}) async-start(f32[64,1,1664]{2,1,0:T(1,128)} %bitcast.4), calls=%async_computation | async-start | bytes 851968 | tf_op jit(solution)/shard_map/all_to_all | solution.py:430
  13.8 5.2 %collective-permute-start = (s32[8,128]{1,0:T(8,128)S(1)}, s32[8,128]{1,0:T(8,128)S(1)}, u32[]{:S(2)}, u32[]{:S(2)}) collective-permute-start(s32[8,128]{1,0:T(8,128)S(1)} %get-tuple-element.21), channel_id=1, source_target_pairs={{0,1},{1,0},{2,3},{3,2},{4,5},{5,4},{6,7},{7,6},{8,9},{9,8},{10,11... | collective-permute-start | bytes 12296 | tf_op jit(solution)/shard_map/ppermute | solution.py:435
  26.1 1.5 %collective-permute-start.1 = (f32[32,128]{1,0:T(8,128)S(1)}, f32[32,128]{1,0:T(8,128)S(1)}, u32[]{:S(2)}, u32[]{:S(2)}) collective-permute-start(f32[32,128]{1,0:T(8,128)S(1)} %pick.1._.mine), channel_id=1, source_target_pairs={{0,1},{1,0},{2,3},{3,2},{4,5},{5,4},{6,7},{7,6},{8,9},{9,8},{10,11... | collective-permute-start | bytes 49160 | tf_op jit(solution)/shard_map/ppermute | solution.py:435
  29.6 1.4 %collective-permute-start.2 = (f32[36,128]{1,0:T(8,128)S(1)}, f32[36,128]{1,0:T(8,128)S(1)}, u32[]{:S(2)}, u32[]{:S(2)}) collective-permute-start(f32[36,128]{1,0:T(8,128)S(1)} %get-tuple-element.27.a), channel_id=1, source_target_pairs={{0,1},{1,0},{2,3},{3,2},{4,5},{5,4},{6,7},{7,6},{8,9},{9,8},{10,11... | collective-permute-start | bytes 55304 | tf_op jit(solution)/shard_map/ppermute | solution.py:435
  31.1 4.1 %collective-permute-start.5 = (f32[72,128]{1,0:T(8,128)S(1)}, f32[72,128]{1,0:T(8,128)S(1)}, u32[]{:S(2)}, u32[]{:S(2)}) collective-permute-start(f32[72,128]{1,0:T(8,128)S(1)} %pair.1._.rec0), channel_id=1, source_target_pairs={{0,96},{1,97},{2,98},{3,99},{4,100},{5,101},{6,102},{7,103},{8,104... | collective-permute-start | bytes 110600 | tf_op jit(solution)/shard_map/ppermute | solution.py:477
  32.0 5.5 %collective-permute-start.4 = (f32[72,128]{1,0:T(8,128)S(1)}, f32[72,128]{1,0:T(8,128)S(1)}, u32[]{:S(2)}, u32[]{:S(2)}) collective-permute-start(f32[72,128]{1,0:T(8,128)S(1)} %pair.1._.rec0), channel_id=1, source_target_pairs={{0,64},{1,65},{2,66},{3,67},{4,68},{5,69},{6,70},{7,71},{8,72},{9,... | collective-permute-start | bytes 110600 | tf_op jit(solution)/shard_map/ppermute | solution.py:477
  33.7 5.2 %collective-permute-start.3 = (f32[72,128]{1,0:T(8,128)S(1)}, f32[72,128]{1,0:T(8,128)S(1)}, u32[]{:S(2)}, u32[]{:S(2)}) collective-permute-start(f32[72,128]{1,0:T(8,128)S(1)} %pair.1._.rec0), channel_id=1, source_target_pairs={{0,32},{1,33},{2,34},{3,35},{4,36},{5,37},{6,38},{7,39},{8,40},{9,... | collective-permute-start | bytes 110600 | tf_op jit(solution)/shard_map/ppermute | solution.py:477
  52.9 1.3 %collective-permute-start.6 = (f32[24,128]{1,0:T(8,128)S(1)}, f32[24,128]{1,0:T(8,128)S(1)}, u32[]{:S(2)}, u32[]{:S(2)}) collective-permute-start(f32[24,128]{1,0:T(8,128)S(1)} %get-tuple-element.33.mine), channel_id=1, source_target_pairs={{0,1},{1,0},{2,3},{3,2},{4,5},{5,4},{6,7},{7,6},{8,9},{9,8},{10,11... | collective-permute-start | bytes 36872 | tf_op jit(solution)/shard_map/ppermute | solution.py:435

commit v9 on v8

--- a/solution.py
+++ b/solution.py
@@ -70,9 +70,9 @@
     out[TS:SEL, :] = jnp.concatenate([ids, ids], axis=0).T[0:8, :]
 
 
-def spread_half(row, buf):
-    for b in range(NRB):
-        block = jnp.broadcast_to(0.5 * row[b : b + 1, :], (L, L))
+def spread_half(rows, buf):
+    for b in range(rows.shape[0]):
+        block = jnp.broadcast_to(0.5 * rows[b : b + 1, :], (L, L))
         buf[b * L : (b + 1) * L, :] = block.T
 
 
@@ -82,9 +82,13 @@
     return xs[0]
 
 
-def write_sums(t, sums, r_buf, cols):
-    for b in range(NRB):
-        sums[t * AR + b : t * AR + b + 1, :] = jnp.sum(r_buf[b * L : (b + 1) * L, :].T, axis=0, keepdims=True)
+def write_rows(sums, r_buf, tiles=(0, 1)):
+    for n in range(len(tiles) * NRB):
+        o = tiles[0] * AR + n
+        sums[o : o + 1, :] = jnp.sum(r_buf[n * L : (n + 1) * L, :].T, axis=0, keepdims=True)
+
+
+def write_cols(t, sums, cols):
     rows = [jnp.sum(c, axis=0, keepdims=True) for c in cols]
     sums[8 + t * SR : 8 + (t + 1) * SR, :] = jnp.concatenate(rows, axis=0)
 
@@ -142,7 +146,8 @@
             for copy in fetch(t, b):
                 copy.wait()
             cols = lax.fori_loop(b * 8, (b + 1) * 8, functools.partial(step, *place(t, b)), cols)
-        write_sums(t, psum, r_buf, cols)
+        write_rows(psum, r_buf, (t,))
+        write_cols(t, psum, cols)
 
 
 def load_kernel(p_hbm, _, out, sem):
@@ -151,34 +156,32 @@
     copy.wait()
 
 
-def first_tile(t, arow, srow, sources, hc_ref, out, usum, a_buf, r_buf, ready):
-    spread_half(arow, a_buf)
+def first_tile(t, srow, sources, hc_ref, out, usum, a_buf, r_buf, ready):
     s = slot_rows(srow)
 
     def step(p_ref, skip, g, cols):
         cols = list(cols)
         us = [[], []]
         r0 = pl.multiple_of(g * 16, 16)
-        a = [a_buf[pl.ds(pl.multiple_of(r0 + 8 * h, 8), 8), :] for h in range(2)]
+        a = [a_buf[pl.ds(pl.multiple_of(t * 512 + r0 + 8 * h, 8), 8), :] for h in range(2)]
         for cb in range(SR):
             lanes = pl.ds(cb * L, L)
             c16 = hc_ref[t, pl.ds(r0, 16), lanes].astype(jnp.float32)
             for h in range(2):
-                rows = pl.ds(pl.multiple_of(r0 + 8 * h, 8), 8)
-                hc = c16[8 * h : 8 * h + 8]
-                u = jnp.minimum(jnp.maximum(((p_ref[pl.ds(pl.multiple_of(r0 + 8 * h - skip, 8), 8), lanes] - hc) - a[h]) - s[cb], 0.0), 1.0)
-                out[t, rows, lanes] = u - hc
+                p = p_ref[pl.ds(pl.multiple_of(r0 + 8 * h - skip, 8), 8), lanes]
+                u = jnp.minimum(jnp.maximum(((p - c16[8 * h : 8 * h + 8]) - a[h]) - s[cb], 0.0), 1.0)
+                out[t, pl.ds(pl.multiple_of(r0 + 8 * h, 8), 8), lanes] = u
                 us[h].append(u)
                 cols[cb] = cols[cb] + u
         for h in range(2):
-            r_buf[pl.ds(pl.multiple_of(r0 + 8 * h, 8), 8), :] = tree(us[h])
+            r_buf[pl.ds(pl.multiple_of(t * 512 + r0 + 8 * h, 8), 8), :] = tree(us[h])
         return tuple(cols)
 
     cols = ZEROS()
     for b in range(NRB):
-        ready(b)
+        ready(t, b)
         cols = lax.fori_loop(b * 8, (b + 1) * 8, functools.partial(step, *sources[b]), cols, unroll=2)
-    write_sums(t, usum, r_buf, cols)
+    write_cols(t, usum, cols)
 
 
 def first_kernel(own_ids, rec, mine, other, bias, psum, hc_ref, head, rest, p_hbm, out, usum, msg, ids, p_ref, a_buf, r_buf, id_buf, p_sems, sem):
@@ -197,12 +200,16 @@
     id_buf[4:8, :] = other[TS : TS + 4, :].astype(jnp.int32)
     keep_ids = pltpu.make_async_copy(id_buf, ids, sem)
     keep_ids.start()
+    slots = []
     for t in range(2):
         a, s = own_ids[t], own_ids[2 + t]
         arow = jnp.where((a & 1) == core, rows_of(rec, a, False), other[AR * t : AR * (t + 1), :])
-        srow = jnp.where((s & 1) == core, rows_of(rec, s, True), other[8 + SR * t : 8 + SR * (t + 1), :])
+        spread_half(arow, a_buf.at[pl.ds(t * 512, 512), :])
+        slots.append(jnp.where((s & 1) == core, rows_of(rec, s, True), other[8 + SR * t : 8 + SR * (t + 1), :]))
+    for t in range(2):
         sources = [(p_ref, 0) if t else (head, 0) if b * RB < HEAD else (rest, HEAD) for b in range(NRB)]
-        first_tile(t, arow, srow, sources, hc_ref, out, usum, a_buf, r_buf, functools.partial(ready, t))
+        first_tile(t, slots[t], sources, hc_ref, out, usum, a_buf, r_buf, ready)
+    write_rows(usum, r_buf)
     msg[0:TS, :] = 2.0 * usum[...] - psum[...]
     msg[TS:MSG, :] = bias[...]
     keep_ids.wait()
@@ -213,7 +220,7 @@
     out[MSG:, :] = b[...]
 
 
-def flags_kernel(own_ids, mine, other, _, flags):
+def between_kernel(own_ids, mine, other, u, hc, _, flags, base):
     me = lax.axis_index("tiles")
     core = me & 1
     lane = lax.broadcasted_iota(jnp.int32, (4, L), 1)
@@ -231,6 +238,14 @@
             earlier = found((ids == i) & (place < me * 2 + k))
             flags[2 * kind + k] = jnp.where((i >= 0) & (earlier == 0), 1, 0)
         flags[4 + kind] = 1 - found(ids == me)
+
+    def step(g, carry):
+        rows = pl.ds(pl.multiple_of(g * 16, 16), 16)
+        for t in range(2):
+            base[t, rows, :] = u[t, rows, :] - hc[t, rows, :].astype(jnp.float32)
+        return carry
+
+    lax.fori_loop(0, 32, step, 0, unroll=2)
 
 
 def users_kernel(ids, rec0, rec1, rec2, rec3, _, out, rec, acc_a0, acc_a1, acc_s0, acc_s1):
@@ -259,7 +274,7 @@
         for i, _ in slot:
             acc_s0[pl.ds(at(i), 8), :] = zero
             acc_s1[pl.ds(at(i), 8), :] = zero
-    for d, part in enumerate((rec0, rec1, rec2, rec3)):
+    for d, part in ((0, rec0), (1, rec1), (3, rec2), (2, rec3)):
         rec[d * both : (d + 1) * both, :] = part[...]
         source = (((x - d) & 3) << 4) | line
         for side in range(2):
@@ -286,13 +301,13 @@
             out[o : o + SR, :] = (acc_s0[rows, :] + acc_s1[rows, :]) + bias(i, TS, SR)
 
 
-def second_tile(t, arow, srow, base, outs, usum, a_buf, r_buf, done):
-    spread_half(arow, a_buf)
+def second_tile(t, srow, base, outs, usum, a_buf, r_buf, done):
     s = slot_rows(srow)
 
     def step(out, skip, g, cols):
         rows = pl.ds(pl.multiple_of(g * 8, 8), 8)
-        a = a_buf[rows, :]
+        wide = pl.ds(pl.multiple_of(t * 512 + g * 8, 8), 8)
+        a = a_buf[wide, :]
         cols = list(cols)
         us = []
         for cb in range(SR):
@@ -301,14 +316,14 @@
             out[pl.ds(pl.multiple_of(g * 8 - skip, 8), 8), lanes] = u
             cols[cb] = cols[cb] + u
             us.append(u)
-        r_buf[rows, :] = tree(us)
+        r_buf[wide, :] = tree(us)
         return tuple(cols)
 
     cols = ZEROS()
     for b in range(NRB):
         cols = lax.fori_loop(b * 16, (b + 1) * 16, functools.partial(step, *outs[b]), cols, unroll=4)
         done(t, b)
-    write_sums(t, usum, r_buf, cols)
+    write_cols(t, usum, cols)
 
 
 def second_kernel(flags, rec, base, psum, primal, sums, tail, out, usum, a_buf, r_buf, sems):
@@ -325,9 +340,11 @@
     total = jnp.maximum(tree([rec[j * TS : (j + 1) * TS, :] for j in range(PLANE)]), 0.0)
     adv = total[0:8] * (1.0 / 1024)
     slot = total[8:24] * (1.0 / 512)
+    spread_half(adv, a_buf)
     for t in range(2):
         outs = [(out, -t * 512) if t * 512 + b * RB < early else (tail, early - t * 512) for b in range(NRB)]
-        second_tile(t, adv[4 * t : 4 * t + 4], slot[8 * t : 8 * t + 8], base, outs, usum, a_buf, r_buf, done)
+        second_tile(t, slot[8 * t : 8 * t + 8], base, outs, usum, a_buf, r_buf, done)
+    write_rows(usum, r_buf)
     for k, (o, n) in enumerate(((0, AR), (AR, AR), (8, SR), (8 + SR, SR))):
         rows = pl.ds(o, n)
         named = total[o : o + n] * jnp.where(flags[k] > 0, 1.0, 0.0)
@@ -463,23 +480,23 @@
         [vmem_out(512 - HEAD, 1024)],
         [pltpu.SemaphoreType.DMA(())],
     )
-    base, usum, message, ids = call(
+    update, usum, message, ids = call(
         first_kernel,
         "first",
         [smem_arg(own_ids), table, vmem_arg(picked), vmem_arg(other), vmem_arg(bias), vmem_arg(psum), vmem_arg(hc)]
         + [vmem_arg(head), vmem_arg(rest), hbm_arg(primal_start)],
         [vmem_out(*tile), vmem_out(TS, L), vmem_out(MSG, L), smem_out(8, L)],
-        [vmem(512, 1024), vmem(512, L), vmem(512, L), pltpu.VMEM((8, L), jnp.int32)]
+        [vmem(512, 1024), vmem(1024, L), vmem(1024, L), pltpu.VMEM((8, L), jnp.int32)]
         + [pltpu.SemaphoreType.DMA((NRB,)), pltpu.SemaphoreType.DMA(())],
         8,
     )
     (both,) = call(pair_kernel, "pair", [vmem_arg(message), vmem_arg(swap(message))], [vmem_out(2 * MSG, L)])
-    parts = [vmem_arg(both)] + [vmem_arg(lax.ppermute(both, "tiles", along_x(d))) for d in range(1, 4)]
-    (flags,) = call(
-        flags_kernel,
-        "flags",
-        [smem_arg(own_ids), vmem_arg(picked), vmem_arg(other), vmem_arg(both)],
-        [smem_out(6)],
+    parts = [vmem_arg(both)] + [vmem_arg(lax.ppermute(both, "tiles", along_x(d))) for d in (1, 3, 2)]
+    flags, base = call(
+        between_kernel,
+        "between",
+        [smem_arg(own_ids), vmem_arg(picked), vmem_arg(other), vmem_arg(update), vmem_arg(hc), vmem_arg(both)],
+        [smem_out(6), vmem_out(*tile)],
     )
     (message,) = call(
         users_kernel,
@@ -493,7 +510,7 @@
         "second",
         [smem_arg(flags), exchange(message, PLANE_GROUPS, TS), vmem_arg(base), vmem_arg(usum)],
         [(f32(*tile), pl.BlockSpec(memory_space=pl.ANY))] + [vmem_out(TS, L), vmem_out(TAIL, 1024)],
-        [vmem(1024 - TAIL, 1024), vmem(TS, L), vmem(512, L), vmem(512, L)]
+        [vmem(1024 - TAIL, 1024), vmem(TS, L), vmem(1024, L), vmem(1024, L)]
         + [pltpu.SemaphoreType.DMA((2 * NRB - TAIL // RB,))],
         8,
     )

time: 71.6 us -> 72.4 us (1.011)
  transfers between devices with their start and end apart: 8 -> 8, of which waited for: 6 -> 5; matrix products, arithmetic and copies ran while one was open for 0% -> 0% of each run, Pallas kernels for 11% -> 11%
where the time goes in v9:
time: 72.4 us; the launch traced here: 72 us
  blocking collectives  27.9 us (39%)
  starting transfers between devices  15.6 us (22%)
  Pallas kernels  15.4 us (21%)
  waiting for transfers between devices  12.3 us (17%)
  between operations  0.75 us (1%)
    all_to_all x2, blocking collectives, exchange(): lax.all_to_all(x.reshape(n, rows * L), 'tiles', 0, 0, axis_index_groups=g...  27.9 us
    pallas_call x12, Pallas kernels, call(): pl.pallas_call(kernel, in_specs=[s for _, s in ins], out_specs=[s for _,...  15.4 us
    all_to_all x1, starting transfers between devices, exchange(): lax.all_to_all(x.reshape(n, rows * L), 'tiles', 0, 0, axis_index_groups=g...  11.5 us
    all_to_all x1, waiting for transfers between devices, exchange(): lax.all_to_all(x.reshape(n, rows * L), 'tiles', 0, 0, axis_index_groups=g...  6.86 us
    ppermute x3, waiting for transfers between devices, body(): lax.ppermute(both, 'tiles', along_x(d))  4.43 us
    ppermute x3, starting transfers between devices, body(): lax.ppermute(both, 'tiles', along_x(d))  3.27 us
  transfers between devices with their start and end apart: 8, of which 5 were waited for; matrix products, arithmetic and copies ran while one was open for 0% of the time, Pallas kernels for 11%

profile of v9, /device:TPU:0, one launch (start us, length us, event | category | flops | bytes accessed | tf_op | source)
XLA Modules:
  0.0 72.0 jit_solution(9182513079394337209)
XLA Ops:
  0.6 1.6 %own.1 = (f32[832,128]{1,0:T(8,128)}, f32[12,128]{1,0:T(8,128)S(1)}, f32[12,128]{1,0:T(8,128)S(1)}, s32[8,128]{1,0:T(8,128)S(1)}, s32[4]{0:T(128)S(4)}) custom-call(s32[2]{0:T(128)} %adv_id.1, s32[2]{0:T(128)} %slot_id.1, f32[4,128]{1,0:T(4,128)} %bitcast.22, f32[8,128]{1,0:T(8,128)} %bitcast.20, f32[4,128]{1,0:T(4,128)} %bitcast.23, f32[8,128]{1,0:T(8,128)} %bitcast.21), custom_call_target="tpu_custom_call" | custom-call | tf_op jit(solution)/shard_map/own/pallas_call | solution.py:409
  2.2 11.5 %all-to-all-start = ((f32[64,1,1664]{2,1,0:T(1,128)}), f32[64,1,1664]{2,1,0:T(1,128)S(1)}, u32[]{:S(2)}, u32[]{:S(2)}) async-start(f32[64,1,1664]{2,1,0:T(1,128)} %bitcast.4), calls=%async_computation | async-start | bytes 851968 | tf_op jit(solution)/shard_map/all_to_all | solution.py:447
  13.8 0.1 collective-permute-start
  13.9 5.1 %prepare.1 = (bf16[2,512,1024]{2,1,0:T(8,128)(2,1)S(1)}, f32[24,128]{1,0:T(8,128)S(1)}, f32[128,1024]{1,0:T(8,128)S(1)}) custom-call(s32[4]{0:T(128)S(4)} %get-tuple-element.22.own_ids, s32[2,8,64]{2,1,0:T(8,128)} %bitcast.19, f32[2,512,1024]{2,1,0:T(8,128)} %p_hbm.5, bf16[2,512,1024]{2,1,0:T(8,128)(2,1)} %c_hbm.1), custom_call_target="tpu_custom_call" | custom-call | tf_op jit(solution)/shard_map/prepare/pallas_call | solution.py:409
  19.0 0.0 collective-permute-done.partner_ids
  19.0 6.9 %all-to-all-done = f32[64,1,1664]{2,1,0:T(1,128)S(1)} async-done(((f32[64,1,1664]{2,1,0:T(1,128)}), f32[64,1,1664]{2,1,0:T(1,128)S(1)}, u32[]{:S(2)}, u32[]{:S(2)}) %all-to-all-start) | async-done | bytes 426016 | tf_op jit(solution)/shard_map/all_to_all | solution.py:447
  25.9 0.2 pick.1._.mine
  26.1 0.1 collective-permute-start.1
  26.2 1.4 %load.1.rest = f32[384,1024]{1,0:T(8,128)S(1)} custom-call(f32[2,512,1024]{2,1,0:T(8,128)} %p_hbm.5, f32[32,128]{1,0:T(8,128)S(1)} %pick.1._.mine), custom_call_target="tpu_custom_call" | custom-call | tf_op jit(solution)/shard_map/load/pallas_call | solution.py:409
  27.6 0.0 collective-permute-done.1.other
  27.6 2.1 %first.1 = (f32[2,512,1024]{2,1,0:T(8,128)S(1)}, f32[24,128]{1,0:T(8,128)S(1)}, f32[36,128]{1,0:T(8,128)S(1)}, s32[8,128]{1,0:T(8,128)S(4)}) custom-call(s32[4]{0:T(128)S(4)} %get-tuple-element.22.own_ids, f32[832,128]{1,0:T(8,128)S(1)} %bitcast.14, f32[32,128]{1,0:T(8,128)S(1)} %pick.1._.mine, f32[32,128]{1,0:T(8,128)S(1)} %collective-permute-done.1.other, ...), custom_call_target="tpu_custom_call" | custom-call | tf_op jit(solution)/shard_map/first/pallas_call | solution.py:409
  29.7 0.6 collective-permute-start.2
  30.3 0.8 %collective-permute-done.2.b = f32[36,128]{1,0:T(8,128)S(1)} collective-permute-done((f32[36,128]{1,0:T(8,128)S(1)}, f32[36,128]{1,0:T(8,128)S(1)}, u32[]{:S(2)}, u32[]{:S(2)}) %collective-permute-start.2) | collective-permute-done | bytes 18464 | tf_op jit(solution)/shard_map/ppermute | solution.py:452
  31.1 0.8 %collective-permute-start.5 = (f32[72,128]{1,0:T(8,128)S(1)}, f32[72,128]{1,0:T(8,128)S(1)}, u32[]{:S(2)}, u32[]{:S(2)}) collective-permute-start(f32[72,128]{1,0:T(8,128)S(1)} %pair.1._.rec0), channel_id=1, source_target_pairs={{0,64},{1,65},{2,66},{3,67},{4,68},{5,69},{6,70},{7,71},{8,72},{9,... | collective-permute-start | bytes 110600 | tf_op jit(solution)/shard_map/ppermute | solution.py:494
  31.9 2.4 %collective-permute-start.4 = (f32[72,128]{1,0:T(8,128)S(1)}, f32[72,128]{1,0:T(8,128)S(1)}, u32[]{:S(2)}, u32[]{:S(2)}) collective-permute-start(f32[72,128]{1,0:T(8,128)S(1)} %pair.1._.rec0), channel_id=1, source_target_pairs={{0,96},{1,97},{2,98},{3,99},{4,100},{5,101},{6,102},{7,103},{8,104... | collective-permute-start | bytes 110600 | tf_op jit(solution)/shard_map/ppermute | solution.py:494
  34.4 0.0 collective-permute-start.3
  34.4 0.7 %between.1 = (s32[6]{0:T(128)S(4)}, f32[2,512,1024]{2,1,0:T(8,128)S(1)}) custom-call(s32[4]{0:T(128)S(4)} %get-tuple-element.22.own_ids, f32[32,128]{1,0:T(8,128)S(1)} %pick.1._.mine, f32[32,128]{1,0:T(8,128)S(1)} %collective-permute-done.1.other, f32[2,512,1024]{2,1,0:T(8,128)S(1)} %get-tuple-element.29.u, ...), custom_call_target="tpu_custom_call" | custom-call | tf_op jit(solution)/shard_map/between/pallas_call | solution.py:409
  35.1 1.5 %collective-permute-done.5.rec3 = f32[72,128]{1,0:T(8,128)S(1)} collective-permute-done((f32[72,128]{1,0:T(8,128)S(1)}, f32[72,128]{1,0:T(8,128)S(1)}, u32[]{:S(2)}, u32[]{:S(2)}) %collective-permute-start.5) | collective-permute-done | bytes 36896 | tf_op jit(solution)/shard_map/ppermute | solution.py:494
  36.6 0.0 collective-permute-done.4.rec2
  36.6 3.0 %collective-permute-done.3.rec1 = f32[72,128]{1,0:T(8,128)S(1)} collective-permute-done((f32[72,128]{1,0:T(8,128)S(1)}, f32[72,128]{1,0:T(8,128)S(1)}, u32[]{:S(2)}, u32[]{:S(2)}) %collective-permute-start.3) | collective-permute-done | bytes 36896 | tf_op jit(solution)/shard_map/ppermute | solution.py:494
  39.6 0.5 users.1
  40.1 11.5 %all_to_all.27 = f32[16,1,3072]{2,1,0:T(1,128)S(1)} all-to-all(f32[16,1,3072]{2,1,0:T(1,128)S(1)} %bitcast.17), channel_id=1, replica_groups={{0,2,4,6,8,10,12,14,16,18,20,22,24,26,28,30},{1,3,5,7,9,11,13,15,17,19,..., dimensions={0} | all-to-all | bytes 393216 | tf_op jit(solution)/shard_map/all_to_all | solution.py:447
  51.6 2.0 %second.1 = (f32[2,512,1024]{2,1,0:T(8,128)}, f32[24,128]{1,0:T(8,128)S(1)}, f32[256,1024]{1,0:T(8,128)S(1)}) custom-call(s32[6]{0:T(128)S(4)} %get-tuple-element.31._.flags, f32[384,128]{1,0:T(8,128)S(1)} %bitcast.18, f32[2,512,1024]{2,1,0:T(8,128)S(1)} %get-tuple-element.33.base, f32[24,128]{1,0:T(8,128)S(1)} %get-tuple-element.34.psum), custom_call_target="tpu_custom_call" | custom-call | tf_op jit(solution)/shard_map/second/pallas_call | solution.py:409
  53.6 0.1 collective-permute-start.6
  53.7 1.0 %store.1._ = f32[2,512,1024]{2,1,0:T(8,128)} custom-call(f32[256,1024]{1,0:T(8,128)S(1)} %get-tuple-element.35.tail, f32[2,512,1024]{2,1,0:T(8,128)} %get-tuple-element.36._), custom_call_target="tpu_custom_call", output_to_operand_aliasing={{}: (1, {})} | custom-call | tf_op jit(solution)/shard_map/store/pallas_call | solution.py:409
  54.7 0.2 collective-permute-done.6.other
  54.9 0.1 owners.1
  55.0 16.4 %all_to_all.28 = f32[64,1,1536]{2,1,0:T(1,128)S(1)} all-to-all(f32[64,1,1536]{2,1,0:T(1,128)S(1)} %bitcast.16), channel_id=1, replica_groups={{0,2,4,6,8,10,12,14,16,18,20,22,24,26,28,30,32,34,36,38,40,42,44,46,48,..., dimensions={0} | all-to-all | bytes 786432 | tf_op jit(solution)/shard_map/all_to_all | solution.py:447
  71.3 0.6 last.1
  (1 shorter events, 0.0 us)
Async XLA Ops:
  2.2 23.6 %all-to-all-start = ((f32[64,1,1664]{2,1,0:T(1,128)}), f32[64,1,1664]{2,1,0:T(1,128)S(1)}, u32[]{:S(2)}, u32[]{:S(2)}) async-start(f32[64,1,1664]{2,1,0:T(1,128)} %bitcast.4), calls=%async_computation | async-start | bytes 851968 | tf_op jit(solution)/shard_map/all_to_all | solution.py:447
  13.8 5.2 %collective-permute-start = (s32[8,128]{1,0:T(8,128)S(1)}, s32[8,128]{1,0:T(8,128)S(1)}, u32[]{:S(2)}, u32[]{:S(2)}) collective-permute-start(s32[8,128]{1,0:T(8,128)S(1)} %get-tuple-element.23), channel_id=1, source_target_pairs={{0,1},{1,0},{2,3},{3,2},{4,5},{5,4},{6,7},{7,6},{8,9},{9,8},{10,11... | collective-permute-start | bytes 12296 | tf_op jit(solution)/shard_map/ppermute | solution.py:452
  26.1 1.5 %collective-permute-start.1 = (f32[32,128]{1,0:T(8,128)S(1)}, f32[32,128]{1,0:T(8,128)S(1)}, u32[]{:S(2)}, u32[]{:S(2)}) collective-permute-start(f32[32,128]{1,0:T(8,128)S(1)} %pick.1._.mine), channel_id=1, source_target_pairs={{0,1},{1,0},{2,3},{3,2},{4,5},{5,4},{6,7},{7,6},{8,9},{9,8},{10,11... | collective-permute-start | bytes 49160 | tf_op jit(solution)/shard_map/ppermute | solution.py:452
  29.7 1.4 %collective-permute-start.2 = (f32[36,128]{1,0:T(8,128)S(1)}, f32[36,128]{1,0:T(8,128)S(1)}, u32[]{:S(2)}, u32[]{:S(2)}) collective-permute-start(f32[36,128]{1,0:T(8,128)S(1)} %get-tuple-element.30.a), channel_id=1, source_target_pairs={{0,1},{1,0},{2,3},{3,2},{4,5},{5,4},{6,7},{7,6},{8,9},{9,8},{10,11... | collective-permute-start | bytes 55304 | tf_op jit(solution)/shard_map/ppermute | solution.py:452
  31.1 5.5 %collective-permute-start.5 = (f32[72,128]{1,0:T(8,128)S(1)}, f32[72,128]{1,0:T(8,128)S(1)}, u32[]{:S(2)}, u32[]{:S(2)}) collective-permute-start(f32[72,128]{1,0:T(8,128)S(1)} %pair.1._.rec0), channel_id=1, source_target_pairs={{0,64},{1,65},{2,66},{3,67},{4,68},{5,69},{6,70},{7,71},{8,72},{9,... | collective-permute-start | bytes 110600 | tf_op jit(solution)/shard_map/ppermute | solution.py:494
  31.9 4.6 %collective-permute-start.4 = (f32[72,128]{1,0:T(8,128)S(1)}, f32[72,128]{1,0:T(8,128)S(1)}, u32[]{:S(2)}, u32[]{:S(2)}) collective-permute-start(f32[72,128]{1,0:T(8,128)S(1)} %pair.1._.rec0), channel_id=1, source_target_pairs={{0,96},{1,97},{2,98},{3,99},{4,100},{5,101},{6,102},{7,103},{8,104... | collective-permute-start | bytes 110600 | tf_op jit(solution)/shard_map/ppermute | solution.py:494
  34.4 5.2 %collective-permute-start.3 = (f32[72,128]{1,0:T(8,128)S(1)}, f32[72,128]{1,0:T(8,128)S(1)}, u32[]{:S(2)}, u32[]{:S(2)}) collective-permute-start(f32[72,128]{1,0:T(8,128)S(1)} %pair.1._.rec0), channel_id=1, source_target_pairs={{0,32},{1,33},{2,34},{3,35},{4,36},{5,37},{6,38},{7,39},{8,40},{9,... | collective-permute-start | bytes 110600 | tf_op jit(solution)/shard_map/ppermute | solution.py:494
  53.6 1.3 %collective-permute-start.6 = (f32[24,128]{1,0:T(8,128)S(1)}, f32[24,128]{1,0:T(8,128)S(1)}, u32[]{:S(2)}, u32[]{:S(2)}) collective-permute-start(f32[24,128]{1,0:T(8,128)S(1)} %get-tuple-element.37.mine), channel_id=1, source_target_pairs={{0,1},{1,0},{2,3},{3,2},{4,5},{5,4},{6,7},{7,6},{8,9},{9,8},{10,11... | collective-permute-start | bytes 36872 | tf_op jit(solution)/shard_map/ppermute | solution.py:452

commit v10 on v9

--- a/solution.py
+++ b/solution.py
@@ -26,11 +26,9 @@
 PLANE = 16
 CORE_GROUPS = [[j * 2 + c for j in range(CHIPS)] for c in range(2)]
 PLANE_GROUPS = [[(x * PLANE + j) * 2 + c for j in range(PLANE)] for x in range(4) for c in range(2)]
+LINE = 8
+LINE_GROUPS = [[(x * PLANE + j) * 2 + c for x in range(4) for c in range(2)] for j in range(PLANE)]
 PARTNERS = [(i, i ^ 1) for i in range(2 * CHIPS)]
-
-
-def along_x(d):
-    return [(i, (i + d * 2 * PLANE) % (2 * CHIPS)) for i in range(2 * CHIPS)]
 
 
 IN_VMEM = pl.BlockSpec(memory_space=pltpu.VMEM)
@@ -169,8 +167,9 @@
             c16 = hc_ref[t, pl.ds(r0, 16), lanes].astype(jnp.float32)
             for h in range(2):
                 p = p_ref[pl.ds(pl.multiple_of(r0 + 8 * h - skip, 8), 8), lanes]
-                u = jnp.minimum(jnp.maximum(((p - c16[8 * h : 8 * h + 8]) - a[h]) - s[cb], 0.0), 1.0)
-                out[t, pl.ds(pl.multiple_of(r0 + 8 * h, 8), 8), lanes] = u
+                hc = c16[8 * h : 8 * h + 8]
+                u = jnp.minimum(jnp.maximum(((p - hc) - a[h]) - s[cb], 0.0), 1.0)
+                out[t, pl.ds(pl.multiple_of(r0 + 8 * h, 8), 8), lanes] = u - hc
                 us[h].append(u)
                 cols[cb] = cols[cb] + u
         for h in range(2):
@@ -210,17 +209,13 @@
         sources = [(p_ref, 0) if t else (head, 0) if b * RB < HEAD else (rest, HEAD) for b in range(NRB)]
         first_tile(t, slots[t], sources, hc_ref, out, usum, a_buf, r_buf, ready)
     write_rows(usum, r_buf)
-    msg[0:TS, :] = 2.0 * usum[...] - psum[...]
-    msg[TS:MSG, :] = bias[...]
+    data = jnp.concatenate([2.0 * usum[...] - psum[...], bias[...]], axis=0)
+    for j in range(LINE):
+        msg[j * MSG : (j + 1) * MSG, :] = data
     keep_ids.wait()
 
 
-def pair_kernel(a, b, out):
-    out[0:MSG, :] = a[...]
-    out[MSG:, :] = b[...]
-
-
-def between_kernel(own_ids, mine, other, u, hc, _, flags, base):
+def write_flags(own_ids, mine, other, flags):
     me = lax.axis_index("tiles")
     core = me & 1
     lane = lax.broadcasted_iota(jnp.int32, (4, L), 1)
@@ -239,22 +234,14 @@
             flags[2 * kind + k] = jnp.where((i >= 0) & (earlier == 0), 1, 0)
         flags[4 + kind] = 1 - found(ids == me)
 
-    def step(g, carry):
-        rows = pl.ds(pl.multiple_of(g * 16, 16), 16)
-        for t in range(2):
-            base[t, rows, :] = u[t, rows, :] - hc[t, rows, :].astype(jnp.float32)
-        return carry
-
-    lax.fori_loop(0, 32, step, 0, unroll=2)
-
-
-def users_kernel(ids, rec0, rec1, rec2, rec3, _, out, rec, acc_a0, acc_a1, acc_s0, acc_s1):
+
+def users_kernel(own_ids, ids, mine, other, rec, out, flags, acc_a0, acc_a1, acc_s0, acc_s1):
+    write_flags(own_ids, mine, other, flags)
     me = lax.axis_index("tiles")
     chip = me >> 1
     core = me & 1
     x = chip >> 4
     line = chip & 15
-    both = 2 * MSG
 
     def at(i):
         return pl.multiple_of(jnp.where(i < 0, BLOCKS, i) * 8, 8)
@@ -274,23 +261,21 @@
         for i, _ in slot:
             acc_s0[pl.ds(at(i), 8), :] = zero
             acc_s1[pl.ds(at(i), 8), :] = zero
-    for d, part in ((0, rec0), (1, rec1), (3, rec2), (2, rec3)):
-        rec[d * both : (d + 1) * both, :] = part[...]
-        source = (((x - d) & 3) << 4) | line
-        for side in range(2):
-            o = side * MSG
-            for k, acc in ((0, acc_a0), (1, acc_a1)):
-                rows = pl.ds(at(ids[4 * side + k, source]), AR)
-                acc[rows, :] = acc[rows, :] + part[o + AR * k : o + AR * (k + 1), :]
-            for k, acc in ((0, acc_s0), (1, acc_s1)):
-                rows = pl.ds(at(ids[4 * side + 2 + k, source]), SR)
-                acc[rows, :] = acc[rows, :] + part[o + 8 + SR * k : o + 8 + SR * (k + 1), :]
+    for j in range(LINE):
+        source = ((j >> 1) << 4) | line
+        side = 4 * ((j & 1) ^ core)
+        o = j * MSG
+        for k, acc in ((0, acc_a0), (1, acc_a1)):
+            rows = pl.ds(at(ids[side + k, source]), AR)
+            acc[rows, :] = acc[rows, :] + rec[o + AR * k : o + AR * (k + 1), :]
+        for k, acc in ((0, acc_s0), (1, acc_s1)):
+            rows = pl.ds(at(ids[side + 2 + k, source]), SR)
+            acc[rows, :] = acc[rows, :] + rec[o + 8 + SR * k : o + 8 + SR * (k + 1), :]
 
     def bias(i, o, n):
         b = jnp.maximum(i, 0)
         here = ((b >> 1) & 15) == line
-        row = ((x - (b >> 5)) & 3) * both + ((b & 1) ^ core) * MSG + o
-        return rec[pl.ds(row, n), :] * jnp.where(here, 1.0, 0.0)
+        return rec[pl.ds(((b >> 5) * 2 + (b & 1)) * MSG + o, n), :] * jnp.where(here, 1.0, 0.0)
 
     for adv, slot in wanted:
         for i, o in adv:
@@ -480,30 +465,23 @@
         [vmem_out(512 - HEAD, 1024)],
         [pltpu.SemaphoreType.DMA(())],
     )
-    update, usum, message, ids = call(
+    base, usum, message, ids = call(
         first_kernel,
         "first",
         [smem_arg(own_ids), table, vmem_arg(picked), vmem_arg(other), vmem_arg(bias), vmem_arg(psum), vmem_arg(hc)]
         + [vmem_arg(head), vmem_arg(rest), hbm_arg(primal_start)],
-        [vmem_out(*tile), vmem_out(TS, L), vmem_out(MSG, L), smem_out(8, L)],
+        [vmem_out(*tile), vmem_out(TS, L), vmem_out(LINE * MSG, L), smem_out(8, L)],
         [vmem(512, 1024), vmem(1024, L), vmem(1024, L), pltpu.VMEM((8, L), jnp.int32)]
         + [pltpu.SemaphoreType.DMA((NRB,)), pltpu.SemaphoreType.DMA(())],
         8,
     )
-    (both,) = call(pair_kernel, "pair", [vmem_arg(message), vmem_arg(swap(message))], [vmem_out(2 * MSG, L)])
-    parts = [vmem_arg(both)] + [vmem_arg(lax.ppermute(both, "tiles", along_x(d))) for d in (1, 3, 2)]
-    flags, base = call(
-        between_kernel,
-        "between",
-        [smem_arg(own_ids), vmem_arg(picked), vmem_arg(other), vmem_arg(update), vmem_arg(hc), vmem_arg(both)],
-        [smem_out(6), vmem_out(*tile)],
-    )
-    (message,) = call(
+    part = exchange(message, LINE_GROUPS, MSG)
+    message, flags = call(
         users_kernel,
         "users",
-        [smem_arg(ids)] + parts + [smem_arg(flags)],
-        [vmem_out(PLANE * TS, L)],
-        [vmem(8 * MSG, L)] + [vmem((BLOCKS + 1) * 8, L)] * 4,
+        [smem_arg(own_ids), smem_arg(ids), vmem_arg(picked), vmem_arg(other), part],
+        [vmem_out(PLANE * TS, L), smem_out(6)],
+        [vmem((BLOCKS + 1) * 8, L)] * 4,
     )
     primal, sums, tail = call(
         second_kernel,

time: 72.4 us -> 71.8 us (level)
  blocking collectives: 27.9 us -> 36.9 us
  waiting for transfers between devices: 12.3 us -> 7.04 us
  starting transfers between devices: 15.6 us -> 11.8 us
    all_to_all x2 -> x3, blocking collectives: 27.9 us -> 36.9 us  [exchange(): lax.all_to_all(x.reshape(n, rows * L), 'tiles', 0, 0, axis_index_groups=g...]
    ppermute x3 -> x0, waiting for transfers between devices: 4.43 us -> none  [body(): lax.ppermute(both, 'tiles', along_x(d))]
    ppermute x3 -> x0, starting transfers between devices: 3.27 us -> none  [body(): lax.ppermute(both, 'tiles', along_x(d))]
    ppermute x4 -> x3, waiting for transfers between devices: 1.02 us -> 0.18 us  [swap(): return lax.ppermute(x, 'tiles', PARTNERS)]
    pallas_call x12 -> x10, Pallas kernels: 15.4 us -> 14.8 us  [call(): pl.pallas_call(kernel, in_specs=[s for _, s in ins], out_specs=[s for _,...]
  transfers between devices with their start and end apart: 8 -> 4, of which waited for: 5 -> 2; matrix products, arithmetic and copies ran while one was open for 0% -> 0% of each run, Pallas kernels for 11% -> 11%
where the time goes in v10:
time: 71.8 us; the launch traced here: 71.3 us
  blocking collectives  36.9 us (51%)
  Pallas kernels  14.8 us (21%)
  starting transfers between devices  11.8 us (16%)
  waiting for transfers between devices  7.04 us (10%)
  between operations  0.75 us (1%)
    all_to_all x3, blocking collectives, exchange(): lax.all_to_all(x.reshape(n, rows * L), 'tiles', 0, 0, axis_index_groups=g...  36.9 us
    pallas_call x10, Pallas kernels, call(): pl.pallas_call(kernel, in_specs=[s for _, s in ins], out_specs=[s for _,...  14.8 us
    all_to_all x1, starting transfers between devices, exchange(): lax.all_to_all(x.reshape(n, rows * L), 'tiles', 0, 0, axis_index_groups=g...  11.5 us
    all_to_all x1, waiting for transfers between devices, exchange(): lax.all_to_all(x.reshape(n, rows * L), 'tiles', 0, 0, axis_index_groups=g...  6.86 us
  transfers between devices with their start and end apart: 4, of which 2 were waited for; matrix products, arithmetic and copies ran while one was open for 0% of the time, Pallas kernels for 11%

profile of v10, /device:TPU:0, one launch (start us, length us, event | category | flops | bytes accessed | tf_op | source)
XLA Modules:
  0.0 71.3 jit_solution(7205772010971951678)
XLA Ops:
  0.6 1.6 %own.1 = (f32[832,128]{1,0:T(8,128)}, f32[12,128]{1,0:T(8,128)S(1)}, f32[12,128]{1,0:T(8,128)S(1)}, s32[8,128]{1,0:T(8,128)S(1)}, s32[4]{0:T(128)S(4)}) custom-call(s32[2]{0:T(128)} %adv_id.1, s32[2]{0:T(128)} %slot_id.1, f32[4,128]{1,0:T(4,128)} %bitcast.26, f32[8,128]{1,0:T(8,128)} %bitcast.24, f32[4,128]{1,0:T(4,128)} %bitcast.27, f32[8,128]{1,0:T(8,128)} %bitcast.25), custom_call_target="tpu_custom_call" | custom-call | tf_op jit(solution)/shard_map/own/pallas_call | solution.py:394
  2.2 11.5 %all-to-all-start = ((f32[64,1,1664]{2,1,0:T(1,128)}), f32[64,1,1664]{2,1,0:T(1,128)S(1)}, u32[]{:S(2)}, u32[]{:S(2)}) async-start(f32[64,1,1664]{2,1,0:T(1,128)} %bitcast.4), calls=%async_computation | async-start | bytes 851968 | tf_op jit(solution)/shard_map/all_to_all | solution.py:432
  13.8 0.1 collective-permute-start
  13.9 5.1 %prepare.1 = (bf16[2,512,1024]{2,1,0:T(8,128)(2,1)S(1)}, f32[24,128]{1,0:T(8,128)S(1)}, f32[128,1024]{1,0:T(8,128)S(1)}) custom-call(s32[4]{0:T(128)S(4)} %get-tuple-element.22.own_ids, s32[2,8,64]{2,1,0:T(8,128)} %bitcast.23, f32[2,512,1024]{2,1,0:T(8,128)} %p_hbm.5, bf16[2,512,1024]{2,1,0:T(8,128)(2,1)} %c_hbm.1), custom_call_target="tpu_custom_call" | custom-call | tf_op jit(solution)/shard_map/prepare/pallas_call | solution.py:394
  19.0 0.0 collective-permute-done.partner_ids
  19.0 6.9 %all-to-all-done = f32[64,1,1664]{2,1,0:T(1,128)S(1)} async-done(((f32[64,1,1664]{2,1,0:T(1,128)}), f32[64,1,1664]{2,1,0:T(1,128)S(1)}, u32[]{:S(2)}, u32[]{:S(2)}) %all-to-all-start) | async-done | bytes 426016 | tf_op jit(solution)/shard_map/all_to_all | solution.py:432
  25.9 0.2 pick.1._.mine
  26.1 0.1 collective-permute-start.1
  26.2 1.4 %load.1.rest = f32[384,1024]{1,0:T(8,128)S(1)} custom-call(f32[2,512,1024]{2,1,0:T(8,128)} %p_hbm.5, f32[32,128]{1,0:T(8,128)S(1)} %pick.1._.mine), custom_call_target="tpu_custom_call" | custom-call | tf_op jit(solution)/shard_map/load/pallas_call | solution.py:394
  27.6 0.0 collective-permute-done.1.other
  27.6 2.1 %first.1 = (f32[2,512,1024]{2,1,0:T(8,128)S(1)}, f32[24,128]{1,0:T(8,128)S(1)}, f32[288,128]{1,0:T(8,128)S(1)}, s32[8,128]{1,0:T(8,128)S(4)}) custom-call(s32[4]{0:T(128)S(4)} %get-tuple-element.22.own_ids, f32[832,128]{1,0:T(8,128)S(1)} %bitcast.16, f32[32,128]{1,0:T(8,128)S(1)} %pick.1._.mine, f32[32,128]{1,0:T(8,128)S(1)} %collective-permute-done.1.other, ...), custom_call_target="tpu_custom_call" | custom-call | tf_op jit(solution)/shard_map/first/pallas_call | solution.py:394
  29.8 8.7 %all_to_all.36 = f32[8,1,4608]{2,1,0:T(1,128)S(1)} all-to-all(f32[8,1,4608]{2,1,0:T(1,128)S(1)} %bitcast.22), channel_id=1, replica_groups={{0,1,32,33,64,65,96,97},{2,3,34,35,66,67,98,99},{4,5,36,37,68,69,100,10..., dimensions={0} | all-to-all | bytes 294912 | tf_op jit(solution)/shard_map/all_to_all | solution.py:432
  38.4 0.6 users.1
  39.0 11.5 %all_to_all.37 = f32[16,1,3072]{2,1,0:T(1,128)S(1)} all-to-all(f32[16,1,3072]{2,1,0:T(1,128)S(1)} %bitcast.21), channel_id=1, replica_groups={{0,2,4,6,8,10,12,14,16,18,20,22,24,26,28,30},{1,3,5,7,9,11,13,15,17,19,..., dimensions={0} | all-to-all | bytes 393216 | tf_op jit(solution)/shard_map/all_to_all | solution.py:432
  50.5 2.0 %second.1 = (f32[2,512,1024]{2,1,0:T(8,128)}, f32[24,128]{1,0:T(8,128)S(1)}, f32[256,1024]{1,0:T(8,128)S(1)}) custom-call(s32[6]{0:T(128)S(4)} %get-tuple-element.31.flags, f32[384,128]{1,0:T(8,128)S(1)} %bitcast.19, f32[2,512,1024]{2,1,0:T(8,128)S(1)} %get-tuple-element.33.base, f32[24,128]{1,0:T(8,128)S(1)} %get-tuple-element.34.psum), custom_call_target="tpu_custom_call" | custom-call | tf_op jit(solution)/shard_map/second/pallas_call | solution.py:394
  52.6 0.1 collective-permute-start.2
  52.7 1.0 %store.1._ = f32[2,512,1024]{2,1,0:T(8,128)} custom-call(f32[256,1024]{1,0:T(8,128)S(1)} %get-tuple-element.35.tail, f32[2,512,1024]{2,1,0:T(8,128)} %get-tuple-element.36._), custom_call_target="tpu_custom_call", output_to_operand_aliasing={{}: (1, {})} | custom-call | tf_op jit(solution)/shard_map/store/pallas_call | solution.py:394
  53.7 0.2 collective-permute-done.2.other
  53.8 0.1 owners.1
  53.9 16.8 %all_to_all.38 = f32[64,1,1536]{2,1,0:T(1,128)S(1)} all-to-all(f32[64,1,1536]{2,1,0:T(1,128)S(1)} %bitcast.18), channel_id=1, replica_groups={{0,2,4,6,8,10,12,14,16,18,20,22,24,26,28,30,32,34,36,38,40,42,44,46,48,..., dimensions={0} | all-to-all | bytes 786432 | tf_op jit(solution)/shard_map/all_to_all | solution.py:432
  70.7 0.6 last.1
Async XLA Ops:
  2.2 23.6 %all-to-all-start = ((f32[64,1,1664]{2,1,0:T(1,128)}), f32[64,1,1664]{2,1,0:T(1,128)S(1)}, u32[]{:S(2)}, u32[]{:S(2)}) async-start(f32[64,1,1664]{2,1,0:T(1,128)} %bitcast.4), calls=%async_computation | async-start | bytes 851968 | tf_op jit(solution)/shard_map/all_to_all | solution.py:432
  13.8 5.2 %collective-permute-start = (s32[8,128]{1,0:T(8,128)S(1)}, s32[8,128]{1,0:T(8,128)S(1)}, u32[]{:S(2)}, u32[]{:S(2)}) collective-permute-start(s32[8,128]{1,0:T(8,128)S(1)} %get-tuple-element.24), channel_id=1, source_target_pairs={{0,1},{1,0},{2,3},{3,2},{4,5},{5,4},{6,7},{7,6},{8,9},{9,8},{10,11... | collective-permute-start | bytes 12296 | tf_op jit(solution)/shard_map/ppermute | solution.py:437
  26.1 1.5 %collective-permute-start.1 = (f32[32,128]{1,0:T(8,128)S(1)}, f32[32,128]{1,0:T(8,128)S(1)}, u32[]{:S(2)}, u32[]{:S(2)}) collective-permute-start(f32[32,128]{1,0:T(8,128)S(1)} %pick.1._.mine), channel_id=1, source_target_pairs={{0,1},{1,0},{2,3},{3,2},{4,5},{5,4},{6,7},{7,6},{8,9},{9,8},{10,11... | collective-permute-start | bytes 49160 | tf_op jit(solution)/shard_map/ppermute | solution.py:437
  52.6 1.3 %collective-permute-start.2 = (f32[24,128]{1,0:T(8,128)S(1)}, f32[24,128]{1,0:T(8,128)S(1)}, u32[]{:S(2)}, u32[]{:S(2)}) collective-permute-start(f32[24,128]{1,0:T(8,128)S(1)} %get-tuple-element.37.mine), channel_id=1, source_target_pairs={{0,1},{1,0},{2,3},{3,2},{4,5},{5,4},{6,7},{7,6},{8,9},{9,8},{10,11... | collective-permute-start | bytes 36872 | tf_op jit(solution)/shard_map/ppermute | solution.py:437

commit v11 on v10

--- a/solution.py
+++ b/solution.py
@@ -5,6 +5,7 @@
 from jax import lax
 from jax.experimental import pallas as pl
 from jax.experimental.pallas import tpu as pltpu
+from jax.sharding import Mesh
 from jax.sharding import PartitionSpec as P
 
 CHIPS = 64
@@ -24,8 +25,7 @@
 TAIL = 256
 
 PLANE = 16
-CORE_GROUPS = [[j * 2 + c for j in range(CHIPS)] for c in range(2)]
-PLANE_GROUPS = [[(x * PLANE + j) * 2 + c for j in range(PLANE)] for x in range(4) for c in range(2)]
+AXES = ("x", "z", "y", "core")
 LINE = 8
 LINE_GROUPS = [[(x * PLANE + j) * 2 + c for x in range(4) for c in range(2)] for j in range(PLANE)]
 PARTNERS = [(i, i ^ 1) for i in range(2 * CHIPS)]
@@ -33,6 +33,11 @@
 
 IN_VMEM = pl.BlockSpec(memory_space=pltpu.VMEM)
 IN_SMEM = pl.BlockSpec(memory_space=pltpu.SMEM)
+
+
+def device():
+    x, z, y, core = (lax.axis_index(a) for a in AXES)
+    return ((x * 4 + z) * 4 + y) * 2 + core
 
 
 def own_kernel(adv_id, slot_id, adv, slot, limit, cap, out, bias, bounds, row_ids, ids):
@@ -194,7 +199,7 @@
 
     for b in range(NRB):
         fetch(b).start()
-    core = lax.axis_index("tiles") & 1
+    core = lax.axis_index("core")
     id_buf[0:4, :] = mine[TS : TS + 4, :].astype(jnp.int32)
     id_buf[4:8, :] = other[TS : TS + 4, :].astype(jnp.int32)
     keep_ids = pltpu.make_async_copy(id_buf, ids, sem)
@@ -216,7 +221,7 @@
 
 
 def write_flags(own_ids, mine, other, flags):
-    me = lax.axis_index("tiles")
+    me = device()
     core = me & 1
     lane = lax.broadcasted_iota(jnp.int32, (4, L), 1)
     row = lax.broadcasted_iota(jnp.int32, (4, L), 0)
@@ -237,7 +242,7 @@
 
 def users_kernel(own_ids, ids, mine, other, rec, out, flags, acc_a0, acc_a1, acc_s0, acc_s1):
     write_flags(own_ids, mine, other, flags)
-    me = lax.axis_index("tiles")
+    me = device()
     chip = me >> 1
     core = me & 1
     x = chip >> 4
@@ -346,7 +351,7 @@
 
 def owners_kernel(ids, mine, other, _, out):
 
-    me = lax.axis_index("tiles")
+    me = device()
     chip = me >> 1
     core = me & 1
     out[...] = jnp.zeros_like(out)
@@ -427,14 +432,14 @@
     return (vmem(*shape), IN_VMEM)
 
 
-def exchange(x, groups, rows):
-    n = len(groups[0])
-    x = lax.all_to_all(x.reshape(n, rows * L), "tiles", 0, 0, axis_index_groups=groups, tiled=True)
+def exchange(x, axes, rows, groups=None):
+    n = x.shape[0] // rows
+    x = lax.all_to_all(x.reshape(n, rows * L), axes, 0, 0, axis_index_groups=groups, tiled=True)
     return vmem_arg(x.reshape(n * rows, L))
 
 
 def swap(x):
-    return lax.ppermute(x, "tiles", PARTNERS)
+    return lax.ppermute(x, AXES, PARTNERS)
 
 
 def body(primal_start, cost, mask, tile_adv, tile_slot, adv_dual, slot_dual, spend_limit, capacity):
@@ -447,7 +452,7 @@
         [vmem_out(CHIPS * OWN, L), vmem_out(OUT, L), vmem_out(OUT, L)]
         + [(pltpu.VMEM((8, L), jnp.int32), IN_VMEM), smem_out(4)],
     )
-    table = exchange(message, CORE_GROUPS, OWN)
+    table = exchange(message, AXES[:3], OWN)
     hc, psum, head = call(
         prepare_kernel,
         "prepare",
@@ -475,7 +480,7 @@
         + [pltpu.SemaphoreType.DMA((NRB,)), pltpu.SemaphoreType.DMA(())],
         8,
     )
-    part = exchange(message, LINE_GROUPS, MSG)
+    part = exchange(message, AXES, MSG, LINE_GROUPS)
     message, flags = call(
         users_kernel,
         "users",
@@ -486,7 +491,7 @@
     primal, sums, tail = call(
         second_kernel,
         "second",
-        [smem_arg(flags), exchange(message, PLANE_GROUPS, TS), vmem_arg(base), vmem_arg(usum)],
+        [smem_arg(flags), exchange(message, AXES[1:3], TS), vmem_arg(base), vmem_arg(usum)],
         [(f32(*tile), pl.BlockSpec(memory_space=pl.ANY))] + [vmem_out(TS, L), vmem_out(TAIL, 1024)],
         [vmem(1024 - TAIL, 1024), vmem(TS, L), vmem(1024, L), vmem(1024, L)]
         + [pltpu.SemaphoreType.DMA((2 * NRB - TAIL // RB,))],
@@ -509,7 +514,7 @@
     adv_out, slot_out = call(
         last_kernel,
         "last",
-        [smem_arg(flags), exchange(message, CORE_GROUPS, OUT), vmem_arg(bias), vmem_arg(bounds)],
+        [smem_arg(flags), exchange(message, AXES[:3], OUT), vmem_arg(bias), vmem_arg(bounds)],
         [(f32(AR, L), IN_VMEM), (f32(SR, L), IN_VMEM)],
     )
     return primal, adv_out.reshape(1, 512), slot_out.reshape(1, 1024)
@@ -518,18 +523,18 @@
 def solution(mesh):
     return jax.shard_map(
         body,
-        mesh=mesh,
+        mesh=Mesh(mesh.devices.reshape(4, 4, 4, 2), AXES),
         in_specs=(
-            P("tiles", None, None),
-            P("tiles", None, None),
-            P("tiles", None, None),
-            P("tiles"),
-            P("tiles"),
-            P("tiles", None),
-            P("tiles", None),
-            P("tiles", None),
-            P("tiles", None),
+            P(AXES, None, None),
+            P(AXES, None, None),
+            P(AXES, None, None),
+            P(AXES),
+            P(AXES),
+            P(AXES, None),
+            P(AXES, None),
+            P(AXES, None),
+            P(AXES, None),
         ),
-        out_specs=(P("tiles", None, None), P("tiles", None), P("tiles", None)),
+        out_specs=(P(AXES, None, None), P(AXES, None), P(AXES, None)),
         check_vma=False,
     )

time: 71.8 us -> 71.8 us (level)
  no operation moved by 1% of the time
where the time goes in v11:
time: 71.8 us; the launch traced here: 71.3 us
  blocking collectives  36.9 us (51%)
  Pallas kernels  14.8 us (21%)
  starting transfers between devices  11.8 us (16%)
  waiting for transfers between devices  7.04 us (10%)
  between operations  0.75 us (1%)
    all_to_all x3, blocking collectives, exchange(): lax.all_to_all(x.reshape(n, rows * L), axes, 0, 0, axis_index_groups=grou...  36.9 us
    pallas_call x10, Pallas kernels, call(): pl.pallas_call(kernel, in_specs=[s for _, s in ins], out_specs=[s for _,...  14.8 us
    all_to_all x1, starting transfers between devices, exchange(): lax.all_to_all(x.reshape(n, rows * L), axes, 0, 0, axis_index_groups=grou...  11.5 us
    all_to_all x1, waiting for transfers between devices, exchange(): lax.all_to_all(x.reshape(n, rows * L), axes, 0, 0, axis_index_groups=grou...  6.86 us
  transfers between devices with their start and end apart: 4, of which 2 were waited for; matrix products, arithmetic and copies ran while one was open for 0% of the time, Pallas kernels for 11%

profile of v11, /device:TPU:0, one launch (start us, length us, event | category | flops | bytes accessed | tf_op | source)
XLA Modules:
  0.0 71.3 jit_solution(18017248911266009808)
XLA Ops:
  0.6 1.6 %own.1 = (f32[832,128]{1,0:T(8,128)}, f32[12,128]{1,0:T(8,128)S(1)}, f32[12,128]{1,0:T(8,128)S(1)}, s32[8,128]{1,0:T(8,128)S(1)}, s32[4]{0:T(128)S(4)}) custom-call(s32[2]{0:T(128)} %adv_id.1, s32[2]{0:T(128)} %slot_id.1, f32[4,128]{1,0:T(4,128)} %bitcast.26, f32[8,128]{1,0:T(8,128)} %bitcast.24, f32[4,128]{1,0:T(4,128)} %bitcast.27, f32[8,128]{1,0:T(8,128)} %bitcast.25), custom_call_target="tpu_custom_call" | custom-call | tf_op jit(solution)/shard_map/own/pallas_call | solution.py:399
  2.2 11.5 %all-to-all-start = ((f32[64,1,1664]{2,1,0:T(1,128)}), f32[64,1,1664]{2,1,0:T(1,128)S(1)}, u32[]{:S(2)}, u32[]{:S(2)}) async-start(f32[64,1,1664]{2,1,0:T(1,128)} %bitcast.4), calls=%async_computation | async-start | bytes 851968 | tf_op jit(solution)/shard_map/all_to_all | solution.py:437
  13.8 0.1 collective-permute-start
  13.9 5.1 %prepare.1 = (bf16[2,512,1024]{2,1,0:T(8,128)(2,1)S(1)}, f32[24,128]{1,0:T(8,128)S(1)}, f32[128,1024]{1,0:T(8,128)S(1)}) custom-call(s32[4]{0:T(128)S(4)} %get-tuple-element.22.own_ids, s32[2,8,64]{2,1,0:T(8,128)} %bitcast.23, f32[2,512,1024]{2,1,0:T(8,128)} %p_hbm.5, bf16[2,512,1024]{2,1,0:T(8,128)(2,1)} %c_hbm.1), custom_call_target="tpu_custom_call" | custom-call | tf_op jit(solution)/shard_map/prepare/pallas_call | solution.py:399
  19.0 0.0 collective-permute-done.partner_ids
  19.0 6.9 %all-to-all-done = f32[64,1,1664]{2,1,0:T(1,128)S(1)} async-done(((f32[64,1,1664]{2,1,0:T(1,128)}), f32[64,1,1664]{2,1,0:T(1,128)S(1)}, u32[]{:S(2)}, u32[]{:S(2)}) %all-to-all-start) | async-done | bytes 426016 | tf_op jit(solution)/shard_map/all_to_all | solution.py:437
  25.9 0.2 pick.1._.mine
  26.1 0.1 collective-permute-start.1
  26.2 1.4 %load.1.rest = f32[384,1024]{1,0:T(8,128)S(1)} custom-call(f32[2,512,1024]{2,1,0:T(8,128)} %p_hbm.5, f32[32,128]{1,0:T(8,128)S(1)} %pick.1._.mine), custom_call_target="tpu_custom_call" | custom-call | tf_op jit(solution)/shard_map/load/pallas_call | solution.py:399
  27.6 0.0 collective-permute-done.1.other
  27.6 2.1 %first.1 = (f32[2,512,1024]{2,1,0:T(8,128)S(1)}, f32[24,128]{1,0:T(8,128)S(1)}, f32[288,128]{1,0:T(8,128)S(1)}, s32[8,128]{1,0:T(8,128)S(4)}) custom-call(s32[4]{0:T(128)S(4)} %get-tuple-element.22.own_ids, f32[832,128]{1,0:T(8,128)S(1)} %bitcast.16, f32[32,128]{1,0:T(8,128)S(1)} %pick.1._.mine, f32[32,128]{1,0:T(8,128)S(1)} %collective-permute-done.1.other, ...), custom_call_target="tpu_custom_call" | custom-call | tf_op jit(solution)/shard_map/first/pallas_call | solution.py:399
  29.8 8.7 %all_to_all.36 = f32[8,1,4608]{2,1,0:T(1,128)S(1)} all-to-all(f32[8,1,4608]{2,1,0:T(1,128)S(1)} %bitcast.22), channel_id=1, replica_groups={{0,1,32,33,64,65,96,97},{2,3,34,35,66,67,98,99},{4,5,36,37,68,69,100,10..., dimensions={0} | all-to-all | bytes 294912 | tf_op jit(solution)/shard_map/all_to_all | solution.py:437
  38.4 0.6 users.1
  39.0 11.5 %all_to_all.37 = f32[16,1,3072]{2,1,0:T(1,128)S(1)} all-to-all(f32[16,1,3072]{2,1,0:T(1,128)S(1)} %bitcast.21), channel_id=1, replica_groups=mesh['x'=4,'z'=4,'y'=4,'core'=2] {'z','y'}, dimensions={0} | all-to-all | bytes 393216 | tf_op jit(solution)/shard_map/all_to_all | solution.py:437
  50.5 2.0 %second.1 = (f32[2,512,1024]{2,1,0:T(8,128)}, f32[24,128]{1,0:T(8,128)S(1)}, f32[256,1024]{1,0:T(8,128)S(1)}) custom-call(s32[6]{0:T(128)S(4)} %get-tuple-element.31.flags, f32[384,128]{1,0:T(8,128)S(1)} %bitcast.19, f32[2,512,1024]{2,1,0:T(8,128)S(1)} %get-tuple-element.33.base, f32[24,128]{1,0:T(8,128)S(1)} %get-tuple-element.34.psum), custom_call_target="tpu_custom_call" | custom-call | tf_op jit(solution)/shard_map/second/pallas_call | solution.py:399
  52.6 0.1 collective-permute-start.2
  52.7 1.0 %store.1._ = f32[2,512,1024]{2,1,0:T(8,128)} custom-call(f32[256,1024]{1,0:T(8,128)S(1)} %get-tuple-element.35.tail, f32[2,512,1024]{2,1,0:T(8,128)} %get-tuple-element.36._), custom_call_target="tpu_custom_call", output_to_operand_aliasing={{}: (1, {})} | custom-call | tf_op jit(solution)/shard_map/store/pallas_call | solution.py:399
  53.7 0.2 collective-permute-done.2.other
  53.8 0.1 owners.1
  53.9 16.8 %all_to_all.38 = f32[64,1,1536]{2,1,0:T(1,128)S(1)} all-to-all(f32[64,1,1536]{2,1,0:T(1,128)S(1)} %bitcast.18), channel_id=1, replica_groups=mesh['x'=4,'z'=4,'y'=4,'core'=2] {'x','z','y'}, dimensions={0} | all-to-all | bytes 786432 | tf_op jit(solution)/shard_map/all_to_all | solution.py:437
  70.7 0.6 last.1
Async XLA Ops:
  2.2 23.6 %all-to-all-start = ((f32[64,1,1664]{2,1,0:T(1,128)}), f32[64,1,1664]{2,1,0:T(1,128)S(1)}, u32[]{:S(2)}, u32[]{:S(2)}) async-start(f32[64,1,1664]{2,1,0:T(1,128)} %bitcast.4), calls=%async_computation | async-start | bytes 851968 | tf_op jit(solution)/shard_map/all_to_all | solution.py:437
  13.8 5.2 %collective-permute-start = (s32[8,128]{1,0:T(8,128)S(1)}, s32[8,128]{1,0:T(8,128)S(1)}, u32[]{:S(2)}, u32[]{:S(2)}) collective-permute-start(s32[8,128]{1,0:T(8,128)S(1)} %get-tuple-element.24), channel_id=1, source_target_pairs={{0,1},{1,0},{2,3},{3,2},{4,5},{5,4},{6,7},{7,6},{8,9},{9,8},{10,11... | collective-permute-start | bytes 12296 | tf_op jit(solution)/shard_map/ppermute | solution.py:442
  26.1 1.5 %collective-permute-start.1 = (f32[32,128]{1,0:T(8,128)S(1)}, f32[32,128]{1,0:T(8,128)S(1)}, u32[]{:S(2)}, u32[]{:S(2)}) collective-permute-start(f32[32,128]{1,0:T(8,128)S(1)} %pick.1._.mine), channel_id=1, source_target_pairs={{0,1},{1,0},{2,3},{3,2},{4,5},{5,4},{6,7},{7,6},{8,9},{9,8},{10,11... | collective-permute-start | bytes 49160 | tf_op jit(solution)/shard_map/ppermute | solution.py:442
  52.6 1.3 %collective-permute-start.2 = (f32[24,128]{1,0:T(8,128)S(1)}, f32[24,128]{1,0:T(8,128)S(1)}, u32[]{:S(2)}, u32[]{:S(2)}) collective-permute-start(f32[24,128]{1,0:T(8,128)S(1)} %get-tuple-element.37.mine), channel_id=1, source_target_pairs={{0,1},{1,0},{2,3},{3,2},{4,5},{5,4},{6,7},{7,6},{8,9},{9,8},{10,11... | collective-permute-start | bytes 36872 | tf_op jit(solution)/shard_map/ppermute | solution.py:442

commit v12 on v11

--- a/solution.py
+++ b/solution.py
@@ -188,7 +188,27 @@
     write_cols(t, usum, cols)
 
 
-def first_kernel(own_ids, rec, mine, other, bias, psum, hc_ref, head, rest, p_hbm, out, usum, msg, ids, p_ref, a_buf, r_buf, id_buf, p_sems, sem):
+def write_flags(own_ids, mine, other, flags):
+    me = device()
+    core = me & 1
+    lane = lax.broadcasted_iota(jnp.int32, (4, L), 1)
+    row = lax.broadcasted_iota(jnp.int32, (4, L), 0)
+    place = lane * 4 + jnp.where(row < 2, core, 1 - core) * 2 + (row & 1)
+
+    def found(where):
+        return jnp.max(jnp.where(where & (lane < CHIPS), 1, 0))
+
+    for kind in range(2):
+        rows = pl.ds(TS + 2 * kind, 2)
+        ids = jnp.concatenate([mine[rows, :], other[rows, :]], axis=0).astype(jnp.int32)
+        for k in range(2):
+            i = own_ids[2 * kind + k]
+            earlier = found((ids == i) & (place < me * 2 + k))
+            flags[2 * kind + k] = jnp.where((i >= 0) & (earlier == 0), 1, 0)
+        flags[4 + kind] = 1 - found(ids == me)
+
+
+def first_kernel(own_ids, rec, mine, other, bias, psum, hc_ref, head, rest, p_hbm, out, usum, msg, ids, flags, p_ref, a_buf, r_buf, id_buf, p_sems, sem):
     def fetch(b):
         rows = pl.ds(b * RB, RB)
         return pltpu.make_async_copy(p_hbm.at[1, rows, :], p_ref.at[rows, :], p_sems.at[b])
@@ -204,6 +224,7 @@
     id_buf[4:8, :] = other[TS : TS + 4, :].astype(jnp.int32)
     keep_ids = pltpu.make_async_copy(id_buf, ids, sem)
     keep_ids.start()
+    write_flags(own_ids, mine, other, flags)
     slots = []
     for t in range(2):
         a, s = own_ids[t], own_ids[2 + t]
@@ -220,28 +241,7 @@
     keep_ids.wait()
 
 
-def write_flags(own_ids, mine, other, flags):
-    me = device()
-    core = me & 1
-    lane = lax.broadcasted_iota(jnp.int32, (4, L), 1)
-    row = lax.broadcasted_iota(jnp.int32, (4, L), 0)
-    place = lane * 4 + jnp.where(row < 2, core, 1 - core) * 2 + (row & 1)
-
-    def found(where):
-        return jnp.max(jnp.where(where & (lane < CHIPS), 1, 0))
-
-    for kind in range(2):
-        rows = pl.ds(TS + 2 * kind, 2)
-        ids = jnp.concatenate([mine[rows, :], other[rows, :]], axis=0).astype(jnp.int32)
-        for k in range(2):
-            i = own_ids[2 * kind + k]
-            earlier = found((ids == i) & (place < me * 2 + k))
-            flags[2 * kind + k] = jnp.where((i >= 0) & (earlier == 0), 1, 0)
-        flags[4 + kind] = 1 - found(ids == me)
-
-
-def users_kernel(own_ids, ids, mine, other, rec, out, flags, acc_a0, acc_a1, acc_s0, acc_s1):
-    write_flags(own_ids, mine, other, flags)
+def users_kernel(ids, rec, out, acc_a0, acc_a1, acc_s0, acc_s1):
     me = device()
     chip = me >> 1
     core = me & 1
@@ -470,22 +470,22 @@
         [vmem_out(512 - HEAD, 1024)],
         [pltpu.SemaphoreType.DMA(())],
     )
-    base, usum, message, ids = call(
+    base, usum, message, ids, flags = call(
         first_kernel,
         "first",
         [smem_arg(own_ids), table, vmem_arg(picked), vmem_arg(other), vmem_arg(bias), vmem_arg(psum), vmem_arg(hc)]
         + [vmem_arg(head), vmem_arg(rest), hbm_arg(primal_start)],
-        [vmem_out(*tile), vmem_out(TS, L), vmem_out(LINE * MSG, L), smem_out(8, L)],
+        [vmem_out(*tile), vmem_out(TS, L), vmem_out(LINE * MSG, L), smem_out(8, L), smem_out(6)],
         [vmem(512, 1024), vmem(1024, L), vmem(1024, L), pltpu.VMEM((8, L), jnp.int32)]
         + [pltpu.SemaphoreType.DMA((NRB,)), pltpu.SemaphoreType.DMA(())],
         8,
     )
     part = exchange(message, AXES, MSG, LINE_GROUPS)
-    message, flags = call(
+    (message,) = call(
         users_kernel,
         "users",
-        [smem_arg(own_ids), smem_arg(ids), vmem_arg(picked), vmem_arg(other), part],
-        [vmem_out(PLANE * TS, L), smem_out(6)],
+        [smem_arg(ids), part],
+        [vmem_out(PLANE * TS, L)],
         [vmem((BLOCKS + 1) * 8, L)] * 4,
     )
     primal, sums, tail = call(

time: 71.8 us -> 71.9 us (level)
  no operation moved by 1% of the time
where the time goes in v12:
time: 71.9 us; the launch traced here: 71.4 us
  blocking collectives  36.9 us (51%)
  Pallas kernels  14.9 us (21%)
  starting transfers between devices  11.8 us (16%)
  waiting for transfers between devices  7.04 us (10%)
  between operations  0.75 us (1%)
    all_to_all x3, blocking collectives, exchange(): lax.all_to_all(x.reshape(n, rows * L), axes, 0, 0, axis_index_groups=grou...  36.9 us
    pallas_call x10, Pallas kernels, call(): pl.pallas_call(kernel, in_specs=[s for _, s in ins], out_specs=[s for _,...  14.9 us
    all_to_all x1, starting transfers between devices, exchange(): lax.all_to_all(x.reshape(n, rows * L), axes, 0, 0, axis_index_groups=grou...  11.5 us
    all_to_all x1, waiting for transfers between devices, exchange(): lax.all_to_all(x.reshape(n, rows * L), axes, 0, 0, axis_index_groups=grou...  6.86 us
  transfers between devices with their start and end apart: 4, of which 2 were waited for; matrix products, arithmetic and copies ran while one was open for 0% of the time, Pallas kernels for 11%

profile of v12, /device:TPU:0, one launch (start us, length us, event | category | flops | bytes accessed | tf_op | source)
XLA Modules:
  0.0 71.4 jit_solution(8404902779235948773)
XLA Ops:
  0.6 1.6 %own.1 = (f32[832,128]{1,0:T(8,128)}, f32[12,128]{1,0:T(8,128)S(1)}, f32[12,128]{1,0:T(8,128)S(1)}, s32[8,128]{1,0:T(8,128)S(1)}, s32[4]{0:T(128)S(4)}) custom-call(s32[2]{0:T(128)} %adv_id.1, s32[2]{0:T(128)} %slot_id.1, f32[4,128]{1,0:T(4,128)} %bitcast.26, f32[8,128]{1,0:T(8,128)} %bitcast.24, f32[4,128]{1,0:T(4,128)} %bitcast.27, f32[8,128]{1,0:T(8,128)} %bitcast.25), custom_call_target="tpu_custom_call" | custom-call | tf_op jit(solution)/shard_map/own/pallas_call | solution.py:399
  2.2 11.5 %all-to-all-start = ((f32[64,1,1664]{2,1,0:T(1,128)}), f32[64,1,1664]{2,1,0:T(1,128)S(1)}, u32[]{:S(2)}, u32[]{:S(2)}) async-start(f32[64,1,1664]{2,1,0:T(1,128)} %bitcast.4), calls=%async_computation | async-start | bytes 851968 | tf_op jit(solution)/shard_map/all_to_all | solution.py:437
  13.8 0.1 collective-permute-start
  13.9 5.1 %prepare.1 = (bf16[2,512,1024]{2,1,0:T(8,128)(2,1)S(1)}, f32[24,128]{1,0:T(8,128)S(1)}, f32[128,1024]{1,0:T(8,128)S(1)}) custom-call(s32[4]{0:T(128)S(4)} %get-tuple-element.21.own_ids, s32[2,8,64]{2,1,0:T(8,128)} %bitcast.23, f32[2,512,1024]{2,1,0:T(8,128)} %p_hbm.5, bf16[2,512,1024]{2,1,0:T(8,128)(2,1)} %c_hbm.1), custom_call_target="tpu_custom_call" | custom-call | tf_op jit(solution)/shard_map/prepare/pallas_call | solution.py:399
  19.0 0.0 collective-permute-done.partner_ids
  19.0 6.9 %all-to-all-done = f32[64,1,1664]{2,1,0:T(1,128)S(1)} async-done(((f32[64,1,1664]{2,1,0:T(1,128)}), f32[64,1,1664]{2,1,0:T(1,128)S(1)}, u32[]{:S(2)}, u32[]{:S(2)}) %all-to-all-start) | async-done | bytes 426016 | tf_op jit(solution)/shard_map/all_to_all | solution.py:437
  25.9 0.2 pick.1._.mine
  26.1 0.1 collective-permute-start.1
  26.2 1.4 %load.1.rest = f32[384,1024]{1,0:T(8,128)S(1)} custom-call(f32[2,512,1024]{2,1,0:T(8,128)} %p_hbm.5, f32[32,128]{1,0:T(8,128)S(1)} %pick.1._.mine), custom_call_target="tpu_custom_call" | custom-call | tf_op jit(solution)/shard_map/load/pallas_call | solution.py:399
  27.6 0.0 collective-permute-done.1.other
  27.6 2.3 %first.1 = (f32[2,512,1024]{2,1,0:T(8,128)S(1)}, f32[24,128]{1,0:T(8,128)S(1)}, f32[288,128]{1,0:T(8,128)S(1)}, s32[8,128]{1,0:T(8,128)S(4)}, s32[6]{0:T(128)S(4)}) custom-call(s32[4]{0:T(128)S(4)} %get-tuple-element.21.own_ids, f32[832,128]{1,0:T(8,128)S(1)} %bitcast.16, f32[32,128]{1,0:T(8,128)S(1)} %pick.1._.mine, ...), custom_call_target="tpu_custom_call" | custom-call | tf_op jit(solution)/shard_map/first/pallas_call | solution.py:399
  30.0 8.7 %all_to_all.36 = f32[8,1,4608]{2,1,0:T(1,128)S(1)} all-to-all(f32[8,1,4608]{2,1,0:T(1,128)S(1)} %bitcast.22), channel_id=1, replica_groups={{0,1,32,33,64,65,96,97},{2,3,34,35,66,67,98,99},{4,5,36,37,68,69,100,10..., dimensions={0} | all-to-all | bytes 294912 | tf_op jit(solution)/shard_map/all_to_all | solution.py:437
  38.6 0.5 users.1
  39.1 11.5 %all_to_all.37 = f32[16,1,3072]{2,1,0:T(1,128)S(1)} all-to-all(f32[16,1,3072]{2,1,0:T(1,128)S(1)} %bitcast.19), channel_id=1, replica_groups=mesh['x'=4,'z'=4,'y'=4,'core'=2] {'z','y'}, dimensions={0} | all-to-all | bytes 393216 | tf_op jit(solution)/shard_map/all_to_all | solution.py:437
  50.6 2.0 %second.1 = (f32[2,512,1024]{2,1,0:T(8,128)}, f32[24,128]{1,0:T(8,128)S(1)}, f32[256,1024]{1,0:T(8,128)S(1)}) custom-call(s32[6]{0:T(128)S(4)} %get-tuple-element.28.flags, f32[384,128]{1,0:T(8,128)S(1)} %bitcast.20, f32[2,512,1024]{2,1,0:T(8,128)S(1)} %get-tuple-element.31.base, f32[24,128]{1,0:T(8,128)S(1)} %get-tuple-element.32.psum), custom_call_target="tpu_custom_call" | custom-call | tf_op jit(solution)/shard_map/second/pallas_call | solution.py:399
  52.7 0.1 collective-permute-start.2
  52.8 1.0 %store.1._ = f32[2,512,1024]{2,1,0:T(8,128)} custom-call(f32[256,1024]{1,0:T(8,128)S(1)} %get-tuple-element.33.tail, f32[2,512,1024]{2,1,0:T(8,128)} %get-tuple-element.34._), custom_call_target="tpu_custom_call", output_to_operand_aliasing={{}: (1, {})} | custom-call | tf_op jit(solution)/shard_map/store/pallas_call | solution.py:399
  53.8 0.2 collective-permute-done.2.other
  53.9 0.1 owners.1
  54.0 16.8 %all_to_all.38 = f32[64,1,1536]{2,1,0:T(1,128)S(1)} all-to-all(f32[64,1,1536]{2,1,0:T(1,128)S(1)} %bitcast.18), channel_id=1, replica_groups=mesh['x'=4,'z'=4,'y'=4,'core'=2] {'x','z','y'}, dimensions={0} | all-to-all | bytes 786432 | tf_op jit(solution)/shard_map/all_to_all | solution.py:437
  70.8 0.6 last.1
Async XLA Ops:
  2.2 23.6 %all-to-all-start = ((f32[64,1,1664]{2,1,0:T(1,128)}), f32[64,1,1664]{2,1,0:T(1,128)S(1)}, u32[]{:S(2)}, u32[]{:S(2)}) async-start(f32[64,1,1664]{2,1,0:T(1,128)} %bitcast.4), calls=%async_computation | async-start | bytes 851968 | tf_op jit(solution)/shard_map/all_to_all | solution.py:437
  13.8 5.2 %collective-permute-start = (s32[8,128]{1,0:T(8,128)S(1)}, s32[8,128]{1,0:T(8,128)S(1)}, u32[]{:S(2)}, u32[]{:S(2)}) collective-permute-start(s32[8,128]{1,0:T(8,128)S(1)} %get-tuple-element.23), channel_id=1, source_target_pairs={{0,1},{1,0},{2,3},{3,2},{4,5},{5,4},{6,7},{7,6},{8,9},{9,8},{10,11... | collective-permute-start | bytes 12296 | tf_op jit(solution)/shard_map/ppermute | solution.py:442
  26.1 1.5 %collective-permute-start.1 = (f32[32,128]{1,0:T(8,128)S(1)}, f32[32,128]{1,0:T(8,128)S(1)}, u32[]{:S(2)}, u32[]{:S(2)}) collective-permute-start(f32[32,128]{1,0:T(8,128)S(1)} %pick.1._.mine), channel_id=1, source_target_pairs={{0,1},{1,0},{2,3},{3,2},{4,5},{5,4},{6,7},{7,6},{8,9},{9,8},{10,11... | collective-permute-start | bytes 49160 | tf_op jit(solution)/shard_map/ppermute | solution.py:442
  52.7 1.3 %collective-permute-start.2 = (f32[24,128]{1,0:T(8,128)S(1)}, f32[24,128]{1,0:T(8,128)S(1)}, u32[]{:S(2)}, u32[]{:S(2)}) collective-permute-start(f32[24,128]{1,0:T(8,128)S(1)} %get-tuple-element.35.mine), channel_id=1, source_target_pairs={{0,1},{1,0},{2,3},{3,2},{4,5},{5,4},{6,7},{7,6},{8,9},{9,8},{10,11... | collective-permute-start | bytes 36872 | tf_op jit(solution)/shard_map/ppermute | solution.py:442

commit v13 on v11

--- a/solution.py
+++ b/solution.py
@@ -204,16 +204,15 @@
     id_buf[4:8, :] = other[TS : TS + 4, :].astype(jnp.int32)
     keep_ids = pltpu.make_async_copy(id_buf, ids, sem)
     keep_ids.start()
-    slots = []
     for t in range(2):
         a, s = own_ids[t], own_ids[2 + t]
+        part = pl.ds(t * 512, 512)
         arow = jnp.where((a & 1) == core, rows_of(rec, a, False), other[AR * t : AR * (t + 1), :])
-        spread_half(arow, a_buf.at[pl.ds(t * 512, 512), :])
-        slots.append(jnp.where((s & 1) == core, rows_of(rec, s, True), other[8 + SR * t : 8 + SR * (t + 1), :]))
-    for t in range(2):
+        srow = jnp.where((s & 1) == core, rows_of(rec, s, True), other[8 + SR * t : 8 + SR * (t + 1), :])
+        spread_half(arow, a_buf.at[part, :])
         sources = [(p_ref, 0) if t else (head, 0) if b * RB < HEAD else (rest, HEAD) for b in range(NRB)]
-        first_tile(t, slots[t], sources, hc_ref, out, usum, a_buf, r_buf, ready)
-    write_rows(usum, r_buf)
+        first_tile(t, srow, sources, hc_ref, out, usum, a_buf, r_buf, ready)
+        write_rows(usum, r_buf.at[part, :], (t,))
     data = jnp.concatenate([2.0 * usum[...] - psum[...], bias[...]], axis=0)
     for j in range(LINE):
         msg[j * MSG : (j + 1) * MSG, :] = data
@@ -330,11 +329,12 @@
     total = jnp.maximum(tree([rec[j * TS : (j + 1) * TS, :] for j in range(PLANE)]), 0.0)
     adv = total[0:8] * (1.0 / 1024)
     slot = total[8:24] * (1.0 / 512)
-    spread_half(adv, a_buf)
     for t in range(2):
         outs = [(out, -t * 512) if t * 512 + b * RB < early else (tail, early - t * 512) for b in range(NRB)]
+        part = pl.ds(t * 512, 512)
+        spread_half(adv[4 * t : 4 * t + 4], a_buf.at[part, :])
         second_tile(t, slot[8 * t : 8 * t + 8], base, outs, usum, a_buf, r_buf, done)
-    write_rows(usum, r_buf)
+        write_rows(usum, r_buf.at[part, :], (t,))
     for k, (o, n) in enumerate(((0, AR), (AR, AR), (8, SR), (8 + SR, SR))):
         rows = pl.ds(o, n)
         named = total[o : o + n] * jnp.where(flags[k] > 0, 1.0, 0.0)

time: 71.8 us -> 71.6 us (level)
  no operation moved by 1% of the time
where the time goes in v13:
time: 71.6 us; the launch traced here: 71.1 us
  blocking collectives  36.9 us (52%)
  Pallas kernels  14.6 us (20%)
  starting transfers between devices  11.8 us (16%)
  waiting for transfers between devices  7.04 us (10%)
  between operations  0.75 us (1%)
    all_to_all x3, blocking collectives, exchange(): lax.all_to_all(x.reshape(n, rows * L), axes, 0, 0, axis_index_groups=grou...  36.9 us
    pallas_call x10, Pallas kernels, call(): pl.pallas_call(kernel, in_specs=[s for _, s in ins], out_specs=[s for _,...  14.6 us
    all_to_all x1, starting transfers between devices, exchange(): lax.all_to_all(x.reshape(n, rows * L), axes, 0, 0, axis_index_groups=grou...  11.5 us
    all_to_all x1, waiting for transfers between devices, exchange(): lax.all_to_all(x.reshape(n, rows * L), axes, 0, 0, axis_index_groups=grou...  6.86 us
  transfers between devices with their start and end apart: 4, of which 2 were waited for; matrix products, arithmetic and copies ran while one was open for 0% of the time, Pallas kernels for 11%

profile of v13, /device:TPU:0, one launch (start us, length us, event | category | flops | bytes accessed | tf_op | source)
XLA Modules:
  0.0 71.1 jit_solution(4308128368251427257)
XLA Ops:
  0.6 1.6 %own.1 = (f32[832,128]{1,0:T(8,128)}, f32[12,128]{1,0:T(8,128)S(1)}, f32[12,128]{1,0:T(8,128)S(1)}, s32[8,128]{1,0:T(8,128)S(1)}, s32[4]{0:T(128)S(4)}) custom-call(s32[2]{0:T(128)} %adv_id.1, s32[2]{0:T(128)} %slot_id.1, f32[4,128]{1,0:T(4,128)} %bitcast.26, f32[8,128]{1,0:T(8,128)} %bitcast.24, f32[4,128]{1,0:T(4,128)} %bitcast.27, f32[8,128]{1,0:T(8,128)} %bitcast.25), custom_call_target="tpu_custom_call" | custom-call | tf_op jit(solution)/shard_map/own/pallas_call | solution.py:399
  2.2 11.5 %all-to-all-start = ((f32[64,1,1664]{2,1,0:T(1,128)}), f32[64,1,1664]{2,1,0:T(1,128)S(1)}, u32[]{:S(2)}, u32[]{:S(2)}) async-start(f32[64,1,1664]{2,1,0:T(1,128)} %bitcast.4), calls=%async_computation | async-start | bytes 851968 | tf_op jit(solution)/shard_map/all_to_all | solution.py:437
  13.8 0.1 collective-permute-start
  13.9 5.1 %prepare.1 = (bf16[2,512,1024]{2,1,0:T(8,128)(2,1)S(1)}, f32[24,128]{1,0:T(8,128)S(1)}, f32[128,1024]{1,0:T(8,128)S(1)}) custom-call(s32[4]{0:T(128)S(4)} %get-tuple-element.22.own_ids, s32[2,8,64]{2,1,0:T(8,128)} %bitcast.23, f32[2,512,1024]{2,1,0:T(8,128)} %p_hbm.5, bf16[2,512,1024]{2,1,0:T(8,128)(2,1)} %c_hbm.1), custom_call_target="tpu_custom_call" | custom-call | tf_op jit(solution)/shard_map/prepare/pallas_call | solution.py:399
  19.0 0.0 collective-permute-done.partner_ids
  19.0 6.9 %all-to-all-done = f32[64,1,1664]{2,1,0:T(1,128)S(1)} async-done(((f32[64,1,1664]{2,1,0:T(1,128)}), f32[64,1,1664]{2,1,0:T(1,128)S(1)}, u32[]{:S(2)}, u32[]{:S(2)}) %all-to-all-start) | async-done | bytes 426016 | tf_op jit(solution)/shard_map/all_to_all | solution.py:437
  25.9 0.2 pick.1._.mine
  26.1 0.1 collective-permute-start.1
  26.2 1.4 %load.1.rest = f32[384,1024]{1,0:T(8,128)S(1)} custom-call(f32[2,512,1024]{2,1,0:T(8,128)} %p_hbm.5, f32[32,128]{1,0:T(8,128)S(1)} %pick.1._.mine), custom_call_target="tpu_custom_call" | custom-call | tf_op jit(solution)/shard_map/load/pallas_call | solution.py:399
  27.6 0.0 collective-permute-done.1.other
  27.6 2.0 %first.1 = (f32[2,512,1024]{2,1,0:T(8,128)S(1)}, f32[24,128]{1,0:T(8,128)S(1)}, f32[288,128]{1,0:T(8,128)S(1)}, s32[8,128]{1,0:T(8,128)S(4)}) custom-call(s32[4]{0:T(128)S(4)} %get-tuple-element.22.own_ids, f32[832,128]{1,0:T(8,128)S(1)} %bitcast.16, f32[32,128]{1,0:T(8,128)S(1)} %pick.1._.mine, f32[32,128]{1,0:T(8,128)S(1)} %collective-permute-done.1.other, ...), custom_call_target="tpu_custom_call" | custom-call | tf_op jit(solution)/shard_map/first/pallas_call | solution.py:399
  29.6 8.7 %all_to_all.36 = f32[8,1,4608]{2,1,0:T(1,128)S(1)} all-to-all(f32[8,1,4608]{2,1,0:T(1,128)S(1)} %bitcast.22), channel_id=1, replica_groups={{0,1,32,33,64,65,96,97},{2,3,34,35,66,67,98,99},{4,5,36,37,68,69,100,10..., dimensions={0} | all-to-all | bytes 294912 | tf_op jit(solution)/shard_map/all_to_all | solution.py:437
  38.3 0.6 users.1
  38.9 11.5 %all_to_all.37 = f32[16,1,3072]{2,1,0:T(1,128)S(1)} all-to-all(f32[16,1,3072]{2,1,0:T(1,128)S(1)} %bitcast.21), channel_id=1, replica_groups=mesh['x'=4,'z'=4,'y'=4,'core'=2] {'z','y'}, dimensions={0} | all-to-all | bytes 393216 | tf_op jit(solution)/shard_map/all_to_all | solution.py:437
  50.4 2.0 %second.1 = (f32[2,512,1024]{2,1,0:T(8,128)}, f32[24,128]{1,0:T(8,128)S(1)}, f32[256,1024]{1,0:T(8,128)S(1)}) custom-call(s32[6]{0:T(128)S(4)} %get-tuple-element.31.flags, f32[384,128]{1,0:T(8,128)S(1)} %bitcast.19, f32[2,512,1024]{2,1,0:T(8,128)S(1)} %get-tuple-element.33.base, f32[24,128]{1,0:T(8,128)S(1)} %get-tuple-element.34.psum), custom_call_target="tpu_custom_call" | custom-call | tf_op jit(solution)/shard_map/second/pallas_call | solution.py:399
  52.4 0.1 collective-permute-start.2
  52.5 1.0 %store.1._ = f32[2,512,1024]{2,1,0:T(8,128)} custom-call(f32[256,1024]{1,0:T(8,128)S(1)} %get-tuple-element.35.tail, f32[2,512,1024]{2,1,0:T(8,128)} %get-tuple-element.36._), custom_call_target="tpu_custom_call", output_to_operand_aliasing={{}: (1, {})} | custom-call | tf_op jit(solution)/shard_map/store/pallas_call | solution.py:399
  53.5 0.2 collective-permute-done.2.other
  53.6 0.1 owners.1
  53.7 16.8 %all_to_all.38 = f32[64,1,1536]{2,1,0:T(1,128)S(1)} all-to-all(f32[64,1,1536]{2,1,0:T(1,128)S(1)} %bitcast.18), channel_id=1, replica_groups=mesh['x'=4,'z'=4,'y'=4,'core'=2] {'x','z','y'}, dimensions={0} | all-to-all | bytes 786432 | tf_op jit(solution)/shard_map/all_to_all | solution.py:437
  70.5 0.6 last.1
Async XLA Ops:
  2.2 23.6 %all-to-all-start = ((f32[64,1,1664]{2,1,0:T(1,128)}), f32[64,1,1664]{2,1,0:T(1,128)S(1)}, u32[]{:S(2)}, u32[]{:S(2)}) async-start(f32[64,1,1664]{2,1,0:T(1,128)} %bitcast.4), calls=%async_computation | async-start | bytes 851968 | tf_op jit(solution)/shard_map/all_to_all | solution.py:437
  13.8 5.2 %collective-permute-start = (s32[8,128]{1,0:T(8,128)S(1)}, s32[8,128]{1,0:T(8,128)S(1)}, u32[]{:S(2)}, u32[]{:S(2)}) collective-permute-start(s32[8,128]{1,0:T(8,128)S(1)} %get-tuple-element.24), channel_id=1, source_target_pairs={{0,1},{1,0},{2,3},{3,2},{4,5},{5,4},{6,7},{7,6},{8,9},{9,8},{10,11... | collective-permute-start | bytes 12296 | tf_op jit(solution)/shard_map/ppermute | solution.py:442
  26.1 1.5 %collective-permute-start.1 = (f32[32,128]{1,0:T(8,128)S(1)}, f32[32,128]{1,0:T(8,128)S(1)}, u32[]{:S(2)}, u32[]{:S(2)}) collective-permute-start(f32[32,128]{1,0:T(8,128)S(1)} %pick.1._.mine), channel_id=1, source_target_pairs={{0,1},{1,0},{2,3},{3,2},{4,5},{5,4},{6,7},{7,6},{8,9},{9,8},{10,11... | collective-permute-start | bytes 49160 | tf_op jit(solution)/shard_map/ppermute | solution.py:442
  52.4 1.3 %collective-permute-start.2 = (f32[24,128]{1,0:T(8,128)S(1)}, f32[24,128]{1,0:T(8,128)S(1)}, u32[]{:S(2)}, u32[]{:S(2)}) collective-permute-start(f32[24,128]{1,0:T(8,128)S(1)} %get-tuple-element.37.mine), channel_id=1, source_target_pairs={{0,1},{1,0},{2,3},{3,2},{4,5},{5,4},{6,7},{7,6},{8,9},{9,8},{10,11... | collective-permute-start | bytes 36872 | tf_op jit(solution)/shard_map/ppermute | solution.py:442

commit v14 on v13

--- a/solution.py
+++ b/solution.py
@@ -22,7 +22,7 @@
 NRB = 4
 BIG = 1e30
 HEAD = 128
-TAIL = 256
+TAIL = 384
 
 PLANE = 16
 AXES = ("x", "z", "y", "core")

time: 71.6 us -> 71.6 us (level)
  transfers between devices with their start and end apart: 4 -> 4, of which waited for: 2 -> 1; matrix products, arithmetic and copies ran while one was open for 0% -> 0% of each run, Pallas kernels for 11% -> 11%
where the time goes in v14:
time: 71.6 us; the launch traced here: 71.1 us
  blocking collectives  37.1 us (52%)
  Pallas kernels  14.6 us (20%)
  starting transfers between devices  11.8 us (16%)
  waiting for transfers between devices  6.87 us (10%)
  between operations  0.75 us (1%)
    all_to_all x3, blocking collectives, exchange(): lax.all_to_all(x.reshape(n, rows * L), axes, 0, 0, axis_index_groups=grou...  37.1 us
    pallas_call x10, Pallas kernels, call(): pl.pallas_call(kernel, in_specs=[s for _, s in ins], out_specs=[s for _,...  14.6 us
    all_to_all x1, starting transfers between devices, exchange(): lax.all_to_all(x.reshape(n, rows * L), axes, 0, 0, axis_index_groups=grou...  11.5 us
    all_to_all x1, waiting for transfers between devices, exchange(): lax.all_to_all(x.reshape(n, rows * L), axes, 0, 0, axis_index_groups=grou...  6.86 us
  transfers between devices with their start and end apart: 4, of which 1 were waited for; matrix products, arithmetic and copies ran while one was open for 0% of the time, Pallas kernels for 11%

profile of v14, /device:TPU:0, one launch (start us, length us, event | category | flops | bytes accessed | tf_op | source)
XLA Modules:
  0.0 71.1 jit_solution(2735868289396286386)
XLA Ops:
  0.6 1.6 %own.1 = (f32[832,128]{1,0:T(8,128)}, f32[12,128]{1,0:T(8,128)S(1)}, f32[12,128]{1,0:T(8,128)S(1)}, s32[8,128]{1,0:T(8,128)S(1)}, s32[4]{0:T(128)S(4)}) custom-call(s32[2]{0:T(128)} %adv_id.1, s32[2]{0:T(128)} %slot_id.1, f32[4,128]{1,0:T(4,128)} %bitcast.26, f32[8,128]{1,0:T(8,128)} %bitcast.24, f32[4,128]{1,0:T(4,128)} %bitcast.27, f32[8,128]{1,0:T(8,128)} %bitcast.25), custom_call_target="tpu_custom_call" | custom-call | tf_op jit(solution)/shard_map/own/pallas_call | solution.py:399
  2.2 11.5 %all-to-all-start = ((f32[64,1,1664]{2,1,0:T(1,128)}), f32[64,1,1664]{2,1,0:T(1,128)S(1)}, u32[]{:S(2)}, u32[]{:S(2)}) async-start(f32[64,1,1664]{2,1,0:T(1,128)} %bitcast.4), calls=%async_computation | async-start | bytes 851968 | tf_op jit(solution)/shard_map/all_to_all | solution.py:437
  13.8 0.1 collective-permute-start
  13.9 5.1 %prepare.1 = (bf16[2,512,1024]{2,1,0:T(8,128)(2,1)S(1)}, f32[24,128]{1,0:T(8,128)S(1)}, f32[128,1024]{1,0:T(8,128)S(1)}) custom-call(s32[4]{0:T(128)S(4)} %get-tuple-element.22.own_ids, s32[2,8,64]{2,1,0:T(8,128)} %bitcast.23, f32[2,512,1024]{2,1,0:T(8,128)} %p_hbm.5, bf16[2,512,1024]{2,1,0:T(8,128)(2,1)} %c_hbm.1), custom_call_target="tpu_custom_call" | custom-call | tf_op jit(solution)/shard_map/prepare/pallas_call | solution.py:399
  19.0 0.0 collective-permute-done.partner_ids
  19.0 6.9 %all-to-all-done = f32[64,1,1664]{2,1,0:T(1,128)S(1)} async-done(((f32[64,1,1664]{2,1,0:T(1,128)}), f32[64,1,1664]{2,1,0:T(1,128)S(1)}, u32[]{:S(2)}, u32[]{:S(2)}) %all-to-all-start) | async-done | bytes 426016 | tf_op jit(solution)/shard_map/all_to_all | solution.py:437
  25.9 0.2 pick.1._.mine
  26.1 0.1 collective-permute-start.1
  26.2 1.4 %load.1.rest = f32[384,1024]{1,0:T(8,128)S(1)} custom-call(f32[2,512,1024]{2,1,0:T(8,128)} %p_hbm.5, f32[32,128]{1,0:T(8,128)S(1)} %pick.1._.mine), custom_call_target="tpu_custom_call" | custom-call | tf_op jit(solution)/shard_map/load/pallas_call | solution.py:399
  27.6 0.0 collective-permute-done.1.other
  27.6 2.0 %first.1 = (f32[2,512,1024]{2,1,0:T(8,128)S(1)}, f32[24,128]{1,0:T(8,128)S(1)}, f32[288,128]{1,0:T(8,128)S(1)}, s32[8,128]{1,0:T(8,128)S(4)}) custom-call(s32[4]{0:T(128)S(4)} %get-tuple-element.22.own_ids, f32[832,128]{1,0:T(8,128)S(1)} %bitcast.16, f32[32,128]{1,0:T(8,128)S(1)} %pick.1._.mine, f32[32,128]{1,0:T(8,128)S(1)} %collective-permute-done.1.other, ...), custom_call_target="tpu_custom_call" | custom-call | tf_op jit(solution)/shard_map/first/pallas_call | solution.py:399
  29.6 8.7 %all_to_all.36 = f32[8,1,4608]{2,1,0:T(1,128)S(1)} all-to-all(f32[8,1,4608]{2,1,0:T(1,128)S(1)} %bitcast.22), channel_id=1, replica_groups={{0,1,32,33,64,65,96,97},{2,3,34,35,66,67,98,99},{4,5,36,37,68,69,100,10..., dimensions={0} | all-to-all | bytes 294912 | tf_op jit(solution)/shard_map/all_to_all | solution.py:437
  38.3 0.6 users.1
  38.9 11.5 %all_to_all.37 = f32[16,1,3072]{2,1,0:T(1,128)S(1)} all-to-all(f32[16,1,3072]{2,1,0:T(1,128)S(1)} %bitcast.21), channel_id=1, replica_groups=mesh['x'=4,'z'=4,'y'=4,'core'=2] {'z','y'}, dimensions={0} | all-to-all | bytes 393216 | tf_op jit(solution)/shard_map/all_to_all | solution.py:437
  50.4 1.8 %second.1 = (f32[2,512,1024]{2,1,0:T(8,128)}, f32[24,128]{1,0:T(8,128)S(1)}, f32[384,1024]{1,0:T(8,128)S(1)}) custom-call(s32[6]{0:T(128)S(4)} %get-tuple-element.31.flags, f32[384,128]{1,0:T(8,128)S(1)} %bitcast.19, f32[2,512,1024]{2,1,0:T(8,128)S(1)} %get-tuple-element.33.base, f32[24,128]{1,0:T(8,128)S(1)} %get-tuple-element.34.psum), custom_call_target="tpu_custom_call" | custom-call | tf_op jit(solution)/shard_map/second/pallas_call | solution.py:399
  52.2 0.1 collective-permute-start.2
  52.3 1.2 %store.1._ = f32[2,512,1024]{2,1,0:T(8,128)} custom-call(f32[384,1024]{1,0:T(8,128)S(1)} %get-tuple-element.35.tail, f32[2,512,1024]{2,1,0:T(8,128)} %get-tuple-element.36._), custom_call_target="tpu_custom_call", output_to_operand_aliasing={{}: (1, {})} | custom-call | tf_op jit(solution)/shard_map/store/pallas_call | solution.py:399
  53.5 0.0 collective-permute-done.2.other
  53.5 0.1 owners.1
  53.6 16.9 %all_to_all.38 = f32[64,1,1536]{2,1,0:T(1,128)S(1)} all-to-all(f32[64,1,1536]{2,1,0:T(1,128)S(1)} %bitcast.18), channel_id=1, replica_groups=mesh['x'=4,'z'=4,'y'=4,'core'=2] {'x','z','y'}, dimensions={0} | all-to-all | bytes 786432 | tf_op jit(solution)/shard_map/all_to_all | solution.py:437
  70.5 0.6 last.1
Async XLA Ops:
  2.2 23.6 %all-to-all-start = ((f32[64,1,1664]{2,1,0:T(1,128)}), f32[64,1,1664]{2,1,0:T(1,128)S(1)}, u32[]{:S(2)}, u32[]{:S(2)}) async-start(f32[64,1,1664]{2,1,0:T(1,128)} %bitcast.4), calls=%async_computation | async-start | bytes 851968 | tf_op jit(solution)/shard_map/all_to_all | solution.py:437
  13.8 5.2 %collective-permute-start = (s32[8,128]{1,0:T(8,128)S(1)}, s32[8,128]{1,0:T(8,128)S(1)}, u32[]{:S(2)}, u32[]{:S(2)}) collective-permute-start(s32[8,128]{1,0:T(8,128)S(1)} %get-tuple-element.24), channel_id=1, source_target_pairs={{0,1},{1,0},{2,3},{3,2},{4,5},{5,4},{6,7},{7,6},{8,9},{9,8},{10,11... | collective-permute-start | bytes 12296 | tf_op jit(solution)/shard_map/ppermute | solution.py:442
  26.1 1.5 %collective-permute-start.1 = (f32[32,128]{1,0:T(8,128)S(1)}, f32[32,128]{1,0:T(8,128)S(1)}, u32[]{:S(2)}, u32[]{:S(2)}) collective-permute-start(f32[32,128]{1,0:T(8,128)S(1)} %pick.1._.mine), channel_id=1, source_target_pairs={{0,1},{1,0},{2,3},{3,2},{4,5},{5,4},{6,7},{7,6},{8,9},{9,8},{10,11... | collective-permute-start | bytes 49160 | tf_op jit(solution)/shard_map/ppermute | solution.py:442
  52.2 1.3 %collective-permute-start.2 = (f32[24,128]{1,0:T(8,128)S(1)}, f32[24,128]{1,0:T(8,128)S(1)}, u32[]{:S(2)}, u32[]{:S(2)}) collective-permute-start(f32[24,128]{1,0:T(8,128)S(1)} %get-tuple-element.37.mine), channel_id=1, source_target_pairs={{0,1},{1,0},{2,3},{3,2},{4,5},{5,4},{6,7},{7,6},{8,9},{9,8},{10,11... | collective-permute-start | bytes 36872 | tf_op jit(solution)/shard_map/ppermute | solution.py:442
